TPU v7x, 32 devices: a whole 2x2x4 slice. The times are simulated.
32 devices in a mesh: groups: 2 (over x), row: 8 (over z, y), col: 2 (over core).
Axes of the slice: x: 2, y: 2, z: 4, core: 2. Of those that a mesh axis runs over, the one named last changes fastest.
Arguments:
- queries: bfloat16 [4096, 2560], P(('groups', 'row', 'col')), parts along dimension 0, may hold values from -32 to 32
- keys: bfloat16 [4096, 2560], P(('groups', 'row', 'col')), parts along dimension 0, may hold values from -6 to 6
- values: bfloat16 [4096, 2560], P(('groups', 'row', 'col')), parts along dimension 0, may hold values from -6 to 6
- pattern: int32 [16, 5], P('groups'), parts along dimension 0, may hold values from 0 to 1, as said below
Outputs:
- attended: bfloat16 [4096, 2560], P(('groups', 'row', 'col')), parts along dimension 0
There are 2 independent parts, one for each index of `groups`. A program takes and returns all parts, laid end to end along the dimension named above; each array names one. Nothing has to cross between parts.
Inputs may be any that keep to these rules, and one draw needn't show every extreme that they name: pattern[r, 0] is 1; pattern[r, j] is 0 where r + off_j lies outside 0 .. 7, or where off_j is -1 or +1 and r + off_j lies in another band of 4 tile rows.
All inputs are finite; a program needn't handle non-finite values.
Results may differ from a plain program's by a relative error of at most 0.0045.
Values may be sent and summed in bfloat16 or wider, within the bound.
No kernel may reach another device: no remote copies, remote signals or barrier semaphores. Data moves between devices by JAX's collectives and lax.ppermute only.
A program may use at most 64 MiB of HBM per device.

v0:
```python
import jax
import jax.numpy as jnp
from jax import lax
from jax.sharding import PartitionSpec as P

HEADS = 20
HD = 128
TILE_H = 4


far_below = -1e30


def passed_along(value, axis, by):
    count = lax.axis_size(axis)
    pairs = [(i, i + by) for i in range(count) if 0 <= i + by < count]
    return lax.ppermute(value, axis, pairs)


def block_terms(query_heads, key_block, value_block):
    key_heads = key_block.reshape(key_block.shape[0], HEADS, HD)
    value_heads = value_block.reshape(value_block.shape[0], HEADS, HD)
    scores = jnp.einsum(
        "qhd,khd->hqk", query_heads, key_heads, preferred_element_type=jnp.float32
    ) * HD ** (-0.5)
    block_max = jnp.max(scores, axis=2)
    weights = jnp.exp(scores - block_max[:, :, None])
    block_total = jnp.sum(weights, axis=2)
    block_out = jnp.einsum(
        "hqk,khd->qhd",
        weights.astype(jnp.bfloat16),
        value_heads,
        preferred_element_type=jnp.float32,
    )
    return (block_out, block_max.T, block_total.T)


def skipped(rows_here):
    return (
        jnp.zeros((rows_here, HEADS, HD), jnp.float32),
        jnp.full((rows_here, HEADS), far_below, jnp.float32),
        jnp.zeros((rows_here, HEADS), jnp.float32),
    )


def guarded(is_live, query_heads, key_block, value_block):
    rows_here = query_heads.shape[0]
    return lax.cond(
        is_live,
        lambda a, b, c: block_terms(a, b, c),
        lambda a, b, c: skipped(rows_here),
        query_heads,
        key_block,
        value_block,
    )


def keep_live(is_live, terms):
    rows_here = terms[0].shape[0]
    empty_terms = skipped(rows_here)
    return tuple(
        (jnp.where(is_live, given, fallback) for given, fallback in zip(terms, empty_terms))
    )


def combine(pieces):
    outs_all = jnp.stack([piece[0] for piece in pieces])
    maxes_all = jnp.stack([piece[1] for piece in pieces])
    totals_all = jnp.stack([piece[2] for piece in pieces])
    top_max = jnp.max(maxes_all, axis=0)
    factors = jnp.exp(maxes_all - top_max)
    numerator = jnp.sum(factors[..., None] * outs_all, axis=0)
    denominator = jnp.sum(factors * totals_all, axis=0)
    return numerator / denominator[..., None]


def shards(queries, keys, values, pattern):
    rows_here = queries.shape[0]
    width = queries.shape[1]
    row_index = lax.axis_index("row")
    row_count = lax.axis_size("row")
    query_heads = queries.reshape(rows_here, HEADS, HD)
    key_row, value_row = (
        lax.all_gather(keys, "col", axis=0, tiled=True),
        lax.all_gather(values, "col", axis=0, tiled=True),
    )
    offsets = [0, -1, 1, -TILE_H, TILE_H]
    pieces = []
    for number in range(5):
        offset = offsets[number]
        is_live = pattern[row_index, number] == 1
        if offset == 0:
            pieces.append(guarded(is_live, query_heads, key_row, value_row))
        else:
            visitors = passed_along(query_heads, "row", offset)
            source = row_index - offset
            inside = (source >= 0) & (source < row_count)
            source_live = inside & (pattern[jnp.clip(source, 0, row_count - 1), number] == 1)
            terms = guarded(source_live, visitors, key_row, value_row)
            returned = passed_along(terms, "row", -offset)
            pieces.append(keep_live(is_live, returned))
    attended = combine(pieces).astype(jnp.bfloat16)
    return attended.reshape(rows_here, width)


def solution(mesh):
    placed = (
        P(("groups", "row", "col"), None),
        P(("groups", "row", "col"), None),
        P(("groups", "row", "col"), None),
        P("groups", None),
    )
    return jax.shard_map(
        shards,
        mesh=mesh,
        in_specs=placed,
        out_specs=P(("groups", "row", "col"), None),
        check_vma=False,
    )
```

profile of v0, /device:TPU:0, one launch (start us, length us, event | category | flops | bytes accessed | tf_op | source)
XLA Modules:
  0.0 199.4 jit_solution(4693203722182766323)
XLA Ops:
  6.5 2.2 %copy.44 = bf16[128,2560]{0,1:T(8,128)(2,1)} copy(bf16[128,2560]{1,0:T(8,128)(2,1)} %param.15) | data formatting | bytes 1310720 | tf_op args[1]
  8.8 2.2 %copy.46 = bf16[128,2560]{0,1:T(8,128)(2,1)} copy(bf16[128,2560]{1,0:T(8,128)(2,1)} %param.16) | data formatting | bytes 1310720 | tf_op args[2]
  13.4 8.0 %collective-permute-start.6 = (bf16[128,20,128]{0,2,1:T(8,128)(2,1)}, bf16[128,20,128]{0,2,1:T(8,128)(2,1)S(1)}, u32[]{:S(2)}, u32[]{:S(2)}) collective-permute-start(bf16[128,20,128]{0,2,1:T(8,128)(2,1)} %bitcast.29), channel_id=1, source_target_pairs={{0,8},{2,10},{4,12},{6,14},{1,9},{3,11},{5,13},{7,15},{16,24},{18,... | collective-permute-start | bytes 1966088 | tf_op jit(solution)/shard_map/ppermute | solution.py:17
  21.4 1.3 collective-permute-start.4
  22.7 2.6 %collective-permute-start.2 = (bf16[128,20,128]{0,2,1:T(8,128)(2,1)}, bf16[128,20,128]{0,2,1:T(8,128)(2,1)S(1)}, u32[]{:S(2)}, u32[]{:S(2)}) collective-permute-start(bf16[128,20,128]{0,2,1:T(8,128)(2,1)} %bitcast.29), channel_id=1, source_target_pairs={{0,2},{2,4},{4,6},{6,8},{8,10},{10,12},{12,14},{1,3},{3,5},{5,7},{... | collective-permute-start | bytes 1966088 | tf_op jit(solution)/shard_map/ppermute | solution.py:17
  32.7 5.8 %conditional.6 = (f32[128,20,128]{2,0,1:T(8,128)S(1)}, f32[128,20]{0,1:T(8,128)}, f32[128,20]{0,1:T(8,128)S(1)}) conditional(s32[]{:T(128)} %convert_element_type.44, () %tuple.63, (bf16[256,2560]{0,1:T(8,128)(2,1)}, bf16[128,20,128]{0,2,1:T(8,128)(2,1)S(1)}, bf16[256,2560]{0,1:T(8,128)(2,1)}) %tuple.64), branch_computations={%region_4.5_spmd, %region_5.8_spmd} | conditional | flops 340782080 | bytes 17735732 | solution.py:48
  32.7 2.7 %multiply_reduce_fusion.1 = (f32[20,128]{1,0:T(8,128)}, f32[20,128,256]{2,1,0:T(8,128)S(1)}) fusion(bf16[128,20,128]{0,2,1:T(8,128)(2,1)S(1)} %get-tuple-element.124, bf16[256,20,128]{0,2,1:T(8,128)(2,1)} %bitcast.100), kind=kOutput, calls=%fused_computation.9 | convolution fusion | flops 169080320 | bytes 4597760 | tf_op jit(solution)/shard_map/cond/branch_1_fun/qhd,khd->hqk/dot_general | solution.py:23
  35.3 1.6 convolution_bitcast_fusion.1
  36.9 1.5 fusion.6
  38.5 5.0 %collective-permute-start.8 = (f32[128,20,128]{2,0,1:T(8,128)S(1)}, f32[128,20,128]{2,0,1:T(8,128)}, u32[]{:S(2)}, u32[]{:S(2)}) collective-permute-start(f32[128,20,128]{2,0,1:T(8,128)S(1)} %get-tuple-element.96), channel_id=1, source_target_pairs={{0,2},{2,4},{4,6},{6,8},{8,10},{10,12},{12,14},{1,3},{3,5},{5,7},{... | collective-permute-start | bytes 3932168 | tf_op jit(solution)/shard_map/ppermute | solution.py:17
  45.5 17.2 %collective-permute-done.4 = bf16[128,20,128]{0,2,1:T(8,128)(2,1)} collective-permute-done((bf16[128,20,128]{0,2,1:T(8,128)(2,1)}, bf16[128,20,128]{0,2,1:T(8,128)(2,1)}, u32[]{:S(2)}, u32[]{:S(2)}) %collective-permute-start.4) | collective-permute-done | bytes 655392 | tf_op jit(solution)/shard_map/ppermute | solution.py:17
  63.5 1.3 collective-permute-start.5
  64.9 6.0 %conditional.5 = (f32[1,128,20,128]{3,1,2,0:T(8,128)S(1)}, f32[1,128,20]{1,2,0:T(8,128)}, f32[1,128,20]{1,2,0:T(8,128)S(1)}) conditional(s32[]{:T(128)} %bitcast.28, () %tuple.61, (bf16[256,2560]{0,1:T(8,128)(2,1)}, bf16[128,20,128]{0,2,1:T(8,128)(2,1)}, bf16[256,2560]{0,1:T(8,128)(2,1)}) %tuple.62), branch_computations={%region_0.0_spmd, %region_1.0_spmd} | conditional | flops 340782080 | bytes 17735732 | solution.py:48
  64.9 2.9 %multiply_reduce_fusion = (f32[20,128]{1,0:T(8,128)}, f32[20,128,256]{2,1,0:T(8,128)S(1)}) fusion(bf16[128,20,128]{0,2,1:T(8,128)(2,1)} %get-tuple-element.121, bf16[256,20,128]{0,2,1:T(8,128)(2,1)} %bitcast.103), kind=kOutput, calls=%fused_computation.1 | convolution fusion | flops 169080320 | bytes 4597760 | tf_op jit(solution)/shard_map/cond/branch_1_fun/qhd,khd->hqk/dot_general | solution.py:23
  67.7 1.6 convolution_bitcast_fusion
  69.3 1.5 fusion
  75.1 4.5 %collective-permute-start.1 = (f32[128,20]{0,1:T(8,128)}, f32[128,20]{0,1:T(8,128)S(1)}, u32[]{:S(2)}, u32[]{:S(2)}) collective-permute-start(f32[128,20]{0,1:T(8,128)} %get-tuple-element.91), channel_id=1, source_target_pairs={{0,2},{2,4},{4,6},{6,8},{8,10},{10,12},{12,14},{1,3},{3,5},{5,7},{... | collective-permute-start | bytes 30728 | tf_op jit(solution)/shard_map/ppermute | solution.py:17
  81.7 7.9 %collective-permute-start.10 = (f32[128,20,128]{2,0,1:T(8,128)}, f32[128,20,128]{2,0,1:T(8,128)S(1)}, u32[]{:S(2)}, u32[]{:S(2)}) collective-permute-start(f32[128,20,128]{2,0,1:T(8,128)} %copy-done.8), channel_id=1, source_target_pairs={{0,8},{2,10},{4,12},{6,14},{1,9},{3,11},{5,13},{7,15},{16,24},{18,... | collective-permute-start | bytes 3932168 | tf_op jit(solution)/shard_map/ppermute | solution.py:17
  89.6 1.3 collective-permute-start.11
  94.9 25.1 %collective-permute-done.13 = f32[128,20]{0,1:T(8,128)S(1)} collective-permute-done((f32[128,20]{0,1:T(8,128)S(1)}, f32[128,20]{0,1:T(8,128)S(1)}, u32[]{:S(2)}, u32[]{:S(2)}) %collective-permute-start.13) | collective-permute-done | bytes 10272 | tf_op jit(solution)/shard_map/ppermute | solution.py:17
  120.0 53.5 %collective-permute-start.14 = (f32[128,20]{0,1:T(8,128)S(1)}, f32[128,20]{0,1:T(8,128)S(1)}, u32[]{:S(2)}, u32[]{:S(2)}) collective-permute-start(f32[128,20]{0,1:T(8,128)S(1)} %get-tuple-element.103), channel_id=1, source_target_pairs={{0,8},{2,10},{4,12},{6,14},{1,9},{3,11},{5,13},{7,15},{16,24},{18,... | collective-permute-start | bytes 30728 | tf_op jit(solution)/shard_map/ppermute | solution.py:17
  173.5 1.4 collective-permute-done.14
  176.2 5.2 %collective-permute-done.15 = f32[128,20]{0,1:T(8,128)S(1)} collective-permute-done((f32[128,20]{0,1:T(8,128)S(1)}, f32[128,20]{0,1:T(8,128)S(1)}, u32[]{:S(2)}, u32[]{:S(2)}) %collective-permute-start.15) | collective-permute-done | bytes 10272 | tf_op jit(solution)/shard_map/ppermute | solution.py:17
  186.1 4.6 %multiply_reduce_fusion.5 = f32[128,20,128]{2,0,1:T(8,128)S(1)} fusion(f32[5,128,20,128]{3,1,2,0:T(8,128)} %bitcast_dynamic-update-slice_fusion, f32[5,128,20]{1,2,0:T(8,128)S(1)} %get-tuple-element.136), kind=kLoop, calls=%fused_computation.40 | loop fusion | flops 2949120 | bytes 7915520 | tf_op jit(solution)/shard_map/reduce_sum | solution.py:72
  (76 shorter events, 27.1 us)
Async XLA Ops:
  6.5 4.5 %copy-start.9 = (bf16[128,2560]{1,0:T(8,128)(2,1)S(1)}, bf16[128,2560]{1,0:T(8,128)(2,1)}, u32[]{:S(2)}) copy-start(bf16[128,2560]{1,0:T(8,128)(2,1)} %param.14) | copy-start | bytes 1966084
  6.5 18.8 %copy-start.10 = (s32[8,5]{1,0:T(8,128)S(1)}, s32[8,5]{1,0:T(8,128)}, u32[]{:S(2)}) copy-start(s32[8,5]{1,0:T(8,128)} %param.17) | copy-start | bytes 484
  6.5 25.4 %all-gather.3.cloned.1.call-start = ((), (), s32[]{:S(2)}) async-start(), calls=%async_computation | async-start | bytes 1966080 | tf_op jit(solution)/shard_map/all_gather | solution.py:84
  8.8 23.9 %all-gather.5.cloned.1.call-start = ((), (), s32[]{:S(2)}) async-start(), calls=%async_computation.1 | async-start | bytes 1966080 | tf_op jit(solution)/shard_map/all_gather | solution.py:85
  12.1 19.8 %collective-permute-start = (bf16[128,20,128]{0,2,1:T(8,128)(2,1)}, bf16[128,20,128]{0,2,1:T(8,128)(2,1)S(1)}, u32[]{:S(2)}, u32[]{:S(2)}) collective-permute-start(bf16[128,20,128]{0,2,1:T(8,128)(2,1)} %bitcast.29), channel_id=1, source_target_pairs={{2,0},{4,2},{6,4},{8,6},{10,8},{12,10},{14,12},{3,1},{5,3},{7,5},{... | collective-permute-start | bytes 1966088 | tf_op jit(solution)/shard_map/ppermute | solution.py:17
  13.4 30.1 %collective-permute-start.6 = (bf16[128,20,128]{0,2,1:T(8,128)(2,1)}, bf16[128,20,128]{0,2,1:T(8,128)(2,1)S(1)}, u32[]{:S(2)}, u32[]{:S(2)}) collective-permute-start(bf16[128,20,128]{0,2,1:T(8,128)(2,1)} %bitcast.29), channel_id=1, source_target_pairs={{0,8},{2,10},{4,12},{6,14},{1,9},{3,11},{5,13},{7,15},{16,24},{18,... | collective-permute-start | bytes 1966088 | tf_op jit(solution)/shard_map/ppermute | solution.py:17
  21.4 41.3 %collective-permute-start.4 = (bf16[128,20,128]{0,2,1:T(8,128)(2,1)}, bf16[128,20,128]{0,2,1:T(8,128)(2,1)}, u32[]{:S(2)}, u32[]{:S(2)}) collective-permute-start(bf16[128,20,128]{0,2,1:T(8,128)(2,1)} %bitcast.29), channel_id=1, source_target_pairs={{8,0},{10,2},{12,4},{14,6},{9,1},{11,3},{13,5},{15,7},{24,16},{26,... | collective-permute-start | bytes 1966088 | tf_op jit(solution)/shard_map/ppermute | solution.py:17
  22.7 49.3 %collective-permute-start.2 = (bf16[128,20,128]{0,2,1:T(8,128)(2,1)}, bf16[128,20,128]{0,2,1:T(8,128)(2,1)S(1)}, u32[]{:S(2)}, u32[]{:S(2)}) collective-permute-start(bf16[128,20,128]{0,2,1:T(8,128)(2,1)} %bitcast.29), channel_id=1, source_target_pairs={{0,2},{2,4},{4,6},{6,8},{8,10},{10,12},{12,14},{1,3},{3,5},{5,7},{... | collective-permute-start | bytes 1966088 | tf_op jit(solution)/shard_map/ppermute | solution.py:17
  32.7 2.7 %copy-start.2 = (bf16[256,2560]{0,1:T(8,128)(2,1)S(1)}, bf16[256,2560]{0,1:T(8,128)(2,1)}, u32[]{:S(2)}) copy-start(bf16[256,2560]{0,1:T(8,128)(2,1)} %get-tuple-element.65) | copy-start | bytes 3932164 | tf_op jit(solution)/shard_map/cond
  38.5 142.9 %collective-permute-start.8 = (f32[128,20,128]{2,0,1:T(8,128)S(1)}, f32[128,20,128]{2,0,1:T(8,128)}, u32[]{:S(2)}, u32[]{:S(2)}) collective-permute-start(f32[128,20,128]{2,0,1:T(8,128)S(1)} %get-tuple-element.96), channel_id=1, source_target_pairs={{0,2},{2,4},{4,6},{6,8},{8,10},{10,12},{12,14},{1,3},{3,5},{5,7},{... | collective-permute-start | bytes 3932168 | tf_op jit(solution)/shard_map/ppermute | solution.py:17
  44.2 18.5 %copy-start.6 = (f32[128,20,128]{2,0,1:T(8,128)}, f32[128,20,128]{2,0,1:T(8,128)S(1)}, u32[]{:S(2)}) copy-start(f32[128,20,128]{2,0,1:T(8,128)S(1)} %get-tuple-element.99) | copy-start | bytes 3932164
  44.3 36.1 %collective-permute-start.7 = (f32[128,20]{0,1:T(8,128)}, f32[128,20]{0,1:T(8,128)S(1)}, u32[]{:S(2)}, u32[]{:S(2)}) collective-permute-start(f32[128,20]{0,1:T(8,128)} %get-tuple-element.94), channel_id=1, source_target_pairs={{8,0},{10,2},{12,4},{14,6},{9,1},{11,3},{13,5},{15,7},{24,16},{26,... | collective-permute-start | bytes 30728 | tf_op jit(solution)/shard_map/ppermute | solution.py:17
  63.5 18.2 %collective-permute-start.5 = (f32[128,20]{0,1:T(8,128)}, f32[128,20]{0,1:T(8,128)S(1)}, u32[]{:S(2)}, u32[]{:S(2)}) collective-permute-start(f32[128,20]{0,1:T(8,128)} %get-tuple-element.93), channel_id=1, source_target_pairs={{0,8},{2,10},{4,12},{6,14},{1,9},{3,11},{5,13},{7,15},{16,24},{18,... | collective-permute-start | bytes 30728 | tf_op jit(solution)/shard_map/ppermute | solution.py:17
  64.9 2.9 %copy-start.5 = (bf16[256,2560]{0,1:T(8,128)(2,1)S(1)}, bf16[256,2560]{0,1:T(8,128)(2,1)}, u32[]{:S(2)}) copy-start(bf16[256,2560]{0,1:T(8,128)(2,1)} %get-tuple-element.62) | copy-start | bytes 3932164 | tf_op jit(solution)/shard_map/cond
  73.1 16.6 %copy-start.7 = (f32[128,20,128]{2,0,1:T(8,128)S(1)}, f32[128,20,128]{2,0,1:T(8,128)}, u32[]{:S(2)}) copy-start(f32[128,20,128]{2,0,1:T(8,128)} %copy-done.6) | copy-start | bytes 3932164
  73.8 15.8 %collective-permute-start.3 = (f32[128,20]{0,1:T(8,128)}, f32[128,20]{0,1:T(8,128)S(1)}, u32[]{:S(2)}, u32[]{:S(2)}) collective-permute-start(f32[128,20]{0,1:T(8,128)} %get-tuple-element.92), channel_id=1, source_target_pairs={{2,0},{4,2},{6,4},{8,6},{10,8},{12,10},{14,12},{3,1},{5,3},{7,5},{... | collective-permute-start | bytes 30728 | tf_op jit(solution)/shard_map/ppermute | solution.py:17
  75.1 15.8 %collective-permute-start.1 = (f32[128,20]{0,1:T(8,128)}, f32[128,20]{0,1:T(8,128)S(1)}, u32[]{:S(2)}, u32[]{:S(2)}) collective-permute-start(f32[128,20]{0,1:T(8,128)} %get-tuple-element.91), channel_id=1, source_target_pairs={{0,2},{2,4},{4,6},{6,8},{8,10},{10,12},{12,14},{1,3},{3,5},{5,7},{... | collective-permute-start | bytes 30728 | tf_op jit(solution)/shard_map/ppermute | solution.py:17
  80.4 102.2 %collective-permute-start.9 = (f32[128,20,128]{2,0,1:T(8,128)S(1)}, f32[128,20,128]{2,0,1:T(8,128)S(1)}, u32[]{:S(2)}, u32[]{:S(2)}) collective-permute-start(f32[128,20,128]{2,0,1:T(8,128)S(1)} %get-tuple-element.97), channel_id=1, source_target_pairs={{2,0},{4,2},{6,4},{8,6},{10,8},{12,10},{14,12},{3,1},{5,3},{7,5},{... | collective-permute-start | bytes 3932168 | tf_op jit(solution)/shard_map/ppermute | solution.py:17
  81.7 102.1 %collective-permute-start.10 = (f32[128,20,128]{2,0,1:T(8,128)}, f32[128,20,128]{2,0,1:T(8,128)S(1)}, u32[]{:S(2)}, u32[]{:S(2)}) collective-permute-start(f32[128,20,128]{2,0,1:T(8,128)} %copy-done.8), channel_id=1, source_target_pairs={{0,8},{2,10},{4,12},{6,14},{1,9},{3,11},{5,13},{7,15},{16,24},{18,... | collective-permute-start | bytes 3932168 | tf_op jit(solution)/shard_map/ppermute | solution.py:17
  89.6 95.3 %collective-permute-start.11 = (f32[128,20,128]{2,0,1:T(8,128)S(1)}, f32[128,20,128]{2,0,1:T(8,128)S(1)}, u32[]{:S(2)}, u32[]{:S(2)}) collective-permute-start(f32[128,20,128]{2,0,1:T(8,128)S(1)} %copy-done.7), channel_id=1, source_target_pairs={{8,0},{10,2},{12,4},{14,6},{9,1},{11,3},{13,5},{15,7},{24,16},{26,... | collective-permute-start | bytes 3932168 | tf_op jit(solution)/shard_map/ppermute | solution.py:17
  91.0 2.7 %collective-permute-start.12 = (f32[128,20]{0,1:T(8,128)S(1)}, f32[128,20]{0,1:T(8,128)S(1)}, u32[]{:S(2)}, u32[]{:S(2)}) collective-permute-start(f32[128,20]{0,1:T(8,128)S(1)} %get-tuple-element.101), channel_id=1, source_target_pairs={{0,2},{2,4},{4,6},{6,8},{8,10},{10,12},{12,14},{1,3},{3,5},{5,7},{... | collective-permute-start | bytes 30728 | tf_op jit(solution)/shard_map/ppermute | solution.py:17
  93.6 26.4 %collective-permute-start.13 = (f32[128,20]{0,1:T(8,128)S(1)}, f32[128,20]{0,1:T(8,128)S(1)}, u32[]{:S(2)}, u32[]{:S(2)}) collective-permute-start(f32[128,20]{0,1:T(8,128)S(1)} %get-tuple-element.102), channel_id=1, source_target_pairs={{2,0},{4,2},{6,4},{8,6},{10,8},{12,10},{14,12},{3,1},{5,3},{7,5},{... | collective-permute-start | bytes 30728 | tf_op jit(solution)/shard_map/ppermute | solution.py:17
  120.0 54.9 %collective-permute-start.14 = (f32[128,20]{0,1:T(8,128)S(1)}, f32[128,20]{0,1:T(8,128)S(1)}, u32[]{:S(2)}, u32[]{:S(2)}) collective-permute-start(f32[128,20]{0,1:T(8,128)S(1)} %get-tuple-element.103), channel_id=1, source_target_pairs={{0,8},{2,10},{4,12},{6,14},{1,9},{3,11},{5,13},{7,15},{16,24},{18,... | collective-permute-start | bytes 30728 | tf_op jit(solution)/shard_map/ppermute | solution.py:17
  174.9 6.5 %collective-permute-start.15 = (f32[128,20]{0,1:T(8,128)S(1)}, f32[128,20]{0,1:T(8,128)S(1)}, u32[]{:S(2)}, u32[]{:S(2)}) collective-permute-start(f32[128,20]{0,1:T(8,128)S(1)} %get-tuple-element.104), channel_id=1, source_target_pairs={{8,0},{10,2},{12,4},{14,6},{9,1},{11,3},{13,5},{15,7},{24,16},{26,... | collective-permute-start | bytes 30728 | tf_op jit(solution)/shard_map/ppermute | solution.py:17
  (3 other events, 5.3 us)
Sparse Core Ops, SparseCore 0:
  8.9 11.8 all-gather.2
  22.3 10.3 all-gather.4
where the time goes:
time: 201 us; the launch traced here: 199 us
  starting transfers between devices  94.6 us (47%)
  waiting for transfers between devices  50.5 us (25%)
  between operations  19.4 us (10%)
  other arithmetic  13.6 us (7%)
  local copies, waits for them, and re-layouts  12.6 us (6%)
  matrix products  8.67 us (4%)
    ppermute x16, starting transfers between devices, passed_along(): return lax.ppermute(value, axis, pairs)  94.5 us
    ppermute x16, waiting for transfers between devices, passed_along(): return lax.ppermute(value, axis, pairs)  49.7 us
    unnamed x20, local copies, waits for them, and re-layouts  8.36 us
    dot_general x2, matrix products, block_terms(): jnp.einsum('qhd,khd->hqk', query_heads, key_heads, preferred_element_type...  5.5 us
    reduce_sum x1, other arithmetic, combine(): numerator = jnp.sum(factors[..., None] * outs_all, axis=0)  4.58 us
  transfers between devices with their start and end apart: 18, of which 7 were waited for; matrix products, arithmetic and copies ran while one was open for 12% of the time, Pallas kernels for 0%

commit v1 on v0

v1 whole, which is shorter than its diff:
```python
import functools

import jax
import jax.numpy as jnp
from jax import lax
from jax.experimental import pallas as pl
from jax.experimental.pallas import tpu as pltpu
from jax.sharding import PartitionSpec as P

HD = 128
TILE_H = 4
OFFSETS = (0, -1, 1, -TILE_H, TILE_H)
SCALE = HD ** (-0.5) * 1.4426950408889634
FAR_BELOW = -1e30
HEADS_AT_ONCE = 4


def plan(rows):
    edges = []
    for to in range(rows):
        for number, offset in enumerate(OFFSETS):
            source = to + offset
            if offset == 0 or not 0 <= source < rows:
                continue
            if abs(offset) == 1 and source // TILE_H != to // TILE_H:
                continue
            place, up = source % TILE_H, to > source
            half = TILE_H // 2
            if abs(offset) == TILE_H:
                wanted = 0 if (place >= half) == up else 1
            elif source // 2 == to // 2:
                wanted = 2
            else:
                odd = (source // TILE_H) % 2 == 1
                wanted = 0 if up != odd else 1
            edges.append((abs(offset) != TILE_H, source, to, number, wanted))
    edges.sort()
    phases = [{}, {}, {}]
    for _, source, to, number, wanted in edges:
        order = [wanted] + list(range(3, len(phases))) + [len(phases)]
        for index in order:
            if index == len(phases):
                phases.append({})
            phase = phases[index]
            if source not in phase and all(t != to for t, _ in phase.values()):
                phase[source] = (to, number)
                break
    return phases


def scores_of(q, k_own, k_other):
    keys = jnp.concatenate([k_own, k_other], axis=0)
    return lax.dot_general(
        q, keys, (((1,), (1,)), ((), ())), preferred_element_type=jnp.float32
    ) * SCALE


def weighted(weights, v_own, v_other):
    return jnp.dot(
        weights.astype(jnp.bfloat16),
        jnp.concatenate([v_own, v_other], axis=0),
        preferred_element_type=jnp.float32,
    )


def absorb(live, head, q_ref, block, max_ref, total_ref, out_ref):
    k_own, k_other, v_own, v_other = block
    here = slice(head * HD, (head + 1) * HD)

    scores = scores_of(q_ref[:, here], k_own[:, here], k_other[:, here])
    before = max_ref[head]
    top = jnp.maximum(before, jnp.max(scores, axis=1, keepdims=True))
    weights = jnp.exp2(scores - top[:, :1])
    factor = jnp.exp2(before - top)
    max_ref[head] = top
    total_ref[head] = factor * total_ref[head] + jnp.sum(weights, axis=1, keepdims=True)
    out_ref[:, here] = factor * out_ref[:, here] + weighted(
        weights, v_own[:, here], v_other[:, here]
    )


def first_kernel(blocks, heads, live_ref, q_ref, *refs):
    kv = refs[: 4 * blocks]
    out_ref, stat_ref, max_ref, total_ref = refs[4 * blocks :]
    max_ref[...] = jnp.full_like(max_ref, FAR_BELOW)
    total_ref[...] = jnp.zeros_like(total_ref)
    out_ref[...] = jnp.zeros_like(out_ref)
    for number in range(blocks):
        block = kv[4 * number : 4 * number + 4]

        @pl.when(live_ref[number] == 1)
        def _():
            for head in range(heads):
                absorb(None, head, q_ref, block, max_ref, total_ref, out_ref)

    for head in range(heads):
        here = slice(head * HD, (head + 1) * HD)
        total = total_ref[head]
        out_ref[:, here] = out_ref[:, here] / total
        stat_ref[:, here] = max_ref[head] + jnp.log2(total)


def last_kernel(blocks, heads, live_ref, q_ref, *refs):
    kv = refs[: 4 * blocks]
    before_ref, stat_ref, out_ref, max_ref, total_ref, sum_ref = refs[4 * blocks :]
    for head in range(heads):
        here = slice(head * HD, (head + 1) * HD)
        max_ref[head] = stat_ref[:, here]
    total_ref[...] = jnp.ones_like(total_ref)
    sum_ref[...] = before_ref[...]
    for number in range(blocks):
        block = kv[4 * number : 4 * number + 4]

        @pl.when(live_ref[number] == 1)
        def _():
            for head in range(heads):
                absorb(None, head, q_ref, block, max_ref, total_ref, sum_ref)

    for head in range(heads):
        here = slice(head * HD, (head + 1) * HD)
        out_ref[:, here] = (sum_ref[:, here] / total_ref[head]).astype(out_ref.dtype)


def heads_at_once(heads):
    return max(n for n in range(1, HEADS_AT_ONCE + 1) if heads % n == 0)


def cost(tokens, keys, width, blocks):
    return pl.CostEstimate(
        flops=4 * tokens * keys * width * blocks,
        transcendentals=tokens * keys * (width // HD) * blocks,
        bytes_accessed=2 * width * (2 * tokens + 2 * keys * blocks),
    )


def attend_first(live, queries, blocks):
    tokens, width = queries.shape
    heads = heads_at_once(width // HD)
    chunk = pl.BlockSpec((tokens, heads * HD), lambda i: (0, i))
    return pl.pallas_call(
        functools.partial(first_kernel, len(blocks), heads),
        grid=(width // (heads * HD),),
        in_specs=[pl.BlockSpec(memory_space=pltpu.SMEM)] + [chunk] * (1 + 4 * len(blocks)),
        out_specs=[chunk, chunk],
        out_shape=[jax.ShapeDtypeStruct((tokens, width), jnp.float32)] * 2,
        scratch_shapes=[pltpu.VMEM((heads, tokens, HD), jnp.float32)] * 2,
        cost_estimate=cost(tokens, 2 * tokens, width, len(blocks)),
        name="attend_first",
    )(live, queries, *[a for block in blocks for a in block])


def attend_last(live, queries, blocks, before, stats):
    tokens, width = queries.shape
    heads = heads_at_once(width // HD)
    chunk = pl.BlockSpec((tokens, heads * HD), lambda i: (0, i))
    return pl.pallas_call(
        functools.partial(last_kernel, len(blocks), heads),
        grid=(width // (heads * HD),),
        in_specs=[pl.BlockSpec(memory_space=pltpu.SMEM)] + [chunk] * (3 + 4 * len(blocks)),
        out_specs=chunk,
        out_shape=jax.ShapeDtypeStruct((tokens, width), jnp.bfloat16),
        scratch_shapes=[pltpu.VMEM((heads, tokens, HD), jnp.float32)] * 2
        + [pltpu.VMEM((tokens, heads * HD), jnp.float32)],
        cost_estimate=cost(tokens, 2 * tokens, width, len(blocks)),
        name="attend_last",
    )(live, queries, *[a for block in blocks for a in block], before, stats)


def after(value, *others):
    return lax.optimization_barrier((value,) + others)[0]


def shards(phases, queries, keys, values, pattern):
    rows = lax.axis_size("row")
    cols = lax.axis_size("col")
    row = lax.axis_index("row")
    swap_pairs = [(c, cols - 1 - c) for c in range(cols)]

    def swapped(value):
        return lax.ppermute(value, "col", swap_pairs)

    def moved(value, phase):
        return lax.ppermute(value, "row", [(s, t) for s, (t, _) in sorted(phase.items())])

    flags = [jnp.ones((), jnp.int32)]
    own_row = lax.dynamic_index_in_dim(pattern, row, 0, keepdims=False)
    table = []
    for phase in phases:
        numbers = [len(OFFSETS)] * rows
        for to, number in phase.values():
            numbers[to] = number
        table.append(numbers)
    table = jnp.asarray(table, jnp.int32)[:, row]
    padded = jnp.concatenate([own_row, jnp.zeros((1,), jnp.int32)])
    arrived_live = jnp.sum(
        jnp.where(table[:, None] == jnp.arange(len(OFFSETS) + 1)[None, :], padded[None, :], 0), axis=1
    )

    x1, x2, near = phases[:3]
    k_x1 = moved(keys, x1)
    v_x1 = moved(values, x1)
    k_near = moved(keys, near)
    v_near = moved(values, near)
    k_own, v_own = swapped(keys), swapped(values)
    later = []
    for phase in [x2] + phases[3:]:
        later.append((moved(after(keys, k_x1), phase), moved(after(values, v_x1), phase)))

    def block(k, v):
        return (k, swapped(k), v, swapped(v))

    first = [(keys, k_own, values, v_own), block(k_near, v_near), block(k_x1, v_x1)]
    live_first = jnp.concatenate([jnp.ones((1,), jnp.int32), arrived_live[2:3], arrived_live[0:1]])
    before, stats = attend_first(live_first, queries, first)
    live_last = jnp.concatenate([arrived_live[1:2], arrived_live[3:]])
    return attend_last(live_last, queries, [block(k, v) for k, v in later], before, stats)


def solution(mesh):
    placed = P(("groups", "row", "col"), None)
    return jax.shard_map(
        functools.partial(shards, plan(mesh.shape["row"])),
        mesh=mesh,
        in_specs=(placed, placed, placed, P("groups", None)),
        out_specs=placed,
        check_vma=False,
    )
```

time: 201 us -> 115 us (0.57)
  the two profiles are of different devices: /device:TPU:0 before, /device:TPU:23 now
where the time goes in v1:
time: 115 us; the launch traced here: 114 us
  waiting for transfers between devices  61.9 us (54%)
  Pallas kernels  26.5 us (23%)
  starting transfers between devices  20.3 us (18%)
  local copies, waits for them, and re-layouts  3.09 us (3%)
  other arithmetic  2.16 us (2%)
    ppermute x6, waiting for transfers between devices, moved(): lax.ppermute(value, 'row', [(s, t) for s, (t, _) in sorted(phase.items())])  61.8 us
    pallas_call x1, Pallas kernels, attend_first(): pl.pallas_call(functools.partial(first_kernel, len(blocks), heads), grid=...  18 us
    ppermute x6, starting transfers between devices, moved(): lax.ppermute(value, 'row', [(s, t) for s, (t, _) in sorted(phase.items())])  10.6 us
    ppermute x8, starting transfers between devices, swapped(): return lax.ppermute(value, 'col', swap_pairs)  9.75 us
    pallas_call x1, Pallas kernels, attend_last(): pl.pallas_call(functools.partial(last_kernel, len(blocks), heads), grid=(...  8.51 us
  transfers between devices with their start and end apart: 14, of which 6 were waited for; matrix products, arithmetic and copies ran while one was open for 3% of the time, Pallas kernels for 16%

profile of v1, /device:TPU:23, one launch (start us, length us, event | category | flops | bytes accessed | tf_op | source)
XLA Modules:
  0.0 114.1 jit_solution(1989467265248441636)
XLA Ops:
  0.0 2.1 %collective-permute-start = (bf16[128,2560]{1,0:T(8,128)(2,1)}, bf16[128,2560]{1,0:T(8,128)(2,1)S(1)}, u32[]{:S(2)}, u32[]{:S(2)}) collective-permute-start(bf16[128,2560]{1,0:T(8,128)(2,1)} %refs_0_.1), channel_id=1, source_target_pairs={{2,4},{4,12},{6,14},{8,0},{10,2},{12,10},{3,5},{5,13},{7,15},{9,1}... | collective-permute-start | bytes 1966088 | tf_op jit(solution)/shard_map/ppermute | solution.py:183
  2.1 3.1 %collective-permute-start.3 = (bf16[128,2560]{1,0:T(8,128)(2,1)}, bf16[128,2560]{1,0:T(8,128)(2,1)S(1)}, u32[]{:S(2)}, u32[]{:S(2)}) collective-permute-start(bf16[128,2560]{1,0:T(8,128)(2,1)} %refs_2_.1), channel_id=1, source_target_pairs={{2,4},{4,12},{6,14},{8,0},{10,2},{12,10},{3,5},{5,13},{7,15},{9,1}... | collective-permute-start | bytes 1966088 | tf_op jit(solution)/shard_map/ppermute | solution.py:183
  5.3 1.5 %collective-permute-start.8 = (bf16[128,2560]{1,0:T(8,128)(2,1)}, bf16[128,2560]{1,0:T(8,128)(2,1)S(1)}, u32[]{:S(2)}, u32[]{:S(2)}) collective-permute-start(bf16[128,2560]{1,0:T(8,128)(2,1)} %refs_0_.1), channel_id=1, source_target_pairs={{0,2},{2,0},{4,6},{6,4},{8,10},{10,8},{12,14},{14,12},{1,3},{3,1},... | collective-permute-start | bytes 1966088 | tf_op jit(solution)/shard_map/ppermute | solution.py:183
  6.8 1.8 %collective-permute-start.6 = (bf16[128,2560]{1,0:T(8,128)(2,1)}, bf16[128,2560]{1,0:T(8,128)(2,1)S(1)}, u32[]{:S(2)}, u32[]{:S(2)}) collective-permute-start(bf16[128,2560]{1,0:T(8,128)(2,1)} %refs_0_.1), channel_id=1, source_target_pairs={{0,1},{1,0},{2,3},{3,2},{4,5},{5,4},{6,7},{7,6},{8,9},{9,8},{10,11... | collective-permute-start | bytes 1966088 | tf_op jit(solution)/shard_map/ppermute | solution.py:180
  8.6 10.2 %collective-permute-done.refs_8_ = bf16[128,2560]{1,0:T(8,128)(2,1)S(1)} collective-permute-done((bf16[128,2560]{1,0:T(8,128)(2,1)}, bf16[128,2560]{1,0:T(8,128)(2,1)S(1)}, u32[]{:S(2)}, u32[]{:S(2)}) %collective-permute-start) | collective-permute-done | bytes 655392 | tf_op jit(solution)/shard_map/ppermute | solution.py:183
  18.8 2.7 %collective-permute-start.7 = (bf16[128,2560]{1,0:T(8,128)(2,1)}, bf16[128,2560]{1,0:T(8,128)(2,1)}, u32[]{:S(2)}, u32[]{:S(2)}) collective-permute-start(bf16[128,2560]{1,0:T(8,128)(2,1)} %refs_2_.1), channel_id=1, source_target_pairs={{0,1},{1,0},{2,3},{3,2},{4,5},{5,4},{6,7},{7,6},{8,9},{9,8},{10,11... | collective-permute-start | bytes 1966088 | tf_op jit(solution)/shard_map/ppermute | solution.py:180
  21.5 11.3 %collective-permute-done.3.refs_10_ = bf16[128,2560]{1,0:T(8,128)(2,1)S(1)} collective-permute-done((bf16[128,2560]{1,0:T(8,128)(2,1)}, bf16[128,2560]{1,0:T(8,128)(2,1)S(1)}, u32[]{:S(2)}, u32[]{:S(2)}) %collective-permute-start.3) | collective-permute-done | bytes 655392 | tf_op jit(solution)/shard_map/ppermute | solution.py:183
  32.8 1.6 %collective-permute-start.12 = (bf16[128,2560]{1,0:T(8,128)(2,1)S(1)}, bf16[128,2560]{1,0:T(8,128)(2,1)}, u32[]{:S(2)}, u32[]{:S(2)}) collective-permute-start(bf16[128,2560]{1,0:T(8,128)(2,1)S(1)} %collective-permute-done.refs_8_), channel_id=1, source_target_pairs={{0,1},{1,0},{2,3},{3,2},{4,5},{5,4},{6,7},{7,6},{8,9},{9,8},{10,11... | collective-permute-start | bytes 1966088 | tf_op jit(solution)/shard_map/ppermute | solution.py:180
  34.4 13.4 %collective-permute-done.10.refs_6_ = bf16[128,2560]{1,0:T(8,128)(2,1)S(1)} collective-permute-done((bf16[128,2560]{1,0:T(8,128)(2,1)}, bf16[128,2560]{1,0:T(8,128)(2,1)S(1)}, u32[]{:S(2)}, u32[]{:S(2)}) %collective-permute-start.10) | collective-permute-done | bytes 655392 | tf_op jit(solution)/shard_map/ppermute | solution.py:183
  47.9 1.9 %collective-permute-start.1 = (bf16[128,2560]{1,0:T(8,128)(2,1)}, bf16[128,2560]{1,0:T(8,128)(2,1)}, u32[]{:S(2)}, u32[]{:S(2)}) collective-permute-start(bf16[128,2560]{1,0:T(8,128)(2,1)} %refs_0_.1), channel_id=1, source_target_pairs={{0,8},{2,10},{4,2},{10,12},{12,4},{14,6},{1,9},{3,11},{5,3},{11,13... | collective-permute-start | bytes 1966088 | tf_op jit(solution)/shard_map/ppermute | solution.py:183
  49.8 12.2 %collective-permute-done.8.refs_4_ = bf16[128,2560]{1,0:T(8,128)(2,1)S(1)} collective-permute-done((bf16[128,2560]{1,0:T(8,128)(2,1)}, bf16[128,2560]{1,0:T(8,128)(2,1)S(1)}, u32[]{:S(2)}, u32[]{:S(2)}) %collective-permute-start.8) | collective-permute-done | bytes 655392 | tf_op jit(solution)/shard_map/ppermute | solution.py:183
  62.0 1.9 %collective-permute-start.4 = (bf16[128,2560]{1,0:T(8,128)(2,1)}, bf16[128,2560]{1,0:T(8,128)(2,1)}, u32[]{:S(2)}, u32[]{:S(2)}) collective-permute-start(bf16[128,2560]{1,0:T(8,128)(2,1)} %refs_2_.1), channel_id=1, source_target_pairs={{0,8},{2,10},{4,2},{10,12},{12,4},{14,6},{1,9},{3,11},{5,3},{11,13... | collective-permute-start | bytes 1966088 | tf_op jit(solution)/shard_map/ppermute | solution.py:183
  64.0 0.5 collective-permute-start.13
  65.0 1.7 %collective-permute-done.1.refs_0_ = bf16[128,2560]{1,0:T(8,128)(2,1)} collective-permute-done((bf16[128,2560]{1,0:T(8,128)(2,1)}, bf16[128,2560]{1,0:T(8,128)(2,1)}, u32[]{:S(2)}, u32[]{:S(2)}) %collective-permute-start.1) | collective-permute-done | bytes 655392 | tf_op jit(solution)/shard_map/ppermute | solution.py:183
  66.7 1.4 %collective-permute-start.2 = (bf16[128,2560]{1,0:T(8,128)(2,1)}, bf16[128,2560]{1,0:T(8,128)(2,1)}, u32[]{:S(2)}, u32[]{:S(2)}) collective-permute-start(bf16[128,2560]{1,0:T(8,128)(2,1)} %collective-permute-done.1.refs_0_), channel_id=1, source_target_pairs={{0,1},{1,0},{2,3},{3,2},{4,5},{5,4},{6,7},{7,6},{8,9},{9,8},{10,11... | collective-permute-start | bytes 1966088 | tf_op jit(solution)/shard_map/ppermute | solution.py:180
  68.1 12.9 %collective-permute-done.4.refs_2_ = bf16[128,2560]{1,0:T(8,128)(2,1)} collective-permute-done((bf16[128,2560]{1,0:T(8,128)(2,1)}, bf16[128,2560]{1,0:T(8,128)(2,1)}, u32[]{:S(2)}, u32[]{:S(2)}) %collective-permute-start.4) | collective-permute-done | bytes 655392 | tf_op jit(solution)/shard_map/ppermute | solution.py:183
  81.0 1.2 %collective-permute-start.5 = (bf16[128,2560]{1,0:T(8,128)(2,1)}, bf16[128,2560]{1,0:T(8,128)(2,1)}, u32[]{:S(2)}, u32[]{:S(2)}) collective-permute-start(bf16[128,2560]{1,0:T(8,128)(2,1)} %collective-permute-done.4.refs_2_), channel_id=1, source_target_pairs={{0,1},{1,0},{2,3},{3,2},{4,5},{5,4},{6,7},{7,6},{8,9},{9,8},{10,11... | collective-permute-start | bytes 1966088 | tf_op jit(solution)/shard_map/ppermute | solution.py:180
  82.3 0.7 dynamic-slice_bitcast_fusion.1
  83.2 0.7 fusion
  83.9 1.9 %pad_add_fusion.1.live_ref = s32[3]{0:T(128)} fusion(s32[1]{0:T(128)} %get-tuple-element.14, s32[1]{0:T(128)} %get-tuple-element.13, s32[1]{0:T(128)} %constant.19.clone.1), kind=kLoop, calls=%fused_computation.3 | loop fusion | flops 6 | bytes 24 | tf_op jit(solution)/shard_map/concatenate | solution.py:213
  85.8 0.9 copy-done.6
  86.6 0.9 copy-done.7
  87.5 18.0 %attend_first.1 = (f32[128,2560]{1,0:T(8,128)}, f32[128,2560]{1,0:T(8,128)}) custom-call(s32[3]{0:T(128)} %pad_add_fusion.1.live_ref, bf16[128,2560]{1,0:T(8,128)(2,1)} %q_ref.3, bf16[128,2560]{1,0:T(8,128)(2,1)} %refs_0_.1, bf16[128,2560]{1,0:T(8,128)(2,1)} %copy-done.5, bf16[128,2560]{1,0:T(8,128)(2,1)} %refs_2_.1, ...), custom_call_target="tpu_custom_call" | custom-call | flops 1006632960 | bytes 9175040 | tf_op jit(solution)/shard_map/attend_first/pallas_call | solution.py:140
  105.6 8.5 %attend_last.1 = bf16[128,2560]{1,0:T(8,128)(2,1)} custom-call(s32[1]{0:T(128)} %get-tuple-element.15.live_ref, bf16[128,2560]{1,0:T(8,128)(2,1)} %q_ref.3, bf16[128,2560]{1,0:T(8,128)(2,1)} %collective-permute-done.1.refs_0_, bf16[128,2560]{1,0:T(8,128)(2,1)} %collective-permute-done.2.refs_1_, bf16[128,2560]{1,0:T(8,128)(2,1)} %collective-permute-done.4.refs_2_, ...), custom_call_target="tpu_custom_call" | custom-call | flops 335544320 | bytes 3932160 | tf_op jit(solution)/shard_map/attend_last/pallas_call | solution.py:156
  (28 shorter events, 0.9 us)
Async XLA Ops:
  0.0 64.9 %copy-start = (s32[8,5]{1,0:T(8,128)S(1)}, s32[8,5]{1,0:T(8,128)}, u32[]{:S(2)}) copy-start(s32[8,5]{1,0:T(8,128)} %param.8) | copy-start | bytes 484
  0.0 18.8 %collective-permute-start = (bf16[128,2560]{1,0:T(8,128)(2,1)}, bf16[128,2560]{1,0:T(8,128)(2,1)S(1)}, u32[]{:S(2)}, u32[]{:S(2)}) collective-permute-start(bf16[128,2560]{1,0:T(8,128)(2,1)} %refs_0_.1), channel_id=1, source_target_pairs={{2,4},{4,12},{6,14},{8,0},{10,2},{12,10},{3,5},{5,13},{7,15},{9,1}... | collective-permute-start | bytes 1966088 | tf_op jit(solution)/shard_map/ppermute | solution.py:183
  2.1 30.7 %collective-permute-start.3 = (bf16[128,2560]{1,0:T(8,128)(2,1)}, bf16[128,2560]{1,0:T(8,128)(2,1)S(1)}, u32[]{:S(2)}, u32[]{:S(2)}) collective-permute-start(bf16[128,2560]{1,0:T(8,128)(2,1)} %refs_2_.1), channel_id=1, source_target_pairs={{2,4},{4,12},{6,14},{8,0},{10,2},{12,10},{3,5},{5,13},{7,15},{9,1}... | collective-permute-start | bytes 1966088 | tf_op jit(solution)/shard_map/ppermute | solution.py:183
  5.3 42.6 %collective-permute-start.10 = (bf16[128,2560]{1,0:T(8,128)(2,1)}, bf16[128,2560]{1,0:T(8,128)(2,1)S(1)}, u32[]{:S(2)}, u32[]{:S(2)}) collective-permute-start(bf16[128,2560]{1,0:T(8,128)(2,1)} %refs_2_.1), channel_id=1, source_target_pairs={{0,2},{2,0},{4,6},{6,4},{8,10},{10,8},{12,14},{14,12},{1,3},{3,1},... | collective-permute-start | bytes 1966088 | tf_op jit(solution)/shard_map/ppermute | solution.py:183
  5.3 56.7 %collective-permute-start.8 = (bf16[128,2560]{1,0:T(8,128)(2,1)}, bf16[128,2560]{1,0:T(8,128)(2,1)S(1)}, u32[]{:S(2)}, u32[]{:S(2)}) collective-permute-start(bf16[128,2560]{1,0:T(8,128)(2,1)} %refs_0_.1), channel_id=1, source_target_pairs={{0,2},{2,0},{4,6},{6,4},{8,10},{10,8},{12,14},{14,12},{1,3},{3,1},... | collective-permute-start | bytes 1966088 | tf_op jit(solution)/shard_map/ppermute | solution.py:183
  6.8 57.2 %collective-permute-start.6 = (bf16[128,2560]{1,0:T(8,128)(2,1)}, bf16[128,2560]{1,0:T(8,128)(2,1)S(1)}, u32[]{:S(2)}, u32[]{:S(2)}) collective-permute-start(bf16[128,2560]{1,0:T(8,128)(2,1)} %refs_0_.1), channel_id=1, source_target_pairs={{0,1},{1,0},{2,3},{3,2},{4,5},{5,4},{6,7},{7,6},{8,9},{9,8},{10,11... | collective-permute-start | bytes 1966088 | tf_op jit(solution)/shard_map/ppermute | solution.py:180
  18.8 68.7 %copy-start.1 = (bf16[128,2560]{1,0:T(8,128)(2,1)}, bf16[128,2560]{1,0:T(8,128)(2,1)S(1)}, u32[]{:S(2)}) copy-start(bf16[128,2560]{1,0:T(8,128)(2,1)S(1)} %collective-permute-done.refs_8_) | copy-start | bytes 1966084
  18.8 45.6 %collective-permute-start.7 = (bf16[128,2560]{1,0:T(8,128)(2,1)}, bf16[128,2560]{1,0:T(8,128)(2,1)}, u32[]{:S(2)}, u32[]{:S(2)}) collective-permute-start(bf16[128,2560]{1,0:T(8,128)(2,1)} %refs_2_.1), channel_id=1, source_target_pairs={{0,1},{1,0},{2,3},{3,2},{4,5},{5,4},{6,7},{7,6},{8,9},{9,8},{10,11... | collective-permute-start | bytes 1966088 | tf_op jit(solution)/shard_map/ppermute | solution.py:180
  32.8 54.7 %copy-start.2 = (bf16[128,2560]{1,0:T(8,128)(2,1)}, bf16[128,2560]{1,0:T(8,128)(2,1)S(1)}, u32[]{:S(2)}) copy-start(bf16[128,2560]{1,0:T(8,128)(2,1)S(1)} %collective-permute-done.3.refs_10_) | copy-start | bytes 1966084
  32.8 31.7 %collective-permute-start.12 = (bf16[128,2560]{1,0:T(8,128)(2,1)S(1)}, bf16[128,2560]{1,0:T(8,128)(2,1)}, u32[]{:S(2)}, u32[]{:S(2)}) collective-permute-start(bf16[128,2560]{1,0:T(8,128)(2,1)S(1)} %collective-permute-done.refs_8_), channel_id=1, source_target_pairs={{0,1},{1,0},{2,3},{3,2},{4,5},{5,4},{6,7},{7,6},{8,9},{9,8},{10,11... | collective-permute-start | bytes 1966088 | tf_op jit(solution)/shard_map/ppermute | solution.py:180
  47.9 39.6 %copy-start.3 = (bf16[128,2560]{1,0:T(8,128)(2,1)}, bf16[128,2560]{1,0:T(8,128)(2,1)S(1)}, u32[]{:S(2)}) copy-start(bf16[128,2560]{1,0:T(8,128)(2,1)S(1)} %collective-permute-done.10.refs_6_) | copy-start | bytes 1966084
  47.9 18.8 %collective-permute-start.1 = (bf16[128,2560]{1,0:T(8,128)(2,1)}, bf16[128,2560]{1,0:T(8,128)(2,1)}, u32[]{:S(2)}, u32[]{:S(2)}) collective-permute-start(bf16[128,2560]{1,0:T(8,128)(2,1)} %refs_0_.1), channel_id=1, source_target_pairs={{0,8},{2,10},{4,2},{10,12},{12,4},{14,6},{1,9},{3,11},{5,3},{11,13... | collective-permute-start | bytes 1966088 | tf_op jit(solution)/shard_map/ppermute | solution.py:183
  62.0 25.5 %copy-start.4 = (bf16[128,2560]{1,0:T(8,128)(2,1)}, bf16[128,2560]{1,0:T(8,128)(2,1)S(1)}, u32[]{:S(2)}) copy-start(bf16[128,2560]{1,0:T(8,128)(2,1)S(1)} %collective-permute-done.8.refs_4_) | copy-start | bytes 1966084
  62.0 19.0 %collective-permute-start.4 = (bf16[128,2560]{1,0:T(8,128)(2,1)}, bf16[128,2560]{1,0:T(8,128)(2,1)}, u32[]{:S(2)}, u32[]{:S(2)}) collective-permute-start(bf16[128,2560]{1,0:T(8,128)(2,1)} %refs_2_.1), channel_id=1, source_target_pairs={{0,8},{2,10},{4,2},{10,12},{12,4},{14,6},{1,9},{3,11},{5,3},{11,13... | collective-permute-start | bytes 1966088 | tf_op jit(solution)/shard_map/ppermute | solution.py:183
  64.0 23.6 %copy-start.5 = (bf16[128,2560]{1,0:T(8,128)(2,1)}, bf16[128,2560]{1,0:T(8,128)(2,1)S(1)}, u32[]{:S(2)}) copy-start(bf16[128,2560]{1,0:T(8,128)(2,1)S(1)} %collective-permute-done.6.refs_1_) | copy-start | bytes 1966084
  64.0 21.8 %collective-permute-start.13 = (bf16[128,2560]{1,0:T(8,128)(2,1)S(1)}, bf16[128,2560]{1,0:T(8,128)(2,1)S(1)}, u32[]{:S(2)}, u32[]{:S(2)}) collective-permute-start(bf16[128,2560]{1,0:T(8,128)(2,1)S(1)} %collective-permute-done.3.refs_10_), channel_id=1, source_target_pairs={{0,1},{1,0},{2,3},{3,2},{4,5},{5,4},{6,7},{7,6},{8,9},{9,8},{10,11... | collective-permute-start | bytes 1966088 | tf_op jit(solution)/shard_map/ppermute | solution.py:180
  64.4 21.4 %collective-permute-start.11 = (bf16[128,2560]{1,0:T(8,128)(2,1)S(1)}, bf16[128,2560]{1,0:T(8,128)(2,1)S(1)}, u32[]{:S(2)}, u32[]{:S(2)}) collective-permute-start(bf16[128,2560]{1,0:T(8,128)(2,1)S(1)} %collective-permute-done.10.refs_6_), channel_id=1, source_target_pairs={{0,1},{1,0},{2,3},{3,2},{4,5},{5,4},{6,7},{7,6},{8,9},{9,8},{10,11... | collective-permute-start | bytes 1966088 | tf_op jit(solution)/shard_map/ppermute | solution.py:180
  64.6 23.0 %collective-permute-start.9 = (bf16[128,2560]{1,0:T(8,128)(2,1)S(1)}, bf16[128,2560]{1,0:T(8,128)(2,1)}, u32[]{:S(2)}, u32[]{:S(2)}) collective-permute-start(bf16[128,2560]{1,0:T(8,128)(2,1)S(1)} %collective-permute-done.8.refs_4_), channel_id=1, source_target_pairs={{0,1},{1,0},{2,3},{3,2},{4,5},{5,4},{6,7},{7,6},{8,9},{9,8},{10,11... | collective-permute-start | bytes 1966088 | tf_op jit(solution)/shard_map/ppermute | solution.py:180
  66.7 38.9 %collective-permute-start.2 = (bf16[128,2560]{1,0:T(8,128)(2,1)}, bf16[128,2560]{1,0:T(8,128)(2,1)}, u32[]{:S(2)}, u32[]{:S(2)}) collective-permute-start(bf16[128,2560]{1,0:T(8,128)(2,1)} %collective-permute-done.1.refs_0_), channel_id=1, source_target_pairs={{0,1},{1,0},{2,3},{3,2},{4,5},{5,4},{6,7},{7,6},{8,9},{9,8},{10,11... | collective-permute-start | bytes 1966088 | tf_op jit(solution)/shard_map/ppermute | solution.py:180
  81.0 24.5 %collective-permute-start.5 = (bf16[128,2560]{1,0:T(8,128)(2,1)}, bf16[128,2560]{1,0:T(8,128)(2,1)}, u32[]{:S(2)}, u32[]{:S(2)}) collective-permute-start(bf16[128,2560]{1,0:T(8,128)(2,1)} %collective-permute-done.4.refs_2_), channel_id=1, source_target_pairs={{0,1},{1,0},{2,3},{3,2},{4,5},{5,4},{6,7},{7,6},{8,9},{9,8},{10,11... | collective-permute-start | bytes 1966088 | tf_op jit(solution)/shard_map/ppermute | solution.py:180
  85.8 0.9 copy-start.6
  86.6 0.9 copy-start.7

commit v2 on v0

v2 whole, which is shorter than its diff:
```python
import functools

import jax
import jax.numpy as jnp
from jax import lax
from jax.experimental import pallas as pl
from jax.experimental.pallas import tpu as pltpu
from jax.sharding import PartitionSpec as P


HD = 128
TILE_H = 4
OFFSETS = (0, -1, 1, -TILE_H, TILE_H)
SCALE = HD ** (-0.5) * 1.4426950408889634
FAR_BELOW = -1e30
HEADS_AT_ONCE = 4
VMEM_BYTES = 16 * 1024 * 1024


def plan(rows):
    edges = []
    for to in range(rows):
        for number, offset in enumerate(OFFSETS):
            source = to + offset
            if offset == 0 or not 0 <= source < rows:
                continue
            if abs(offset) == 1 and source // TILE_H != to // TILE_H:
                continue
            low = min(source, to)
            odd = (low // TILE_H) % 2
            late = low % TILE_H >= TILE_H // 2
            if abs(offset) == TILE_H:
                wanted = (0 if not late else 2) if not odd else None
            else:
                crossing = low % 2 == 1
                wanted = 1 if crossing == bool(odd) else 3
            edges.append((wanted is None, low, source, to, number, wanted))
    edges.sort()
    phases = [{}, {}, {}, {}]
    for _, _, source, to, number, wanted in edges:
        order = [] if wanted is None else [wanted]
        order += list(range(4, len(phases))) + [len(phases)]
        for index in order:
            if index == len(phases):
                phases.append({})
            phase = phases[index]
            if source not in phase and all(t != to for t, _ in phase.values()):
                phase[source] = (to, number)
                break
    return phases[:2] + phases[4:], phases[2:4]


def scores_of(q, keys, biases):
    scores = [
        lax.dot_general(q, k, (((1,), (1,)), ((), ())), preferred_element_type=jnp.float32) * SCALE
        for k in keys
    ]
    return [s if b is None else s + b for s, b in zip(scores, biases)]


def first_kernel(blocks, heads, bias_ref, q_ref, *refs):
    kv = refs[: 4 * blocks]
    out_ref, stat_ref = refs[4 * blocks :]
    for head in range(heads):
        here = slice(head * HD, (head + 1) * HD)
        keys, values, biases = [], [], []
        for number in range(blocks):
            k_own, k_other, v_own, v_other = kv[4 * number : 4 * number + 4]
            keys.append(jnp.concatenate([k_own[:, here], k_other[:, here]], axis=0))
            values += [v_own[:, here], v_other[:, here]]
            biases.append(None if number == 0 else bias_ref[number - 1])
        scores = jnp.concatenate(scores_of(q_ref[:, here], keys, biases), axis=1)
        top = jnp.max(scores, axis=1, keepdims=True)
        weights = jnp.exp2(scores - top)
        total = jnp.sum(weights, axis=1, keepdims=True)
        out = jnp.dot(
            weights.astype(jnp.bfloat16),
            jnp.concatenate(values, axis=0),
            preferred_element_type=jnp.float32,
        )
        out_ref[:, here] = out / total
        stat_ref[:, here] = jnp.broadcast_to(top + jnp.log2(total), out.shape)


def weigh_kernel(blocks, heads, bias_ref, q_ref, *refs):
    k_refs = refs[: 2 * blocks]
    before_ref, stat_ref = refs[2 * blocks : 2 * blocks + 2]
    weight_refs, base_ref = refs[2 * blocks + 2 : -1], refs[-1]
    keys_each = 2 * k_refs[0].shape[0]
    for head in range(heads):
        here = slice(head * HD, (head + 1) * HD)
        keys = [
            jnp.concatenate([k_refs[2 * n][:, here], k_refs[2 * n + 1][:, here]], axis=0)
            for n in range(blocks)
        ]
        biases = [bias_ref[n] for n in range(blocks)]
        scores = jnp.concatenate(scores_of(q_ref[:, here], keys, biases), axis=1)
        before = stat_ref[:, here][:, :1]
        top = jnp.maximum(before, jnp.max(scores, axis=1, keepdims=True))
        weights = jnp.exp2(scores - top)
        factor = jnp.exp2(before - top)
        inverse = 1.0 / (factor + jnp.sum(weights, axis=1, keepdims=True))
        weights = (weights * inverse).astype(jnp.bfloat16)
        for n in range(blocks):
            weight_refs[n][:, head * keys_each : (head + 1) * keys_each] = weights[
                :, n * keys_each : (n + 1) * keys_each
            ]
        base_ref[:, here] = before_ref[:, here] * (factor * inverse)


def last_kernel(blocks, heads, base_ref, *refs):
    weight_refs, v_refs, out_ref = refs[:blocks], refs[blocks : 3 * blocks], refs[-1]
    keys_each = 2 * v_refs[0].shape[0]
    for head in range(heads):
        here = slice(head * HD, (head + 1) * HD)
        weights = [w[:, head * keys_each : (head + 1) * keys_each] for w in weight_refs]
        out = jnp.dot(
            jnp.concatenate(weights, axis=1),
            jnp.concatenate([v[:, here] for v in v_refs], axis=0),
            preferred_element_type=jnp.float32,
        )
        out_ref[:, here] = (base_ref[:, here] + out).astype(out_ref.dtype)


def heads_at_once(heads):
    return max(n for n in range(1, HEADS_AT_ONCE + 1) if heads % n == 0)


def chunked(kernel, scalars, operands, out_types, blocks, dots):
    tokens, width = operands[0].shape
    heads = heads_at_once(width // HD)
    steps = width // (heads * HD)

    def spec(shape):
        return pl.BlockSpec((shape[0], shape[1] // steps), lambda i: (0, i))

    return pl.pallas_call(
        functools.partial(kernel, blocks, heads),
        grid=(steps,),
        in_specs=[pl.BlockSpec(memory_space=pltpu.SMEM)] * len(scalars)
        + [spec(a.shape) for a in operands],
        out_specs=[spec(t.shape) for t in out_types],
        out_shape=out_types,
        cost_estimate=pl.CostEstimate(
            flops=dots * 2 * tokens * 2 * tokens * width * blocks,
            transcendentals=tokens * 2 * tokens * (width // HD) * blocks,
            bytes_accessed=sum(a.size * a.dtype.itemsize for a in operands)
            + sum(t.size * t.dtype.itemsize for t in out_types),
        ),
        compiler_params=pltpu.CompilerParams(vmem_limit_bytes=VMEM_BYTES),
    )(*scalars, *operands)


def after(value, *others):
    return lax.optimization_barrier((value,) + others)[0]


def shards(stages, queries, keys, values, pattern):
    tokens, width = queries.shape
    rows = lax.axis_size("row")
    cols = lax.axis_size("col")
    row = lax.axis_index("row")

    def moved(value, phase):
        return lax.ppermute(value, "row", [(s, t) for s, (t, _) in sorted(phase.items())])

    def swapped(value, phase=None):
        reached = range(rows) if phase is None else sorted(t for t, _ in phase.values())
        pairs = [(r * cols + c, r * cols + cols - 1 - c) for r in reached for c in range(cols)]
        return lax.ppermute(value, ("row", "col"), pairs)

    def biases(stage):
        table = [[len(OFFSETS)] * len(stage) for _ in range(rows)]
        for index, phase in enumerate(stage):
            for to, number in phase.values():
                table[to][index] = number
        picks = jnp.asarray(table, jnp.int32)[row]
        here = jnp.arange(len(OFFSETS), dtype=jnp.int32)[None, :] == picks[:, None]
        live = jnp.sum(jnp.where(here, own_row, 0), axis=1)
        return jnp.where(live == 1, 0.0, FAR_BELOW).astype(jnp.float32)

    own_row = lax.dynamic_index_in_dim(pattern, row, 0, keepdims=True)
    early, late = stages
    k_early = [moved(keys, p) for p in early]
    v_early = [moved(values, p) for p in early]
    k_swap, v_swap = swapped(keys), swapped(values)
    k_again = after(keys, *k_early)
    v_again = after(values, *k_early)
    k_late = [moved(k_again, p) for p in late]
    v_late = [moved(v_again, p) for p in late]

    blocks = [keys, k_swap, values, v_swap]
    for k, v, p in zip(k_early, v_early, early):
        blocks += [k, swapped(k, p), v, swapped(v, p)]
    full = jax.ShapeDtypeStruct((tokens, width), jnp.float32)
    before, stats = chunked(
        first_kernel, [biases(early)], [queries] + blocks, [full] * 2, 1 + len(early), 2
    )
    k_both = []
    for k, p in zip(k_late, late):
        k_both += [k, swapped(k, p)]
    weight = jax.ShapeDtypeStruct((tokens, width // HD * 2 * tokens), jnp.bfloat16)
    *weights, base = chunked(
        weigh_kernel, [biases(late)], [queries] + k_both + [before, stats],
        [weight] * len(late) + [full], len(late), 1,
    )
    v_both = []
    for v, p in zip(v_late, late):
        v_both += [v, swapped(v, p)]
    out = jax.ShapeDtypeStruct((tokens, width), queries.dtype)
    return chunked(last_kernel, [], [base] + weights + v_both, [out], len(late), 1)[0]


def solution(mesh):
    placed = P(("groups", "row", "col"), None)
    stages = plan(mesh.shape["row"])

    def body(*args):
        return shards(stages, *args)

    return jax.shard_map(
        body,
        mesh=mesh,
        in_specs=(placed, placed, placed, P("groups", None)),
        out_specs=placed,
        check_vma=False,
    )
```

time: 201 us -> 111 us (0.55)
  the two profiles are of different devices: /device:TPU:0 before, /device:TPU:5 now
where the time goes in v2:
time: 111 us; the launch traced here: 110 us
  starting transfers between devices  47.4 us (43%)
  waiting for transfers between devices  29 us (26%)
  Pallas kernels  23.1 us (21%)
  local copies, waits for them, and re-layouts  9.77 us (9%)
    ppermute x8, waiting for transfers between devices, moved(): lax.ppermute(value, 'row', [(s, t) for s, (t, _) in sorted(phase.items())])  28.9 us
    ppermute x10, starting transfers between devices, swapped(): return lax.ppermute(value, ('row', 'col'), pairs)  26.2 us
    pallas_call x3, Pallas kernels, chunked(): pl.pallas_call(functools.partial(kernel, blocks, heads), grid=(steps,), i...  23.1 us
    ppermute x8, starting transfers between devices, moved(): lax.ppermute(value, 'row', [(s, t) for s, (t, _) in sorted(phase.items())])  21.2 us
    unnamed x22, local copies, waits for them, and re-layouts  9.03 us
  transfers between devices with their start and end apart: 18, of which 5 were waited for; matrix products, arithmetic and copies ran while one was open for 1% of the time, Pallas kernels for 17%

profile of v2, /device:TPU:5, one launch (start us, length us, event | category | flops | bytes accessed | tf_op | source)
XLA Modules:
  0.0 109.8 jit_solution(11709767640382198586)
XLA Ops:
  0.0 2.0 %collective-permute-start.1 = (bf16[128,2560]{1,0:T(8,128)(2,1)}, bf16[128,2560]{1,0:T(8,128)(2,1)S(1)}, u32[]{:S(2)}, u32[]{:S(2)}) collective-permute-start(bf16[128,2560]{1,0:T(8,128)(2,1)} %refs_0_.1), channel_id=1, source_target_pairs={{0,2},{2,0},{4,6},{6,4},{10,12},{12,10},{1,3},{3,1},{5,7},{7,5},{1... | collective-permute-start | bytes 1966088 | tf_op jit(solution)/shard_map/ppermute | solution.py:165
  2.1 5.4 %collective-permute-start = (bf16[128,2560]{1,0:T(8,128)(2,1)}, bf16[128,2560]{1,0:T(8,128)(2,1)S(1)}, u32[]{:S(2)}, u32[]{:S(2)}) collective-permute-start(bf16[128,2560]{1,0:T(8,128)(2,1)} %refs_0_.1), channel_id=1, source_target_pairs={{0,8},{2,10},{8,0},{10,2},{1,9},{3,11},{9,1},{11,3},{16,24},{18,26... | collective-permute-start | bytes 1966088 | tf_op jit(solution)/shard_map/ppermute | solution.py:165
  7.5 1.9 %collective-permute-start.9 = (bf16[128,2560]{1,0:T(8,128)(2,1)}, bf16[128,2560]{1,0:T(8,128)(2,1)S(1)}, u32[]{:S(2)}, u32[]{:S(2)}) collective-permute-start(bf16[128,2560]{1,0:T(8,128)(2,1)} %refs_2_.1), channel_id=1, source_target_pairs={{0,8},{2,10},{8,0},{10,2},{1,9},{3,11},{9,1},{11,3},{16,24},{18,26... | collective-permute-start | bytes 1966088 | tf_op jit(solution)/shard_map/ppermute | solution.py:165
  9.4 2.2 %collective-permute-start.12 = (bf16[128,2560]{1,0:T(8,128)(2,1)}, bf16[128,2560]{1,0:T(8,128)(2,1)S(1)}, u32[]{:S(2)}, u32[]{:S(2)}) collective-permute-start(bf16[128,2560]{1,0:T(8,128)(2,1)} %refs_2_.1), channel_id=1, source_target_pairs={{0,2},{2,0},{4,6},{6,4},{10,12},{12,10},{1,3},{3,1},{5,7},{7,5},{1... | collective-permute-start | bytes 1966088 | tf_op jit(solution)/shard_map/ppermute | solution.py:165
  11.6 1.9 %collective-permute-start.6 = (bf16[128,2560]{1,0:T(8,128)(2,1)}, bf16[128,2560]{1,0:T(8,128)(2,1)S(1)}, u32[]{:S(2)}, u32[]{:S(2)}) collective-permute-start(bf16[128,2560]{1,0:T(8,128)(2,1)} %refs_0_.1), channel_id=1, source_target_pairs={{0,1},{1,0},{2,3},{3,2},{4,5},{5,4},{6,7},{7,6},{8,9},{9,8},{10,11... | collective-permute-start | bytes 1966088 | tf_op jit(solution)/shard_map/ppermute | solution.py:170
  13.5 4.4 %collective-permute-done.1.refs_8_ = bf16[128,2560]{1,0:T(8,128)(2,1)S(1)} collective-permute-done((bf16[128,2560]{1,0:T(8,128)(2,1)}, bf16[128,2560]{1,0:T(8,128)(2,1)S(1)}, u32[]{:S(2)}, u32[]{:S(2)}) %collective-permute-start.1) | collective-permute-done | bytes 655392 | tf_op jit(solution)/shard_map/ppermute | solution.py:165
  17.8 2.7 %collective-permute-start.7 = (bf16[128,2560]{1,0:T(8,128)(2,1)}, bf16[128,2560]{1,0:T(8,128)(2,1)S(1)}, u32[]{:S(2)}, u32[]{:S(2)}) collective-permute-start(bf16[128,2560]{1,0:T(8,128)(2,1)} %refs_2_.1), channel_id=1, source_target_pairs={{0,1},{1,0},{2,3},{3,2},{4,5},{5,4},{6,7},{7,6},{8,9},{9,8},{10,11... | collective-permute-start | bytes 1966088 | tf_op jit(solution)/shard_map/ppermute | solution.py:170
  20.5 1.4 %collective-permute-done.refs_4_ = bf16[128,2560]{1,0:T(8,128)(2,1)S(1)} collective-permute-done((bf16[128,2560]{1,0:T(8,128)(2,1)}, bf16[128,2560]{1,0:T(8,128)(2,1)S(1)}, u32[]{:S(2)}, u32[]{:S(2)}) %collective-permute-start) | collective-permute-done | bytes 655392 | tf_op jit(solution)/shard_map/ppermute | solution.py:165
  21.9 4.6 %collective-permute-start.11 = (bf16[128,2560]{1,0:T(8,128)(2,1)S(1)}, bf16[128,2560]{1,0:T(8,128)(2,1)S(1)}, u32[]{:S(2)}, u32[]{:S(2)}) collective-permute-start(bf16[128,2560]{1,0:T(8,128)(2,1)S(1)} %collective-permute-done.1.refs_8_), channel_id=1, source_target_pairs={{0,1},{1,0},{2,3},{3,2},{4,5},{5,4},{6,7},{7,6},{10,11},{11,10},{1... | collective-permute-start | bytes 1966088 | tf_op jit(solution)/shard_map/ppermute | solution.py:170
  26.4 9.5 %collective-permute-done.9.refs_6_ = bf16[128,2560]{1,0:T(8,128)(2,1)S(1)} collective-permute-done((bf16[128,2560]{1,0:T(8,128)(2,1)}, bf16[128,2560]{1,0:T(8,128)(2,1)S(1)}, u32[]{:S(2)}, u32[]{:S(2)}) %collective-permute-start.9) | collective-permute-done | bytes 655392 | tf_op jit(solution)/shard_map/ppermute | solution.py:165
  35.9 3.4 %collective-permute-start.8 = (bf16[128,2560]{1,0:T(8,128)(2,1)S(1)}, bf16[128,2560]{1,0:T(8,128)(2,1)S(1)}, u32[]{:S(2)}, u32[]{:S(2)}) collective-permute-start(bf16[128,2560]{1,0:T(8,128)(2,1)S(1)} %collective-permute-done.refs_4_), channel_id=1, source_target_pairs={{0,1},{1,0},{2,3},{3,2},{8,9},{9,8},{10,11},{11,10},{16,17},{17,16... | collective-permute-start | bytes 1966088 | tf_op jit(solution)/shard_map/ppermute | solution.py:170
  39.4 1.9 %collective-permute-start.10 = (bf16[128,2560]{1,0:T(8,128)(2,1)S(1)}, bf16[128,2560]{1,0:T(8,128)(2,1)}, u32[]{:S(2)}, u32[]{:S(2)}) collective-permute-start(bf16[128,2560]{1,0:T(8,128)(2,1)S(1)} %collective-permute-done.9.refs_6_), channel_id=1, source_target_pairs={{0,1},{1,0},{2,3},{3,2},{8,9},{9,8},{10,11},{11,10},{16,17},{17,16... | collective-permute-start | bytes 1966088 | tf_op jit(solution)/shard_map/ppermute | solution.py:170
  41.3 1.5 %collective-permute-start.2 = (bf16[128,2560]{1,0:T(8,128)(2,1)}, bf16[128,2560]{1,0:T(8,128)(2,1)}, u32[]{:S(2)}, u32[]{:S(2)}) collective-permute-start(bf16[128,2560]{1,0:T(8,128)(2,1)} %refs_0_.1), channel_id=1, source_target_pairs={{4,12},{6,14},{12,4},{14,6},{5,13},{7,15},{13,5},{15,7},{20,28},{2... | collective-permute-start | bytes 1966088 | tf_op jit(solution)/shard_map/ppermute | solution.py:165
  43.6 1.9 %collective-permute-start.4 = (bf16[128,2560]{1,0:T(8,128)(2,1)}, bf16[128,2560]{1,0:T(8,128)(2,1)}, u32[]{:S(2)}, u32[]{:S(2)}) collective-permute-start(bf16[128,2560]{1,0:T(8,128)(2,1)} %refs_0_.1), channel_id=1, source_target_pairs={{2,4},{4,2},{8,10},{10,8},{12,14},{14,12},{3,5},{5,3},{9,11},{11,9... | collective-permute-start | bytes 1966088 | tf_op jit(solution)/shard_map/ppermute | solution.py:165
  46.4 1.5 %collective-permute-start.14 = (bf16[128,2560]{1,0:T(8,128)(2,1)}, bf16[128,2560]{1,0:T(8,128)(2,1)}, u32[]{:S(2)}, u32[]{:S(2)}) collective-permute-start(bf16[128,2560]{1,0:T(8,128)(2,1)} %refs_2_.1), channel_id=1, source_target_pairs={{4,12},{6,14},{12,4},{14,6},{5,13},{7,15},{13,5},{15,7},{20,28},{2... | collective-permute-start | bytes 1966088 | tf_op jit(solution)/shard_map/ppermute | solution.py:165
  48.8 4.7 %collective-permute-start.16 = (bf16[128,2560]{1,0:T(8,128)(2,1)}, bf16[128,2560]{1,0:T(8,128)(2,1)}, u32[]{:S(2)}, u32[]{:S(2)}) collective-permute-start(bf16[128,2560]{1,0:T(8,128)(2,1)} %refs_2_.1), channel_id=1, source_target_pairs={{2,4},{4,2},{8,10},{10,8},{12,14},{14,12},{3,5},{5,3},{9,11},{11,9... | collective-permute-start | bytes 1966088 | tf_op jit(solution)/shard_map/ppermute | solution.py:165
  54.2 3.0 %collective-permute-start.13 = (bf16[128,2560]{1,0:T(8,128)(2,1)S(1)}, bf16[128,2560]{1,0:T(8,128)(2,1)S(1)}, u32[]{:S(2)}, u32[]{:S(2)}) collective-permute-start(bf16[128,2560]{1,0:T(8,128)(2,1)S(1)} %collective-permute-done.12.refs_10_), channel_id=1, source_target_pairs={{0,1},{1,0},{2,3},{3,2},{4,5},{5,4},{6,7},{7,6},{10,11},{11,10},{1... | collective-permute-start | bytes 1966088 | tf_op jit(solution)/shard_map/ppermute | solution.py:170
  57.9 4.6 %collective-permute-done.4.refs_2_ = bf16[128,2560]{1,0:T(8,128)(2,1)} collective-permute-done((bf16[128,2560]{1,0:T(8,128)(2,1)}, bf16[128,2560]{1,0:T(8,128)(2,1)}, u32[]{:S(2)}, u32[]{:S(2)}) %collective-permute-start.4) | collective-permute-done | bytes 655392 | tf_op jit(solution)/shard_map/ppermute | solution.py:165
  62.5 4.2 %collective-permute-start.5 = (bf16[128,2560]{1,0:T(8,128)(2,1)}, bf16[128,2560]{1,0:T(8,128)(2,1)S(1)}, u32[]{:S(2)}, u32[]{:S(2)}) collective-permute-start(bf16[128,2560]{1,0:T(8,128)(2,1)} %collective-permute-done.4.refs_2_), channel_id=1, source_target_pairs={{2,3},{3,2},{4,5},{5,4},{8,9},{9,8},{10,11},{11,10},{12,13},{13,12... | collective-permute-start | bytes 1966088 | tf_op jit(solution)/shard_map/ppermute | solution.py:170
  67.5 9.1 %collective-permute-done.16.refs_4_ = bf16[128,2560]{1,0:T(8,128)(2,1)} collective-permute-done((bf16[128,2560]{1,0:T(8,128)(2,1)}, bf16[128,2560]{1,0:T(8,128)(2,1)}, u32[]{:S(2)}, u32[]{:S(2)}) %collective-permute-start.16) | collective-permute-done | bytes 655392 | tf_op jit(solution)/shard_map/ppermute | solution.py:165
  76.6 3.3 %collective-permute-start.17 = (bf16[128,2560]{1,0:T(8,128)(2,1)}, bf16[128,2560]{1,0:T(8,128)(2,1)S(1)}, u32[]{:S(2)}, u32[]{:S(2)}) collective-permute-start(bf16[128,2560]{1,0:T(8,128)(2,1)} %collective-permute-done.16.refs_4_), channel_id=1, source_target_pairs={{2,3},{3,2},{4,5},{5,4},{8,9},{9,8},{10,11},{11,10},{12,13},{13,12... | collective-permute-start | bytes 1966088 | tf_op jit(solution)/shard_map/ppermute | solution.py:170
  86.6 8.8 %shard_map.64 = (f32[128,2560]{1,0:T(8,128)S(1)}, f32[128,2560]{1,0:T(8,128)S(1)}) custom-call(f32[2]{0:T(128)S(1)} %compare_select_fusion.bias_ref, bf16[128,2560]{1,0:T(8,128)(2,1)S(1)} %copy-done.1, bf16[128,2560]{1,0:T(8,128)(2,1)S(1)} %copy-done.3, bf16[128,2560]{1,0:T(8,128)(2,1)S(1)} %collective-permute-done.6.refs_1_, ...), custom_call_target="tpu_custom_call" | custom-call | flops 1006632960 | bytes 11141120 | tf_op jit(solution)/shard_map/pallas_call | solution.py:137
  95.5 9.6 %shard_map.65 = (bf16[128,5120]{1,0:T(8,128)(2,1)S(1)}, bf16[128,5120]{1,0:T(8,128)(2,1)S(1)}, f32[128,2560]{1,0:T(8,128)S(1)}) custom-call(f32[2]{0:T(128)S(1)} %compare_select_fusion.2.bias_ref, bf16[128,2560]{1,0:T(8,128)(2,1)S(1)} %copy-done.2, bf16[128,2560]{1,0:T(8,128)(2,1)} %collective-permute-done.2.refs_0_, ...), custom_call_target="tpu_custom_call" | custom-call | flops 335544320 | bytes 9830400 | tf_op jit(solution)/shard_map/pallas_call | solution.py:137
  105.1 4.7 %shard_map.66 = bf16[128,2560]{1,0:T(8,128)(2,1)} custom-call(f32[128,2560]{1,0:T(8,128)S(1)} %get-tuple-element.15.base_ref, bf16[128,5120]{1,0:T(8,128)(2,1)S(1)} %get-tuple-element.16.refs_0_, bf16[128,5120]{1,0:T(8,128)(2,1)S(1)} %get-tuple-element.17.refs_1_, bf16[128,2560]{1,0:T(8,128)(2,1)} %collective-permute-done.14.refs_2_, ...), custom_call_target="tpu_custom_call" | custom-call | flops 335544320 | bytes 7208960 | tf_op jit(solution)/shard_map/pallas_call | solution.py:137
  (42 shorter events, 11.4 us)
Async XLA Ops:
  0.0 57.2 %copy-start = (s32[8,5]{1,0:T(8,128)S(1)}, s32[8,5]{1,0:T(8,128)}, u32[]{:S(2)}) copy-start(s32[8,5]{1,0:T(8,128)} %param.9) | copy-start | bytes 484
  0.0 17.8 %collective-permute-start.1 = (bf16[128,2560]{1,0:T(8,128)(2,1)}, bf16[128,2560]{1,0:T(8,128)(2,1)S(1)}, u32[]{:S(2)}, u32[]{:S(2)}) collective-permute-start(bf16[128,2560]{1,0:T(8,128)(2,1)} %refs_0_.1), channel_id=1, source_target_pairs={{0,2},{2,0},{4,6},{6,4},{10,12},{12,10},{1,3},{3,1},{5,7},{7,5},{1... | collective-permute-start | bytes 1966088 | tf_op jit(solution)/shard_map/ppermute | solution.py:165
  2.1 19.8 %collective-permute-start = (bf16[128,2560]{1,0:T(8,128)(2,1)}, bf16[128,2560]{1,0:T(8,128)(2,1)S(1)}, u32[]{:S(2)}, u32[]{:S(2)}) collective-permute-start(bf16[128,2560]{1,0:T(8,128)(2,1)} %refs_0_.1), channel_id=1, source_target_pairs={{0,8},{2,10},{8,0},{10,2},{1,9},{3,11},{9,1},{11,3},{16,24},{18,26... | collective-permute-start | bytes 1966088 | tf_op jit(solution)/shard_map/ppermute | solution.py:165
  7.5 28.4 %collective-permute-start.9 = (bf16[128,2560]{1,0:T(8,128)(2,1)}, bf16[128,2560]{1,0:T(8,128)(2,1)S(1)}, u32[]{:S(2)}, u32[]{:S(2)}) collective-permute-start(bf16[128,2560]{1,0:T(8,128)(2,1)} %refs_2_.1), channel_id=1, source_target_pairs={{0,8},{2,10},{8,0},{10,2},{1,9},{3,11},{9,1},{11,3},{16,24},{18,26... | collective-permute-start | bytes 1966088 | tf_op jit(solution)/shard_map/ppermute | solution.py:165
  9.4 29.9 %collective-permute-start.12 = (bf16[128,2560]{1,0:T(8,128)(2,1)}, bf16[128,2560]{1,0:T(8,128)(2,1)S(1)}, u32[]{:S(2)}, u32[]{:S(2)}) collective-permute-start(bf16[128,2560]{1,0:T(8,128)(2,1)} %refs_2_.1), channel_id=1, source_target_pairs={{0,2},{2,0},{4,6},{6,4},{10,12},{12,10},{1,3},{3,1},{5,7},{7,5},{1... | collective-permute-start | bytes 1966088 | tf_op jit(solution)/shard_map/ppermute | solution.py:165
  11.6 29.7 %collective-permute-start.6 = (bf16[128,2560]{1,0:T(8,128)(2,1)}, bf16[128,2560]{1,0:T(8,128)(2,1)S(1)}, u32[]{:S(2)}, u32[]{:S(2)}) collective-permute-start(bf16[128,2560]{1,0:T(8,128)(2,1)} %refs_0_.1), channel_id=1, source_target_pairs={{0,1},{1,0},{2,3},{3,2},{4,5},{5,4},{6,7},{7,6},{8,9},{9,8},{10,11... | collective-permute-start | bytes 1966088 | tf_op jit(solution)/shard_map/ppermute | solution.py:170
  17.8 25.0 %collective-permute-start.7 = (bf16[128,2560]{1,0:T(8,128)(2,1)}, bf16[128,2560]{1,0:T(8,128)(2,1)S(1)}, u32[]{:S(2)}, u32[]{:S(2)}) collective-permute-start(bf16[128,2560]{1,0:T(8,128)(2,1)} %refs_2_.1), channel_id=1, source_target_pairs={{0,1},{1,0},{2,3},{3,2},{4,5},{5,4},{6,7},{7,6},{8,9},{9,8},{10,11... | collective-permute-start | bytes 1966088 | tf_op jit(solution)/shard_map/ppermute | solution.py:170
  21.9 23.7 %collective-permute-start.11 = (bf16[128,2560]{1,0:T(8,128)(2,1)S(1)}, bf16[128,2560]{1,0:T(8,128)(2,1)S(1)}, u32[]{:S(2)}, u32[]{:S(2)}) collective-permute-start(bf16[128,2560]{1,0:T(8,128)(2,1)S(1)} %collective-permute-done.1.refs_8_), channel_id=1, source_target_pairs={{0,1},{1,0},{2,3},{3,2},{4,5},{5,4},{6,7},{7,6},{10,11},{11,10},{1... | collective-permute-start | bytes 1966088 | tf_op jit(solution)/shard_map/ppermute | solution.py:170
  35.9 12.0 %collective-permute-start.8 = (bf16[128,2560]{1,0:T(8,128)(2,1)S(1)}, bf16[128,2560]{1,0:T(8,128)(2,1)S(1)}, u32[]{:S(2)}, u32[]{:S(2)}) collective-permute-start(bf16[128,2560]{1,0:T(8,128)(2,1)S(1)} %collective-permute-done.refs_4_), channel_id=1, source_target_pairs={{0,1},{1,0},{2,3},{3,2},{8,9},{9,8},{10,11},{11,10},{16,17},{17,16... | collective-permute-start | bytes 1966088 | tf_op jit(solution)/shard_map/ppermute | solution.py:170
  39.4 14.8 %collective-permute-start.10 = (bf16[128,2560]{1,0:T(8,128)(2,1)S(1)}, bf16[128,2560]{1,0:T(8,128)(2,1)}, u32[]{:S(2)}, u32[]{:S(2)}) collective-permute-start(bf16[128,2560]{1,0:T(8,128)(2,1)S(1)} %collective-permute-done.9.refs_6_), channel_id=1, source_target_pairs={{0,1},{1,0},{2,3},{3,2},{8,9},{9,8},{10,11},{11,10},{16,17},{17,16... | collective-permute-start | bytes 1966088 | tf_op jit(solution)/shard_map/ppermute | solution.py:170
  41.3 15.9 %collective-permute-start.2 = (bf16[128,2560]{1,0:T(8,128)(2,1)}, bf16[128,2560]{1,0:T(8,128)(2,1)}, u32[]{:S(2)}, u32[]{:S(2)}) collective-permute-start(bf16[128,2560]{1,0:T(8,128)(2,1)} %refs_0_.1), channel_id=1, source_target_pairs={{4,12},{6,14},{12,4},{14,6},{5,13},{7,15},{13,5},{15,7},{20,28},{2... | collective-permute-start | bytes 1966088 | tf_op jit(solution)/shard_map/ppermute | solution.py:165
  43.6 18.9 %collective-permute-start.4 = (bf16[128,2560]{1,0:T(8,128)(2,1)}, bf16[128,2560]{1,0:T(8,128)(2,1)}, u32[]{:S(2)}, u32[]{:S(2)}) collective-permute-start(bf16[128,2560]{1,0:T(8,128)(2,1)} %refs_0_.1), channel_id=1, source_target_pairs={{2,4},{4,2},{8,10},{10,8},{12,14},{14,12},{3,5},{5,3},{9,11},{11,9... | collective-permute-start | bytes 1966088 | tf_op jit(solution)/shard_map/ppermute | solution.py:165
  46.4 20.3 %collective-permute-start.14 = (bf16[128,2560]{1,0:T(8,128)(2,1)}, bf16[128,2560]{1,0:T(8,128)(2,1)}, u32[]{:S(2)}, u32[]{:S(2)}) collective-permute-start(bf16[128,2560]{1,0:T(8,128)(2,1)} %refs_2_.1), channel_id=1, source_target_pairs={{4,12},{6,14},{12,4},{14,6},{5,13},{7,15},{13,5},{15,7},{20,28},{2... | collective-permute-start | bytes 1966088 | tf_op jit(solution)/shard_map/ppermute | solution.py:165
  48.8 27.8 %collective-permute-start.16 = (bf16[128,2560]{1,0:T(8,128)(2,1)}, bf16[128,2560]{1,0:T(8,128)(2,1)}, u32[]{:S(2)}, u32[]{:S(2)}) collective-permute-start(bf16[128,2560]{1,0:T(8,128)(2,1)} %refs_2_.1), channel_id=1, source_target_pairs={{2,4},{4,2},{8,10},{10,8},{12,14},{14,12},{3,5},{5,3},{9,11},{11,9... | collective-permute-start | bytes 1966088 | tf_op jit(solution)/shard_map/ppermute | solution.py:165
  54.2 25.9 %collective-permute-start.13 = (bf16[128,2560]{1,0:T(8,128)(2,1)S(1)}, bf16[128,2560]{1,0:T(8,128)(2,1)S(1)}, u32[]{:S(2)}, u32[]{:S(2)}) collective-permute-start(bf16[128,2560]{1,0:T(8,128)(2,1)S(1)} %collective-permute-done.12.refs_10_), channel_id=1, source_target_pairs={{0,1},{1,0},{2,3},{3,2},{4,5},{5,4},{6,7},{7,6},{10,11},{11,10},{1... | collective-permute-start | bytes 1966088 | tf_op jit(solution)/shard_map/ppermute | solution.py:170
  57.2 38.3 %collective-permute-start.3 = (bf16[128,2560]{1,0:T(8,128)(2,1)}, bf16[128,2560]{1,0:T(8,128)(2,1)S(1)}, u32[]{:S(2)}, u32[]{:S(2)}) collective-permute-start(bf16[128,2560]{1,0:T(8,128)(2,1)} %collective-permute-done.2.refs_0_), channel_id=1, source_target_pairs={{4,5},{5,4},{6,7},{7,6},{12,13},{13,12},{14,15},{15,14},{20,21},{2... | collective-permute-start | bytes 1966088 | tf_op jit(solution)/shard_map/ppermute | solution.py:170
  62.5 32.9 %collective-permute-start.5 = (bf16[128,2560]{1,0:T(8,128)(2,1)}, bf16[128,2560]{1,0:T(8,128)(2,1)S(1)}, u32[]{:S(2)}, u32[]{:S(2)}) collective-permute-start(bf16[128,2560]{1,0:T(8,128)(2,1)} %collective-permute-done.4.refs_2_), channel_id=1, source_target_pairs={{2,3},{3,2},{4,5},{5,4},{8,9},{9,8},{10,11},{11,10},{12,13},{13,12... | collective-permute-start | bytes 1966088 | tf_op jit(solution)/shard_map/ppermute | solution.py:170
  66.8 38.3 %collective-permute-start.15 = (bf16[128,2560]{1,0:T(8,128)(2,1)}, bf16[128,2560]{1,0:T(8,128)(2,1)S(1)}, u32[]{:S(2)}, u32[]{:S(2)}) collective-permute-start(bf16[128,2560]{1,0:T(8,128)(2,1)} %collective-permute-done.14.refs_2_), channel_id=1, source_target_pairs={{4,5},{5,4},{6,7},{7,6},{12,13},{13,12},{14,15},{15,14},{20,21},{2... | collective-permute-start | bytes 1966088 | tf_op jit(solution)/shard_map/ppermute | solution.py:170
  76.6 28.5 %collective-permute-start.17 = (bf16[128,2560]{1,0:T(8,128)(2,1)}, bf16[128,2560]{1,0:T(8,128)(2,1)S(1)}, u32[]{:S(2)}, u32[]{:S(2)}) collective-permute-start(bf16[128,2560]{1,0:T(8,128)(2,1)} %collective-permute-done.16.refs_4_), channel_id=1, source_target_pairs={{2,3},{3,2},{4,5},{5,4},{8,9},{9,8},{10,11},{11,10},{12,13},{13,12... | collective-permute-start | bytes 1966088 | tf_op jit(solution)/shard_map/ppermute | solution.py:170
  80.1 1.1 copy-start.1
  81.2 1.1 copy-start.3
  82.3 1.1 copy-start.4
  84.4 1.1 copy-start.8
  86.6 8.9 %copy-start.2 = (bf16[128,2560]{1,0:T(8,128)(2,1)S(1)}, bf16[128,2560]{1,0:T(8,128)(2,1)}, u32[]{:S(2)}) copy-start(bf16[128,2560]{1,0:T(8,128)(2,1)} %q_ref.3) | copy-start | bytes 1966084
  (5 other events, 4.7 us)

commit v3 on v2

--- a/solution.py
+++ b/solution.py
@@ -50,62 +50,84 @@
     return phases[:2] + phases[4:], phases[2:4]
 
 
-def scores_of(q, keys, biases):
-    scores = [
-        lax.dot_general(q, k, (((1,), (1,)), ((), ())), preferred_element_type=jnp.float32) * SCALE
-        for k in keys
-    ]
-    return [s if b is None else s + b for s, b in zip(scores, biases)]
-
-
-def first_kernel(blocks, heads, bias_ref, q_ref, *refs):
-    kv = refs[: 4 * blocks]
-    out_ref, stat_ref = refs[4 * blocks :]
-    for head in range(heads):
-        here = slice(head * HD, (head + 1) * HD)
-        keys, values, biases = [], [], []
-        for number in range(blocks):
-            k_own, k_other, v_own, v_other = kv[4 * number : 4 * number + 4]
-            keys.append(jnp.concatenate([k_own[:, here], k_other[:, here]], axis=0))
-            values += [v_own[:, here], v_other[:, here]]
-            biases.append(None if number == 0 else bias_ref[number - 1])
-        scores = jnp.concatenate(scores_of(q_ref[:, here], keys, biases), axis=1)
-        top = jnp.max(scores, axis=1, keepdims=True)
-        weights = jnp.exp2(scores - top)
-        total = jnp.sum(weights, axis=1, keepdims=True)
+def lanes(value):
+    return [value[:, at : at + HD] for at in range(0, value.shape[1], HD)]
+
+
+def over_row(reduce, join, slices):
+    found = reduce(functools.reduce(join, slices), axis=1, keepdims=True)
+    return jnp.broadcast_to(found, slices[0].shape)
+
+
+def merge_kernel(blocks, heads, merging, finishing, *refs):
+    refs = list(refs)
+    bias_ref = refs.pop(0) if merging else None
+    q_ref = refs.pop(0)
+    k_refs, refs = refs[: 2 * blocks], refs[2 * blocks :]
+    if finishing:
+        v_refs, refs = refs[: 2 * blocks], refs[2 * blocks :]
+    if merging:
+        before_ref, stat_ref, *refs = refs
+    if finishing:
+        out_ref, total_ref, score_ref, weight_ref = refs
+    else:
+        weight_refs, base_ref, score_ref = refs[:blocks], refs[blocks], refs[blocks + 1]
+    keys_each = 2 * k_refs[0].shape[0]
+    kept = {}
+
+    def score(head, here):
+        for n in range(blocks):
+            keys = jnp.concatenate([k_refs[2 * n][:, here], k_refs[2 * n + 1][:, here]], axis=0)
+            found = lax.dot_general(
+                q_ref[:, here], keys, (((1,), (1,)), ((), ())), preferred_element_type=jnp.float32
+            )
+            found = found * SCALE
+            if merging:
+                found = found + bias_ref[n]
+            score_ref[head, :, n * keys_each : (n + 1) * keys_each] = found
+
+    def weigh(head, here):
+        slices = lanes(score_ref[head])
+        top = over_row(jnp.max, jnp.maximum, slices)
+        if merging:
+            before = stat_ref[:, here]
+            top = jnp.maximum(top, before)
+        weights = [jnp.exp2(s - top) for s in slices]
+        total = over_row(jnp.sum, jnp.add, weights)
+        if merging:
+            factor = jnp.exp2(before - top)
+            total = total + factor
+        inverse = 1.0 / total
+        if finishing:
+            total_ref[:, here] = top + jnp.log2(total)
+            kept[head] = (inverse, factor * inverse if merging else None)
+            for at, w in enumerate(weights):
+                weight_ref[head, :, at * HD : (at + 1) * HD] = w.astype(jnp.bfloat16)
+        else:
+            base_ref[:, here] = before_ref[:, here] * (factor * inverse)
+            each = keys_each // HD
+            for at, w in enumerate(weights):
+                start = head * keys_each + at % each * HD
+                weight_refs[at // each][:, start : start + HD] = (w * inverse).astype(jnp.bfloat16)
+
+    def mix(head, here):
+        inverse, factor = kept.pop(head)
         out = jnp.dot(
-            weights.astype(jnp.bfloat16),
-            jnp.concatenate(values, axis=0),
+            weight_ref[head],
+            jnp.concatenate([v[:, here] for v in v_refs], axis=0),
             preferred_element_type=jnp.float32,
         )
-        out_ref[:, here] = out / total
-        stat_ref[:, here] = jnp.broadcast_to(top + jnp.log2(total), out.shape)
-
-
-def weigh_kernel(blocks, heads, bias_ref, q_ref, *refs):
-    k_refs = refs[: 2 * blocks]
-    before_ref, stat_ref = refs[2 * blocks : 2 * blocks + 2]
-    weight_refs, base_ref = refs[2 * blocks + 2 : -1], refs[-1]
-    keys_each = 2 * k_refs[0].shape[0]
-    for head in range(heads):
-        here = slice(head * HD, (head + 1) * HD)
-        keys = [
-            jnp.concatenate([k_refs[2 * n][:, here], k_refs[2 * n + 1][:, here]], axis=0)
-            for n in range(blocks)
-        ]
-        biases = [bias_ref[n] for n in range(blocks)]
-        scores = jnp.concatenate(scores_of(q_ref[:, here], keys, biases), axis=1)
-        before = stat_ref[:, here][:, :1]
-        top = jnp.maximum(before, jnp.max(scores, axis=1, keepdims=True))
-        weights = jnp.exp2(scores - top)
-        factor = jnp.exp2(before - top)
-        inverse = 1.0 / (factor + jnp.sum(weights, axis=1, keepdims=True))
-        weights = (weights * inverse).astype(jnp.bfloat16)
-        for n in range(blocks):
-            weight_refs[n][:, head * keys_each : (head + 1) * keys_each] = weights[
-                :, n * keys_each : (n + 1) * keys_each
-            ]
-        base_ref[:, here] = before_ref[:, here] * (factor * inverse)
+        out = out * inverse
+        if merging:
+            out = out + before_ref[:, here] * factor
+        out_ref[:, here] = out
+
+    steps = [score, weigh, mix] if finishing else [score, weigh]
+    for time in range(heads + len(steps) - 1):
+        for number, step in enumerate(steps):
+            head = time - number
+            if 0 <= head < heads:
+                step(head, slice(head * HD, (head + 1) * HD))
 
 
 def last_kernel(blocks, heads, base_ref, *refs):
@@ -126,7 +148,7 @@
     return max(n for n in range(1, HEADS_AT_ONCE + 1) if heads % n == 0)
 
 
-def chunked(kernel, scalars, operands, out_types, blocks, dots):
+def chunked(kernel, scalars, operands, out_types, blocks, dots, scratch=()):
     tokens, width = operands[0].shape
     heads = heads_at_once(width // HD)
     steps = width // (heads * HD)
@@ -134,13 +156,15 @@
     def spec(shape):
         return pl.BlockSpec((shape[0], shape[1] // steps), lambda i: (0, i))
 
-    return pl.pallas_call(
+    keys = 2 * tokens * blocks
+    call = pl.pallas_call(
         functools.partial(kernel, blocks, heads),
         grid=(steps,),
         in_specs=[pl.BlockSpec(memory_space=pltpu.SMEM)] * len(scalars)
         + [spec(a.shape) for a in operands],
         out_specs=[spec(t.shape) for t in out_types],
         out_shape=out_types,
+        scratch_shapes=[pltpu.VMEM((heads, tokens, keys), t) for t in scratch],
         cost_estimate=pl.CostEstimate(
             flops=dots * 2 * tokens * 2 * tokens * width * blocks,
             transcendentals=tokens * 2 * tokens * (width // HD) * blocks,
@@ -148,7 +172,8 @@
             + sum(t.size * t.dtype.itemsize for t in out_types),
         ),
         compiler_params=pltpu.CompilerParams(vmem_limit_bytes=VMEM_BYTES),
-    )(*scalars, *operands)
+    )
+    return list(call(*scalars, *operands))
 
 
 def after(value, *others):
@@ -185,25 +210,38 @@
     v_early = [moved(values, p) for p in early]
     k_swap, v_swap = swapped(keys), swapped(values)
     k_again = after(keys, *k_early)
-    v_again = after(values, *k_early)
+    v_again = after(values, *v_early)
     k_late = [moved(k_again, p) for p in late]
     v_late = [moved(v_again, p) for p in late]
 
-    blocks = [keys, k_swap, values, v_swap]
+    full = jax.ShapeDtypeStruct((tokens, width), jnp.float32)
+
+    def attend(merged, operands, blocks):
+        def kernel(blocks, heads, *refs):
+            merge_kernel(blocks, heads, merged is not None, True, *refs)
+
+        scalars = [] if merged is None else [merged]
+        scratch = (jnp.float32, jnp.bfloat16)
+        return chunked(kernel, scalars, operands, [full] * 2, blocks, 2, scratch)
+
+    def weigh(merged, operands, blocks):
+        def kernel(blocks, heads, *refs):
+            merge_kernel(blocks, heads, True, False, *refs)
+
+        weight = jax.ShapeDtypeStruct((tokens, width // HD * 2 * tokens), jnp.bfloat16)
+        outs = [weight] * blocks + [full]
+        return chunked(kernel, [merged], operands, outs, blocks, 1, (jnp.float32,))
+
+    carried = attend(None, [queries, keys, k_swap, values, v_swap], 1)
+    k_both, v_both = [], []
     for k, v, p in zip(k_early, v_early, early):
-        blocks += [k, swapped(k, p), v, swapped(v, p)]
-    full = jax.ShapeDtypeStruct((tokens, width), jnp.float32)
-    before, stats = chunked(
-        first_kernel, [biases(early)], [queries] + blocks, [full] * 2, 1 + len(early), 2
-    )
+        k_both += [k, swapped(k, p)]
+        v_both += [v, swapped(v, p)]
+    carried = attend(biases(early), [queries] + k_both + v_both + carried, len(early))
     k_both = []
     for k, p in zip(k_late, late):
         k_both += [k, swapped(k, p)]
-    weight = jax.ShapeDtypeStruct((tokens, width // HD * 2 * tokens), jnp.bfloat16)
-    *weights, base = chunked(
-        weigh_kernel, [biases(late)], [queries] + k_both + [before, stats],
-        [weight] * len(late) + [full], len(late), 1,
-    )
+    *weights, base = weigh(biases(late), [queries] + k_both + carried, len(late))
     v_both = []
     for v, p in zip(v_late, late):
         v_both += [v, swapped(v, p)]

time: 111 us -> 104 us (0.937)
  the two profiles are of different devices: /device:TPU:5 before, /device:TPU:9 now
where the time goes in v3:
time: 104 us; the launch traced here: 103 us
  starting transfers between devices  42.3 us (41%)
  waiting for transfers between devices  33.3 us (32%)
  Pallas kernels  18 us (17%)
  local copies, waits for them, and re-layouts  8.68 us (8%)
    ppermute x8, waiting for transfers between devices, moved(): lax.ppermute(value, 'row', [(s, t) for s, (t, _) in sorted(phase.items())])  33.3 us
    ppermute x10, starting transfers between devices, swapped(): return lax.ppermute(value, ('row', 'col'), pairs)  22.7 us
    ppermute x8, starting transfers between devices, moved(): lax.ppermute(value, 'row', [(s, t) for s, (t, _) in sorted(phase.items())])  19.6 us
    pallas_call x4, Pallas kernels, chunked(): return list(call(*scalars, *operands))  18 us
    unnamed x20, local copies, waits for them, and re-layouts  7.94 us
  transfers between devices with their start and end apart: 18, of which 6 were waited for; matrix products, arithmetic and copies ran while one was open for 1% of the time, Pallas kernels for 13%

profile of v3, /device:TPU:9, one launch (start us, length us, event | category | flops | bytes accessed | tf_op | source)
XLA Modules:
  0.0 102.9 jit_solution(7977890770756752737)
XLA Ops:
  0.0 3.3 %collective-permute-start.10 = (bf16[128,2560]{1,0:T(8,128)(2,1)}, bf16[128,2560]{1,0:T(8,128)(2,1)S(1)}, u32[]{:S(2)}, u32[]{:S(2)}) collective-permute-start(bf16[128,2560]{1,0:T(8,128)(2,1)} %refs_3_.1), channel_id=1, source_target_pairs={{0,2},{2,0},{4,6},{6,4},{10,12},{12,10},{1,3},{3,1},{5,7},{7,5},{1... | collective-permute-start | bytes 1966088 | tf_op jit(solution)/shard_map/ppermute | solution.py:190
  4.0 2.1 %collective-permute-start.1 = (bf16[128,2560]{1,0:T(8,128)(2,1)}, bf16[128,2560]{1,0:T(8,128)(2,1)S(1)}, u32[]{:S(2)}, u32[]{:S(2)}) collective-permute-start(bf16[128,2560]{1,0:T(8,128)(2,1)} %refs_1_.3), channel_id=1, source_target_pairs={{0,2},{2,0},{4,6},{6,4},{10,12},{12,10},{1,3},{3,1},{5,7},{7,5},{1... | collective-permute-start | bytes 1966088 | tf_op jit(solution)/shard_map/ppermute | solution.py:190
  6.8 1.3 %collective-permute-start.12 = (bf16[128,2560]{1,0:T(8,128)(2,1)}, bf16[128,2560]{1,0:T(8,128)(2,1)S(1)}, u32[]{:S(2)}, u32[]{:S(2)}) collective-permute-start(bf16[128,2560]{1,0:T(8,128)(2,1)} %refs_1_.3), channel_id=1, source_target_pairs={{0,1},{1,0},{2,3},{3,2},{4,5},{5,4},{6,7},{7,6},{8,9},{9,8},{10,11... | collective-permute-start | bytes 1966088 | tf_op jit(solution)/shard_map/ppermute | solution.py:195
  8.1 9.7 %collective-permute-done.10.refs_8_ = bf16[128,2560]{1,0:T(8,128)(2,1)S(1)} collective-permute-done((bf16[128,2560]{1,0:T(8,128)(2,1)}, bf16[128,2560]{1,0:T(8,128)(2,1)S(1)}, u32[]{:S(2)}, u32[]{:S(2)}) %collective-permute-start.10) | collective-permute-done | bytes 655392 | tf_op jit(solution)/shard_map/ppermute | solution.py:190
  17.8 2.7 %collective-permute-start.13 = (bf16[128,2560]{1,0:T(8,128)(2,1)}, bf16[128,2560]{1,0:T(8,128)(2,1)S(1)}, u32[]{:S(2)}, u32[]{:S(2)}) collective-permute-start(bf16[128,2560]{1,0:T(8,128)(2,1)} %refs_3_.1), channel_id=1, source_target_pairs={{0,1},{1,0},{2,3},{3,2},{4,5},{5,4},{6,7},{7,6},{8,9},{9,8},{10,11... | collective-permute-start | bytes 1966088 | tf_op jit(solution)/shard_map/ppermute | solution.py:195
  20.5 1.9 %collective-permute-start.11 = (bf16[128,2560]{1,0:T(8,128)(2,1)S(1)}, bf16[128,2560]{1,0:T(8,128)(2,1)S(1)}, u32[]{:S(2)}, u32[]{:S(2)}) collective-permute-start(bf16[128,2560]{1,0:T(8,128)(2,1)S(1)} %collective-permute-done.10.refs_8_), channel_id=1, source_target_pairs={{0,1},{1,0},{2,3},{3,2},{4,5},{5,4},{6,7},{7,6},{10,11},{11,10},{1... | collective-permute-start | bytes 1966088 | tf_op jit(solution)/shard_map/ppermute | solution.py:195
  22.4 9.5 %collective-permute-done.1.refs_4_ = bf16[128,2560]{1,0:T(8,128)(2,1)S(1)} collective-permute-done((bf16[128,2560]{1,0:T(8,128)(2,1)}, bf16[128,2560]{1,0:T(8,128)(2,1)S(1)}, u32[]{:S(2)}, u32[]{:S(2)}) %collective-permute-start.1) | collective-permute-done | bytes 655392 | tf_op jit(solution)/shard_map/ppermute | solution.py:190
  32.6 3.4 %collective-permute-start.7 = (bf16[128,2560]{1,0:T(8,128)(2,1)S(1)}, bf16[128,2560]{1,0:T(8,128)(2,1)}, u32[]{:S(2)}, u32[]{:S(2)}) collective-permute-start(bf16[128,2560]{1,0:T(8,128)(2,1)S(1)} %collective-permute-done.1.refs_4_), channel_id=1, source_target_pairs={{0,1},{1,0},{2,3},{3,2},{4,5},{5,4},{6,7},{7,6},{10,11},{11,10},{1... | collective-permute-start | bytes 1966088 | tf_op jit(solution)/shard_map/ppermute | solution.py:195
  36.9 5.1 %collective-permute-start.2 = (bf16[128,2560]{1,0:T(8,128)(2,1)}, bf16[128,2560]{1,0:T(8,128)(2,1)}, u32[]{:S(2)}, u32[]{:S(2)}) collective-permute-start(bf16[128,2560]{1,0:T(8,128)(2,1)} %refs_1_.3), channel_id=1, source_target_pairs={{4,12},{6,14},{12,4},{14,6},{5,13},{7,15},{13,5},{15,7},{20,28},{2... | collective-permute-start | bytes 1966088 | tf_op jit(solution)/shard_map/ppermute | solution.py:190
  42.9 2.7 %collective-permute-start.4 = (bf16[128,2560]{1,0:T(8,128)(2,1)}, bf16[128,2560]{1,0:T(8,128)(2,1)}, u32[]{:S(2)}, u32[]{:S(2)}) collective-permute-start(bf16[128,2560]{1,0:T(8,128)(2,1)} %refs_1_.3), channel_id=1, source_target_pairs={{2,4},{4,2},{8,10},{10,8},{12,14},{14,12},{3,5},{5,3},{9,11},{11,9... | collective-permute-start | bytes 1966088 | tf_op jit(solution)/shard_map/ppermute | solution.py:190
  45.6 1.9 %collective-permute-start.14 = (bf16[128,2560]{1,0:T(8,128)(2,1)}, bf16[128,2560]{1,0:T(8,128)(2,1)}, u32[]{:S(2)}, u32[]{:S(2)}) collective-permute-start(bf16[128,2560]{1,0:T(8,128)(2,1)} %refs_3_.1), channel_id=1, source_target_pairs={{4,12},{6,14},{12,4},{14,6},{5,13},{7,15},{13,5},{15,7},{20,28},{2... | collective-permute-start | bytes 1966088 | tf_op jit(solution)/shard_map/ppermute | solution.py:190
  48.4 3.0 %collective-permute-start.16 = (bf16[128,2560]{1,0:T(8,128)(2,1)}, bf16[128,2560]{1,0:T(8,128)(2,1)}, u32[]{:S(2)}, u32[]{:S(2)}) collective-permute-start(bf16[128,2560]{1,0:T(8,128)(2,1)} %refs_3_.1), channel_id=1, source_target_pairs={{2,4},{4,2},{8,10},{10,8},{12,14},{14,12},{3,5},{5,3},{9,11},{11,9... | collective-permute-start | bytes 1966088 | tf_op jit(solution)/shard_map/ppermute | solution.py:190
  52.9 4.5 %collective-permute-done.2.refs_2_ = bf16[128,2560]{1,0:T(8,128)(2,1)} collective-permute-done((bf16[128,2560]{1,0:T(8,128)(2,1)}, bf16[128,2560]{1,0:T(8,128)(2,1)}, u32[]{:S(2)}, u32[]{:S(2)}) %collective-permute-start.2) | collective-permute-done | bytes 655392 | tf_op jit(solution)/shard_map/ppermute | solution.py:190
  57.4 2.7 %collective-permute-start.3 = (bf16[128,2560]{1,0:T(8,128)(2,1)}, bf16[128,2560]{1,0:T(8,128)(2,1)S(1)}, u32[]{:S(2)}, u32[]{:S(2)}) collective-permute-start(bf16[128,2560]{1,0:T(8,128)(2,1)} %collective-permute-done.2.refs_2_), channel_id=1, source_target_pairs={{4,5},{5,4},{6,7},{7,6},{12,13},{13,12},{14,15},{15,14},{20,21},{2... | collective-permute-start | bytes 1966088 | tf_op jit(solution)/shard_map/ppermute | solution.py:195
  60.1 1.9 %collective-permute-done.4.refs_4_ = bf16[128,2560]{1,0:T(8,128)(2,1)} collective-permute-done((bf16[128,2560]{1,0:T(8,128)(2,1)}, bf16[128,2560]{1,0:T(8,128)(2,1)}, u32[]{:S(2)}, u32[]{:S(2)}) %collective-permute-start.4) | collective-permute-done | bytes 655392 | tf_op jit(solution)/shard_map/ppermute | solution.py:190
  62.0 3.8 %collective-permute-start.5 = (bf16[128,2560]{1,0:T(8,128)(2,1)}, bf16[128,2560]{1,0:T(8,128)(2,1)S(1)}, u32[]{:S(2)}, u32[]{:S(2)}) collective-permute-start(bf16[128,2560]{1,0:T(8,128)(2,1)} %collective-permute-done.4.refs_4_), channel_id=1, source_target_pairs={{2,3},{3,2},{4,5},{5,4},{8,9},{9,8},{10,11},{11,10},{12,13},{13,12... | collective-permute-start | bytes 1966088 | tf_op jit(solution)/shard_map/ppermute | solution.py:195
  65.8 5.7 %collective-permute-done.14.refs_2_ = bf16[128,2560]{1,0:T(8,128)(2,1)} collective-permute-done((bf16[128,2560]{1,0:T(8,128)(2,1)}, bf16[128,2560]{1,0:T(8,128)(2,1)}, u32[]{:S(2)}, u32[]{:S(2)}) %collective-permute-start.14) | collective-permute-done | bytes 655392 | tf_op jit(solution)/shard_map/ppermute | solution.py:190
  71.5 2.5 %collective-permute-start.15 = (bf16[128,2560]{1,0:T(8,128)(2,1)}, bf16[128,2560]{1,0:T(8,128)(2,1)S(1)}, u32[]{:S(2)}, u32[]{:S(2)}) collective-permute-start(bf16[128,2560]{1,0:T(8,128)(2,1)} %collective-permute-done.14.refs_2_), channel_id=1, source_target_pairs={{4,5},{5,4},{6,7},{7,6},{12,13},{13,12},{14,15},{15,14},{20,21},{2... | collective-permute-start | bytes 1966088 | tf_op jit(solution)/shard_map/ppermute | solution.py:195
  74.0 2.1 %collective-permute-done.16.refs_4_ = bf16[128,2560]{1,0:T(8,128)(2,1)} collective-permute-done((bf16[128,2560]{1,0:T(8,128)(2,1)}, bf16[128,2560]{1,0:T(8,128)(2,1)}, u32[]{:S(2)}, u32[]{:S(2)}) %collective-permute-start.16) | collective-permute-done | bytes 655392 | tf_op jit(solution)/shard_map/ppermute | solution.py:190
  76.0 3.0 %collective-permute-start.17 = (bf16[128,2560]{1,0:T(8,128)(2,1)}, bf16[128,2560]{1,0:T(8,128)(2,1)S(1)}, u32[]{:S(2)}, u32[]{:S(2)}) collective-permute-start(bf16[128,2560]{1,0:T(8,128)(2,1)} %collective-permute-done.16.refs_4_), channel_id=1, source_target_pairs={{2,3},{3,2},{4,5},{5,4},{8,9},{9,8},{10,11},{11,10},{12,13},{13,12... | collective-permute-start | bytes 1966088 | tf_op jit(solution)/shard_map/ppermute | solution.py:195
  84.7 3.0 %shard_map.64 = (f32[128,2560]{1,0:T(8,128)S(1)}, f32[128,2560]{1,0:T(8,128)S(1)}) custom-call(bf16[128,2560]{1,0:T(8,128)(2,1)S(1)} %copy-done.1, bf16[128,2560]{1,0:T(8,128)(2,1)S(1)} %copy-done.4, bf16[128,2560]{1,0:T(8,128)(2,1)S(1)} %copy-done.7, bf16[128,2560]{1,0:T(8,128)(2,1)S(1)} %copy-done.5, bf16[128,2560]{1,0:T(8,128)(2,1)S(1)} %copy-done.9), custom_call_target="tpu_custom_call" | custom-call | flops 335544320 | bytes 5898240 | tf_op jit(solution)/shard_map/pallas_call | solution.py:176
  87.7 5.4 %shard_map.65 = (f32[128,2560]{1,0:T(8,128)S(1)}, f32[128,2560]{1,0:T(8,128)S(1)}) custom-call(f32[2]{0:T(128)S(1)} %compare_select_fusion.refs_0_, bf16[128,2560]{1,0:T(8,128)(2,1)S(1)} %copy-done.1, bf16[128,2560]{1,0:T(8,128)(2,1)S(1)} %collective-permute-done.refs_2_, bf16[128,2560]{1,0:T(8,128)(2,1)S(1)} %copy-done.3, ...), custom_call_target="tpu_custom_call" | custom-call | flops 671088640 | bytes 11141120 | tf_op jit(solution)/shard_map/pallas_call | solution.py:176
  93.2 5.0 %shard_map.66 = (bf16[128,5120]{1,0:T(8,128)(2,1)S(1)}, bf16[128,5120]{1,0:T(8,128)(2,1)S(1)}, f32[128,2560]{1,0:T(8,128)S(1)}) custom-call(f32[2]{0:T(128)S(1)} %compare_select_fusion.2.refs_0_, bf16[128,2560]{1,0:T(8,128)(2,1)S(1)} %copy-done.1, bf16[128,2560]{1,0:T(8,128)(2,1)} %collective-permute-done.2.refs_2_, ...), custom_call_target="tpu_custom_call" | custom-call | flops 335544320 | bytes 9830400 | tf_op jit(solution)/shard_map/pallas_call | solution.py:176
  98.2 4.7 %shard_map.67 = bf16[128,2560]{1,0:T(8,128)(2,1)} custom-call(f32[128,2560]{1,0:T(8,128)S(1)} %get-tuple-element.19.base_ref, bf16[128,5120]{1,0:T(8,128)(2,1)S(1)} %get-tuple-element.20.refs_0_, bf16[128,5120]{1,0:T(8,128)(2,1)S(1)} %get-tuple-element.21.refs_1_, bf16[128,2560]{1,0:T(8,128)(2,1)} %collective-permute-done.14.refs_2_, ...), custom_call_target="tpu_custom_call" | custom-call | flops 335544320 | bytes 7208960 | tf_op jit(solution)/shard_map/pallas_call | solution.py:176
  (41 shorter events, 11.7 us)
Async XLA Ops:
  0.0 52.8 %copy-start = (s32[8,5]{1,0:T(8,128)S(1)}, s32[8,5]{1,0:T(8,128)}, u32[]{:S(2)}) copy-start(s32[8,5]{1,0:T(8,128)} %param.9) | copy-start | bytes 484
  0.0 17.8 %collective-permute-start.10 = (bf16[128,2560]{1,0:T(8,128)(2,1)}, bf16[128,2560]{1,0:T(8,128)(2,1)S(1)}, u32[]{:S(2)}, u32[]{:S(2)}) collective-permute-start(bf16[128,2560]{1,0:T(8,128)(2,1)} %refs_3_.1), channel_id=1, source_target_pairs={{0,2},{2,0},{4,6},{6,4},{10,12},{12,10},{1,3},{3,1},{5,7},{7,5},{1... | collective-permute-start | bytes 1966088 | tf_op jit(solution)/shard_map/ppermute | solution.py:190
  3.3 17.2 %collective-permute-start = (bf16[128,2560]{1,0:T(8,128)(2,1)}, bf16[128,2560]{1,0:T(8,128)(2,1)S(1)}, u32[]{:S(2)}, u32[]{:S(2)}) collective-permute-start(bf16[128,2560]{1,0:T(8,128)(2,1)} %refs_1_.3), channel_id=1, source_target_pairs={{0,8},{2,10},{8,0},{10,2},{1,9},{3,11},{9,1},{11,3},{16,24},{18,26... | collective-permute-start | bytes 1966088 | tf_op jit(solution)/shard_map/ppermute | solution.py:190
  4.0 27.9 %collective-permute-start.1 = (bf16[128,2560]{1,0:T(8,128)(2,1)}, bf16[128,2560]{1,0:T(8,128)(2,1)S(1)}, u32[]{:S(2)}, u32[]{:S(2)}) collective-permute-start(bf16[128,2560]{1,0:T(8,128)(2,1)} %refs_1_.3), channel_id=1, source_target_pairs={{0,2},{2,0},{4,6},{6,4},{10,12},{12,10},{1,3},{3,1},{5,7},{7,5},{1... | collective-permute-start | bytes 1966088 | tf_op jit(solution)/shard_map/ppermute | solution.py:190
  6.1 26.5 %collective-permute-start.8 = (bf16[128,2560]{1,0:T(8,128)(2,1)}, bf16[128,2560]{1,0:T(8,128)(2,1)S(1)}, u32[]{:S(2)}, u32[]{:S(2)}) collective-permute-start(bf16[128,2560]{1,0:T(8,128)(2,1)} %refs_3_.1), channel_id=1, source_target_pairs={{0,8},{2,10},{8,0},{10,2},{1,9},{3,11},{9,1},{11,3},{16,24},{18,26... | collective-permute-start | bytes 1966088 | tf_op jit(solution)/shard_map/ppermute | solution.py:190
  6.8 29.2 %collective-permute-start.12 = (bf16[128,2560]{1,0:T(8,128)(2,1)}, bf16[128,2560]{1,0:T(8,128)(2,1)S(1)}, u32[]{:S(2)}, u32[]{:S(2)}) collective-permute-start(bf16[128,2560]{1,0:T(8,128)(2,1)} %refs_1_.3), channel_id=1, source_target_pairs={{0,1},{1,0},{2,3},{3,2},{4,5},{5,4},{6,7},{7,6},{8,9},{9,8},{10,11... | collective-permute-start | bytes 1966088 | tf_op jit(solution)/shard_map/ppermute | solution.py:195
  17.8 24.2 %collective-permute-start.13 = (bf16[128,2560]{1,0:T(8,128)(2,1)}, bf16[128,2560]{1,0:T(8,128)(2,1)S(1)}, u32[]{:S(2)}, u32[]{:S(2)}) collective-permute-start(bf16[128,2560]{1,0:T(8,128)(2,1)} %refs_3_.1), channel_id=1, source_target_pairs={{0,1},{1,0},{2,3},{3,2},{4,5},{5,4},{6,7},{7,6},{8,9},{9,8},{10,11... | collective-permute-start | bytes 1966088 | tf_op jit(solution)/shard_map/ppermute | solution.py:195
  20.5 25.1 %collective-permute-start.11 = (bf16[128,2560]{1,0:T(8,128)(2,1)S(1)}, bf16[128,2560]{1,0:T(8,128)(2,1)S(1)}, u32[]{:S(2)}, u32[]{:S(2)}) collective-permute-start(bf16[128,2560]{1,0:T(8,128)(2,1)S(1)} %collective-permute-done.10.refs_8_), channel_id=1, source_target_pairs={{0,1},{1,0},{2,3},{3,2},{4,5},{5,4},{6,7},{7,6},{10,11},{11,10},{1... | collective-permute-start | bytes 1966088 | tf_op jit(solution)/shard_map/ppermute | solution.py:195
  31.9 15.7 %collective-permute-start.6 = (bf16[128,2560]{1,0:T(8,128)(2,1)S(1)}, bf16[128,2560]{1,0:T(8,128)(2,1)S(1)}, u32[]{:S(2)}, u32[]{:S(2)}) collective-permute-start(bf16[128,2560]{1,0:T(8,128)(2,1)S(1)} %collective-permute-done.refs_2_), channel_id=1, source_target_pairs={{0,1},{1,0},{2,3},{3,2},{8,9},{9,8},{10,11},{11,10},{16,17},{17,16... | collective-permute-start | bytes 1966088 | tf_op jit(solution)/shard_map/ppermute | solution.py:195
  32.6 19.5 %collective-permute-start.7 = (bf16[128,2560]{1,0:T(8,128)(2,1)S(1)}, bf16[128,2560]{1,0:T(8,128)(2,1)}, u32[]{:S(2)}, u32[]{:S(2)}) collective-permute-start(bf16[128,2560]{1,0:T(8,128)(2,1)S(1)} %collective-permute-done.1.refs_4_), channel_id=1, source_target_pairs={{0,1},{1,0},{2,3},{3,2},{4,5},{5,4},{6,7},{7,6},{10,11},{11,10},{1... | collective-permute-start | bytes 1966088 | tf_op jit(solution)/shard_map/ppermute | solution.py:195
  36.9 20.5 %collective-permute-start.2 = (bf16[128,2560]{1,0:T(8,128)(2,1)}, bf16[128,2560]{1,0:T(8,128)(2,1)}, u32[]{:S(2)}, u32[]{:S(2)}) collective-permute-start(bf16[128,2560]{1,0:T(8,128)(2,1)} %refs_1_.3), channel_id=1, source_target_pairs={{4,12},{6,14},{12,4},{14,6},{5,13},{7,15},{13,5},{15,7},{20,28},{2... | collective-permute-start | bytes 1966088 | tf_op jit(solution)/shard_map/ppermute | solution.py:190
  42.9 19.1 %collective-permute-start.4 = (bf16[128,2560]{1,0:T(8,128)(2,1)}, bf16[128,2560]{1,0:T(8,128)(2,1)}, u32[]{:S(2)}, u32[]{:S(2)}) collective-permute-start(bf16[128,2560]{1,0:T(8,128)(2,1)} %refs_1_.3), channel_id=1, source_target_pairs={{2,4},{4,2},{8,10},{10,8},{12,14},{14,12},{3,5},{5,3},{9,11},{11,9... | collective-permute-start | bytes 1966088 | tf_op jit(solution)/shard_map/ppermute | solution.py:190
  45.6 25.8 %collective-permute-start.14 = (bf16[128,2560]{1,0:T(8,128)(2,1)}, bf16[128,2560]{1,0:T(8,128)(2,1)}, u32[]{:S(2)}, u32[]{:S(2)}) collective-permute-start(bf16[128,2560]{1,0:T(8,128)(2,1)} %refs_3_.1), channel_id=1, source_target_pairs={{4,12},{6,14},{12,4},{14,6},{5,13},{7,15},{13,5},{15,7},{20,28},{2... | collective-permute-start | bytes 1966088 | tf_op jit(solution)/shard_map/ppermute | solution.py:190
  48.4 27.6 %collective-permute-start.16 = (bf16[128,2560]{1,0:T(8,128)(2,1)}, bf16[128,2560]{1,0:T(8,128)(2,1)}, u32[]{:S(2)}, u32[]{:S(2)}) collective-permute-start(bf16[128,2560]{1,0:T(8,128)(2,1)} %refs_3_.1), channel_id=1, source_target_pairs={{2,4},{4,2},{8,10},{10,8},{12,14},{14,12},{3,5},{5,3},{9,11},{11,9... | collective-permute-start | bytes 1966088 | tf_op jit(solution)/shard_map/ppermute | solution.py:190
  52.1 35.6 %collective-permute-start.9 = (bf16[128,2560]{1,0:T(8,128)(2,1)S(1)}, bf16[128,2560]{1,0:T(8,128)(2,1)S(1)}, u32[]{:S(2)}, u32[]{:S(2)}) collective-permute-start(bf16[128,2560]{1,0:T(8,128)(2,1)S(1)} %collective-permute-done.8.refs_6_), channel_id=1, source_target_pairs={{0,1},{1,0},{2,3},{3,2},{8,9},{9,8},{10,11},{11,10},{16,17},{17,16... | collective-permute-start | bytes 1966088 | tf_op jit(solution)/shard_map/ppermute | solution.py:195
  57.4 35.7 %collective-permute-start.3 = (bf16[128,2560]{1,0:T(8,128)(2,1)}, bf16[128,2560]{1,0:T(8,128)(2,1)S(1)}, u32[]{:S(2)}, u32[]{:S(2)}) collective-permute-start(bf16[128,2560]{1,0:T(8,128)(2,1)} %collective-permute-done.2.refs_2_), channel_id=1, source_target_pairs={{4,5},{5,4},{6,7},{7,6},{12,13},{13,12},{14,15},{15,14},{20,21},{2... | collective-permute-start | bytes 1966088 | tf_op jit(solution)/shard_map/ppermute | solution.py:195
  62.0 31.2 %collective-permute-start.5 = (bf16[128,2560]{1,0:T(8,128)(2,1)}, bf16[128,2560]{1,0:T(8,128)(2,1)S(1)}, u32[]{:S(2)}, u32[]{:S(2)}) collective-permute-start(bf16[128,2560]{1,0:T(8,128)(2,1)} %collective-permute-done.4.refs_4_), channel_id=1, source_target_pairs={{2,3},{3,2},{4,5},{5,4},{8,9},{9,8},{10,11},{11,10},{12,13},{13,12... | collective-permute-start | bytes 1966088 | tf_op jit(solution)/shard_map/ppermute | solution.py:195
  71.5 26.7 %collective-permute-start.15 = (bf16[128,2560]{1,0:T(8,128)(2,1)}, bf16[128,2560]{1,0:T(8,128)(2,1)S(1)}, u32[]{:S(2)}, u32[]{:S(2)}) collective-permute-start(bf16[128,2560]{1,0:T(8,128)(2,1)} %collective-permute-done.14.refs_2_), channel_id=1, source_target_pairs={{4,5},{5,4},{6,7},{7,6},{12,13},{13,12},{14,15},{15,14},{20,21},{2... | collective-permute-start | bytes 1966088 | tf_op jit(solution)/shard_map/ppermute | solution.py:195
  76.0 22.2 %collective-permute-start.17 = (bf16[128,2560]{1,0:T(8,128)(2,1)}, bf16[128,2560]{1,0:T(8,128)(2,1)S(1)}, u32[]{:S(2)}, u32[]{:S(2)}) collective-permute-start(bf16[128,2560]{1,0:T(8,128)(2,1)} %collective-permute-done.16.refs_4_), channel_id=1, source_target_pairs={{2,3},{3,2},{4,5},{5,4},{8,9},{9,8},{10,11},{11,10},{12,13},{13,12... | collective-permute-start | bytes 1966088 | tf_op jit(solution)/shard_map/ppermute | solution.py:195
  79.3 1.1 %copy-start.1 = (bf16[128,2560]{1,0:T(8,128)(2,1)S(1)}, bf16[128,2560]{1,0:T(8,128)(2,1)}, u32[]{:S(2)}) copy-start(bf16[128,2560]{1,0:T(8,128)(2,1)} %refs_1_.5) | copy-start | bytes 1966084
  80.4 1.1 %copy-start.4 = (bf16[128,2560]{1,0:T(8,128)(2,1)S(1)}, bf16[128,2560]{1,0:T(8,128)(2,1)}, u32[]{:S(2)}) copy-start(bf16[128,2560]{1,0:T(8,128)(2,1)} %refs_1_.3) | copy-start | bytes 1966084
  81.5 1.1 %copy-start.5 = (bf16[128,2560]{1,0:T(8,128)(2,1)S(1)}, bf16[128,2560]{1,0:T(8,128)(2,1)}, u32[]{:S(2)}) copy-start(bf16[128,2560]{1,0:T(8,128)(2,1)} %refs_3_.1) | copy-start | bytes 1966084
  83.7 1.1 %copy-start.9 = (bf16[128,2560]{1,0:T(8,128)(2,1)S(1)}, bf16[128,2560]{1,0:T(8,128)(2,1)}, u32[]{:S(2)}) copy-start(bf16[128,2560]{1,0:T(8,128)(2,1)} %copy-done.8) | copy-start | bytes 1966084
  84.7 3.0 %copy-start.3 = (bf16[128,2560]{1,0:T(8,128)(2,1)S(1)}, bf16[128,2560]{1,0:T(8,128)(2,1)}, u32[]{:S(2)}) copy-start(bf16[128,2560]{1,0:T(8,128)(2,1)} %copy-done.2) | copy-start | bytes 1966084
  (4 other events, 3.6 us)

commit v4 on v3

--- a/solution.py
+++ b/solution.py
@@ -71,7 +71,7 @@
     if finishing:
         out_ref, total_ref, score_ref, weight_ref = refs
     else:
-        weight_refs, base_ref, score_ref = refs[:blocks], refs[blocks], refs[blocks + 1]
+        weight_refs, (base_ref, total_ref, score_ref) = refs[:blocks], refs[blocks:]
     keys_each = 2 * k_refs[0].shape[0]
     kept = {}
 
@@ -98,8 +98,8 @@
             factor = jnp.exp2(before - top)
             total = total + factor
         inverse = 1.0 / total
+        total_ref[:, here] = top + jnp.log2(total)
         if finishing:
-            total_ref[:, here] = top + jnp.log2(total)
             kept[head] = (inverse, factor * inverse if merging else None)
             for at, w in enumerate(weights):
                 weight_ref[head, :, at * HD : (at + 1) * HD] = w.astype(jnp.bfloat16)
@@ -148,7 +148,7 @@
     return max(n for n in range(1, HEADS_AT_ONCE + 1) if heads % n == 0)
 
 
-def chunked(kernel, scalars, operands, out_types, blocks, dots, scratch=()):
+def chunked(kernel, scalars, operands, out_types, blocks, dots, scratch=(), vmem=None):
     tokens, width = operands[0].shape
     heads = heads_at_once(width // HD)
     steps = width // (heads * HD)
@@ -171,7 +171,7 @@
             bytes_accessed=sum(a.size * a.dtype.itemsize for a in operands)
             + sum(t.size * t.dtype.itemsize for t in out_types),
         ),
-        compiler_params=pltpu.CompilerParams(vmem_limit_bytes=VMEM_BYTES),
+        compiler_params=pltpu.CompilerParams(vmem_limit_bytes=vmem),
     )
     return list(call(*scalars, *operands))
 
@@ -208,7 +208,7 @@
     early, late = stages
     k_early = [moved(keys, p) for p in early]
     v_early = [moved(values, p) for p in early]
-    k_swap, v_swap = swapped(keys), swapped(values)
+    k_swap, v_swap = swapped(keys, None), swapped(values, None)
     k_again = after(keys, *k_early)
     v_again = after(values, *v_early)
     k_late = [moved(k_again, p) for p in late]
@@ -224,29 +224,37 @@
         scratch = (jnp.float32, jnp.bfloat16)
         return chunked(kernel, scalars, operands, [full] * 2, blocks, 2, scratch)
 
-    def weigh(merged, operands, blocks):
+    def weigh(merged, operands, blocks, vmem=None):
         def kernel(blocks, heads, *refs):
             merge_kernel(blocks, heads, True, False, *refs)
 
         weight = jax.ShapeDtypeStruct((tokens, width // HD * 2 * tokens), jnp.bfloat16)
-        outs = [weight] * blocks + [full]
-        return chunked(kernel, [merged], operands, outs, blocks, 1, (jnp.float32,))
-
-    carried = attend(None, [queries, keys, k_swap, values, v_swap], 1)
-    k_both, v_both = [], []
-    for k, v, p in zip(k_early, v_early, early):
-        k_both += [k, swapped(k, p)]
-        v_both += [v, swapped(v, p)]
-    carried = attend(biases(early), [queries] + k_both + v_both + carried, len(early))
-    k_both = []
-    for k, p in zip(k_late, late):
-        k_both += [k, swapped(k, p)]
-    *weights, base = weigh(biases(late), [queries] + k_both + carried, len(late))
-    v_both = []
-    for v, p in zip(v_late, late):
-        v_both += [v, swapped(v, p)]
-    out = jax.ShapeDtypeStruct((tokens, width), queries.dtype)
-    return chunked(last_kernel, [], [base] + weights + v_both, [out], len(late), 1)[0]
+        outs = [weight] * blocks + [full] * 2
+        scratch = (jnp.float32,)
+        *weights, base, stats = chunked(kernel, [merged], operands, outs, blocks, 1, scratch, vmem)
+        return weights, base, stats
+
+    def mix(base, weights, values, dtype, vmem=None):
+        out = jax.ShapeDtypeStruct((tokens, width), dtype)
+        return chunked(last_kernel, [], [base] + weights + values, [out], len(weights), 1, (), vmem)[0]
+
+    def both(given, stage):
+        found = []
+        for value, phase in zip(given, stage):
+            found += [value, swapped(value, phase)]
+        return found
+
+    before, stats = attend(None, [queries, keys, k_swap, values, v_swap], 1)
+    k_both = both(k_early, early)
+    weights, base, stats = weigh(biases(early), [queries] + k_both + [before, stats], len(early))
+    v_both = both(v_early, early)
+    before = mix(base, weights, v_both, jnp.float32)
+    k_both = both(k_late, late)
+    weights, base, _ = weigh(
+        biases(late), [queries] + k_both + [before, stats], len(late), VMEM_BYTES
+    )
+    v_both = both(v_late, late)
+    return mix(base, weights, v_both, queries.dtype, VMEM_BYTES)
 
 
 def solution(mesh):

time: 104 us -> 111 us (1.067)
  the two profiles are of different devices: /device:TPU:9 before, /device:TPU:5 now
where the time goes in v4:
time: 111 us; the launch traced here: 110 us
  starting transfers between devices  48.1 us (43%)
  Pallas kernels  31.3 us (28%)
  waiting for transfers between devices  26.7 us (24%)
  local copies, waits for them, and re-layouts  2.92 us (3%)
    pallas_call x5, Pallas kernels, chunked(): return list(call(*scalars, *operands))  31.3 us
    ppermute x10, starting transfers between devices, swapped(): return lax.ppermute(value, ('row', 'col'), pairs)  27.7 us
    ppermute x8, waiting for transfers between devices, moved(): lax.ppermute(value, 'row', [(s, t) for s, (t, _) in sorted(phase.items())])  26.7 us
    ppermute x8, starting transfers between devices, moved(): lax.ppermute(value, 'row', [(s, t) for s, (t, _) in sorted(phase.items())])  20.4 us
  transfers between devices with their start and end apart: 18, of which 5 were waited for; matrix products, arithmetic and copies ran while one was open for 1% of the time, Pallas kernels for 24%

profile of v4, /device:TPU:5, one launch (start us, length us, event | category | flops | bytes accessed | tf_op | source)
XLA Modules:
  0.0 110.1 jit_solution(1822248651650248523)
XLA Ops:
  0.0 4.3 %collective-permute-start = (bf16[128,2560]{1,0:T(8,128)(2,1)}, bf16[128,2560]{1,0:T(8,128)(2,1)S(1)}, u32[]{:S(2)}, u32[]{:S(2)}) collective-permute-start(bf16[128,2560]{1,0:T(8,128)(2,1)} %refs_1_.3), channel_id=1, source_target_pairs={{0,8},{2,10},{8,0},{10,2},{1,9},{3,11},{9,1},{11,3},{16,24},{18,26... | collective-permute-start | bytes 1966088 | tf_op jit(solution)/shard_map/ppermute | solution.py:190
  4.3 2.1 %collective-permute-start.1 = (bf16[128,2560]{1,0:T(8,128)(2,1)}, bf16[128,2560]{1,0:T(8,128)(2,1)S(1)}, u32[]{:S(2)}, u32[]{:S(2)}) collective-permute-start(bf16[128,2560]{1,0:T(8,128)(2,1)} %refs_1_.3), channel_id=1, source_target_pairs={{0,2},{2,0},{4,6},{6,4},{10,12},{12,10},{1,3},{3,1},{5,7},{7,5},{1... | collective-permute-start | bytes 1966088 | tf_op jit(solution)/shard_map/ppermute | solution.py:190
  6.5 1.9 %collective-permute-start.10 = (bf16[128,2560]{1,0:T(8,128)(2,1)}, bf16[128,2560]{1,0:T(8,128)(2,1)}, u32[]{:S(2)}, u32[]{:S(2)}) collective-permute-start(bf16[128,2560]{1,0:T(8,128)(2,1)} %refs_3_.1), channel_id=1, source_target_pairs={{0,8},{2,10},{8,0},{10,2},{1,9},{3,11},{9,1},{11,3},{16,24},{18,26... | collective-permute-start | bytes 1966088 | tf_op jit(solution)/shard_map/ppermute | solution.py:190
  8.4 3.2 %collective-permute-start.12 = (bf16[128,2560]{1,0:T(8,128)(2,1)}, bf16[128,2560]{1,0:T(8,128)(2,1)}, u32[]{:S(2)}, u32[]{:S(2)}) collective-permute-start(bf16[128,2560]{1,0:T(8,128)(2,1)} %refs_3_.1), channel_id=1, source_target_pairs={{0,2},{2,0},{4,6},{6,4},{10,12},{12,10},{1,3},{3,1},{5,7},{7,5},{1... | collective-permute-start | bytes 1966088 | tf_op jit(solution)/shard_map/ppermute | solution.py:190
  11.6 1.6 %collective-permute-start.8 = (bf16[128,2560]{1,0:T(8,128)(2,1)}, bf16[128,2560]{1,0:T(8,128)(2,1)S(1)}, u32[]{:S(2)}, u32[]{:S(2)}) collective-permute-start(bf16[128,2560]{1,0:T(8,128)(2,1)} %refs_1_.3), channel_id=1, source_target_pairs={{0,1},{1,0},{2,3},{3,2},{4,5},{5,4},{6,7},{7,6},{8,9},{9,8},{10,11... | collective-permute-start | bytes 1966088 | tf_op jit(solution)/shard_map/ppermute | solution.py:195
  13.2 5.6 %collective-permute-done.refs_2_ = bf16[128,2560]{1,0:T(8,128)(2,1)S(1)} collective-permute-done((bf16[128,2560]{1,0:T(8,128)(2,1)}, bf16[128,2560]{1,0:T(8,128)(2,1)S(1)}, u32[]{:S(2)}, u32[]{:S(2)}) %collective-permute-start) | collective-permute-done | bytes 655392 | tf_op jit(solution)/shard_map/ppermute | solution.py:190
  18.7 2.7 %collective-permute-start.9 = (bf16[128,2560]{1,0:T(8,128)(2,1)}, bf16[128,2560]{1,0:T(8,128)(2,1)S(1)}, u32[]{:S(2)}, u32[]{:S(2)}) collective-permute-start(bf16[128,2560]{1,0:T(8,128)(2,1)} %refs_3_.1), channel_id=1, source_target_pairs={{0,1},{1,0},{2,3},{3,2},{4,5},{5,4},{6,7},{7,6},{8,9},{9,8},{10,11... | collective-permute-start | bytes 1966088 | tf_op jit(solution)/shard_map/ppermute | solution.py:195
  21.9 5.0 %collective-permute-start.6 = (bf16[128,2560]{1,0:T(8,128)(2,1)S(1)}, bf16[128,2560]{1,0:T(8,128)(2,1)S(1)}, u32[]{:S(2)}, u32[]{:S(2)}) collective-permute-start(bf16[128,2560]{1,0:T(8,128)(2,1)S(1)} %collective-permute-done.refs_2_), channel_id=1, source_target_pairs={{0,1},{1,0},{2,3},{3,2},{8,9},{9,8},{10,11},{11,10},{16,17},{17,16... | collective-permute-start | bytes 1966088 | tf_op jit(solution)/shard_map/ppermute | solution.py:195
  26.9 6.0 %collective-permute-done.10.refs_2_ = bf16[128,2560]{1,0:T(8,128)(2,1)} collective-permute-done((bf16[128,2560]{1,0:T(8,128)(2,1)}, bf16[128,2560]{1,0:T(8,128)(2,1)}, u32[]{:S(2)}, u32[]{:S(2)}) %collective-permute-start.10) | collective-permute-done | bytes 655392 | tf_op jit(solution)/shard_map/ppermute | solution.py:190
  32.9 3.4 %collective-permute-start.7 = (bf16[128,2560]{1,0:T(8,128)(2,1)S(1)}, bf16[128,2560]{1,0:T(8,128)(2,1)S(1)}, u32[]{:S(2)}, u32[]{:S(2)}) collective-permute-start(bf16[128,2560]{1,0:T(8,128)(2,1)S(1)} %collective-permute-done.1.refs_4_), channel_id=1, source_target_pairs={{0,1},{1,0},{2,3},{3,2},{4,5},{5,4},{6,7},{7,6},{10,11},{11,10},{1... | collective-permute-start | bytes 1966088 | tf_op jit(solution)/shard_map/ppermute | solution.py:195
  36.3 3.3 %collective-permute-start.11 = (bf16[128,2560]{1,0:T(8,128)(2,1)}, bf16[128,2560]{1,0:T(8,128)(2,1)}, u32[]{:S(2)}, u32[]{:S(2)}) collective-permute-start(bf16[128,2560]{1,0:T(8,128)(2,1)} %collective-permute-done.10.refs_2_), channel_id=1, source_target_pairs={{0,1},{1,0},{2,3},{3,2},{8,9},{9,8},{10,11},{11,10},{16,17},{17,16... | collective-permute-start | bytes 1966088 | tf_op jit(solution)/shard_map/ppermute | solution.py:195
  40.4 2.1 %collective-permute-start.4 = (bf16[128,2560]{1,0:T(8,128)(2,1)}, bf16[128,2560]{1,0:T(8,128)(2,1)}, u32[]{:S(2)}, u32[]{:S(2)}) collective-permute-start(bf16[128,2560]{1,0:T(8,128)(2,1)} %refs_1_.3), channel_id=1, source_target_pairs={{2,4},{4,2},{8,10},{10,8},{12,14},{14,12},{3,5},{5,3},{9,11},{11,9... | collective-permute-start | bytes 1966088 | tf_op jit(solution)/shard_map/ppermute | solution.py:190
  44.1 5.3 %collective-permute-start.16 = (bf16[128,2560]{1,0:T(8,128)(2,1)}, bf16[128,2560]{1,0:T(8,128)(2,1)}, u32[]{:S(2)}, u32[]{:S(2)}) collective-permute-start(bf16[128,2560]{1,0:T(8,128)(2,1)} %refs_3_.1), channel_id=1, source_target_pairs={{2,4},{4,2},{8,10},{10,8},{12,14},{14,12},{3,5},{5,3},{9,11},{11,9... | collective-permute-start | bytes 1966088 | tf_op jit(solution)/shard_map/ppermute | solution.py:190
  50.2 2.7 %collective-permute-start.13 = (bf16[128,2560]{1,0:T(8,128)(2,1)}, bf16[128,2560]{1,0:T(8,128)(2,1)}, u32[]{:S(2)}, u32[]{:S(2)}) collective-permute-start(bf16[128,2560]{1,0:T(8,128)(2,1)} %collective-permute-done.12.refs_4_), channel_id=1, source_target_pairs={{0,1},{1,0},{2,3},{3,2},{4,5},{5,4},{6,7},{7,6},{10,11},{11,10},{1... | collective-permute-start | bytes 1966088 | tf_op jit(solution)/shard_map/ppermute | solution.py:195
  52.9 1.5 %collective-permute-start.3 = (bf16[128,2560]{1,0:T(8,128)(2,1)S(1)}, bf16[128,2560]{1,0:T(8,128)(2,1)}, u32[]{:S(2)}, u32[]{:S(2)}) collective-permute-start(bf16[128,2560]{1,0:T(8,128)(2,1)S(1)} %collective-permute-done.2.refs_2_), channel_id=1, source_target_pairs={{4,5},{5,4},{6,7},{7,6},{12,13},{13,12},{14,15},{15,14},{20,21},{2... | collective-permute-start | bytes 1966088 | tf_op jit(solution)/shard_map/ppermute | solution.py:195
  54.4 5.4 %collective-permute-done.4.refs_4_ = bf16[128,2560]{1,0:T(8,128)(2,1)} collective-permute-done((bf16[128,2560]{1,0:T(8,128)(2,1)}, bf16[128,2560]{1,0:T(8,128)(2,1)}, u32[]{:S(2)}, u32[]{:S(2)}) %collective-permute-start.4) | collective-permute-done | bytes 655392 | tf_op jit(solution)/shard_map/ppermute | solution.py:190
  59.8 3.2 %collective-permute-start.5 = (bf16[128,2560]{1,0:T(8,128)(2,1)}, bf16[128,2560]{1,0:T(8,128)(2,1)}, u32[]{:S(2)}, u32[]{:S(2)}) collective-permute-start(bf16[128,2560]{1,0:T(8,128)(2,1)} %collective-permute-done.4.refs_4_), channel_id=1, source_target_pairs={{2,3},{3,2},{4,5},{5,4},{8,9},{9,8},{10,11},{11,10},{12,13},{13,12... | collective-permute-start | bytes 1966088 | tf_op jit(solution)/shard_map/ppermute | solution.py:195
  64.6 9.3 %collective-permute-done.16.refs_4_ = bf16[128,2560]{1,0:T(8,128)(2,1)} collective-permute-done((bf16[128,2560]{1,0:T(8,128)(2,1)}, bf16[128,2560]{1,0:T(8,128)(2,1)}, u32[]{:S(2)}, u32[]{:S(2)}) %collective-permute-start.16) | collective-permute-done | bytes 655392 | tf_op jit(solution)/shard_map/ppermute | solution.py:190
  73.8 2.8 %collective-permute-start.17 = (bf16[128,2560]{1,0:T(8,128)(2,1)}, bf16[128,2560]{1,0:T(8,128)(2,1)}, u32[]{:S(2)}, u32[]{:S(2)}) collective-permute-start(bf16[128,2560]{1,0:T(8,128)(2,1)} %collective-permute-done.16.refs_4_), channel_id=1, source_target_pairs={{2,3},{3,2},{4,5},{5,4},{8,9},{9,8},{10,11},{11,10},{12,13},{13,12... | collective-permute-start | bytes 1966088 | tf_op jit(solution)/shard_map/ppermute | solution.py:195
  77.4 6.1 %shard_map.64 = (f32[128,2560]{1,0:T(8,128)}, f32[128,2560]{1,0:T(8,128)}) custom-call(bf16[128,2560]{1,0:T(8,128)(2,1)} %refs_1_.5, bf16[128,2560]{1,0:T(8,128)(2,1)} %refs_1_.3, bf16[128,2560]{1,0:T(8,128)(2,1)} %copy-done.8, bf16[128,2560]{1,0:T(8,128)(2,1)} %refs_3_.1, bf16[128,2560]{1,0:T(8,128)(2,1)} %copy-done.9), custom_call_target="tpu_custom_call" | custom-call | flops 335544320 | bytes 5898240 | tf_op jit(solution)/shard_map/pallas_call | solution.py:176
  83.5 8.2 %shard_map.65 = (bf16[128,5120]{1,0:T(8,128)(2,1)}, bf16[128,5120]{1,0:T(8,128)(2,1)}, f32[128,2560]{1,0:T(8,128)}, f32[128,2560]{1,0:T(8,128)}) custom-call(f32[2]{0:T(128)} %compare_select_fusion.refs_0_, bf16[128,2560]{1,0:T(8,128)(2,1)} %refs_1_.5, bf16[128,2560]{1,0:T(8,128)(2,1)} %copy-done.4, bf16[128,2560]{1,0:T(8,128)(2,1)} %copy-done.6, ...), custom_call_target="tpu_custom_call" | custom-call | flops 335544320 | bytes 11141120 | tf_op jit(solution)/shard_map/pallas_call | solution.py:176
  91.7 6.0 %shard_map.66.refs_6_ = f32[128,2560]{1,0:T(8,128)} custom-call(f32[128,2560]{1,0:T(8,128)} %get-tuple-element.19.base_ref, bf16[128,5120]{1,0:T(8,128)(2,1)} %get-tuple-element.20.refs_0_, bf16[128,5120]{1,0:T(8,128)(2,1)} %get-tuple-element.21.refs_1_, bf16[128,2560]{1,0:T(8,128)(2,1)} %collective-permute-done.10.refs_2_, ...), custom_call_target="tpu_custom_call" | custom-call | flops 335544320 | bytes 7864320 | tf_op jit(solution)/shard_map/pallas_call | solution.py:176
  99.1 6.1 %shard_map.67 = (bf16[128,5120]{1,0:T(8,128)(2,1)S(1)}, bf16[128,5120]{1,0:T(8,128)(2,1)S(1)}, f32[128,2560]{1,0:T(8,128)S(1)}, f32[128,2560]{1,0:T(8,128)}) custom-call(f32[2]{0:T(128)S(1)} %compare_select_fusion.2.refs_0_, bf16[128,2560]{1,0:T(8,128)(2,1)S(1)} %copy-done.1, bf16[128,2560]{1,0:T(8,128)(2,1)S(1)} %collective-permute-done.2.refs_2_, ...), custom_call_target="tpu_custom_call" | custom-call | flops 335544320 | bytes 11141120 | tf_op jit(solution)/shard_map/pallas_call | solution.py:176
  105.2 4.9 %shard_map.68 = bf16[128,2560]{1,0:T(8,128)(2,1)} custom-call(f32[128,2560]{1,0:T(8,128)S(1)} %get-tuple-element.23.base_ref, bf16[128,5120]{1,0:T(8,128)(2,1)S(1)} %get-tuple-element.24.refs_0_, bf16[128,5120]{1,0:T(8,128)(2,1)S(1)} %get-tuple-element.25.refs_1_, bf16[128,2560]{1,0:T(8,128)(2,1)S(1)} %collective-permute-done.14.refs_2_, ...), custom_call_target="tpu_custom_call" | custom-call | flops 335544320 | bytes 7208960 | tf_op jit(solution)/shard_map/pallas_call | solution.py:176
  (42 shorter events, 7.1 us)
Async XLA Ops:
  0.0 52.9 %copy-start = (s32[8,5]{1,0:T(8,128)S(1)}, s32[8,5]{1,0:T(8,128)}, u32[]{:S(2)}) copy-start(s32[8,5]{1,0:T(8,128)} %param.9) | copy-start | bytes 484
  0.0 18.7 %collective-permute-start = (bf16[128,2560]{1,0:T(8,128)(2,1)}, bf16[128,2560]{1,0:T(8,128)(2,1)S(1)}, u32[]{:S(2)}, u32[]{:S(2)}) collective-permute-start(bf16[128,2560]{1,0:T(8,128)(2,1)} %refs_1_.3), channel_id=1, source_target_pairs={{0,8},{2,10},{8,0},{10,2},{1,9},{3,11},{9,1},{11,3},{16,24},{18,26... | collective-permute-start | bytes 1966088 | tf_op jit(solution)/shard_map/ppermute | solution.py:190
  4.3 17.5 %collective-permute-start.1 = (bf16[128,2560]{1,0:T(8,128)(2,1)}, bf16[128,2560]{1,0:T(8,128)(2,1)S(1)}, u32[]{:S(2)}, u32[]{:S(2)}) collective-permute-start(bf16[128,2560]{1,0:T(8,128)(2,1)} %refs_1_.3), channel_id=1, source_target_pairs={{0,2},{2,0},{4,6},{6,4},{10,12},{12,10},{1,3},{3,1},{5,7},{7,5},{1... | collective-permute-start | bytes 1966088 | tf_op jit(solution)/shard_map/ppermute | solution.py:190
  6.5 26.4 %collective-permute-start.10 = (bf16[128,2560]{1,0:T(8,128)(2,1)}, bf16[128,2560]{1,0:T(8,128)(2,1)}, u32[]{:S(2)}, u32[]{:S(2)}) collective-permute-start(bf16[128,2560]{1,0:T(8,128)(2,1)} %refs_3_.1), channel_id=1, source_target_pairs={{0,8},{2,10},{8,0},{10,2},{1,9},{3,11},{9,1},{11,3},{16,24},{18,26... | collective-permute-start | bytes 1966088 | tf_op jit(solution)/shard_map/ppermute | solution.py:190
  8.4 27.9 %collective-permute-start.12 = (bf16[128,2560]{1,0:T(8,128)(2,1)}, bf16[128,2560]{1,0:T(8,128)(2,1)}, u32[]{:S(2)}, u32[]{:S(2)}) collective-permute-start(bf16[128,2560]{1,0:T(8,128)(2,1)} %refs_3_.1), channel_id=1, source_target_pairs={{0,2},{2,0},{4,6},{6,4},{10,12},{12,10},{1,3},{3,1},{5,7},{7,5},{1... | collective-permute-start | bytes 1966088 | tf_op jit(solution)/shard_map/ppermute | solution.py:190
  11.6 28.1 %collective-permute-start.8 = (bf16[128,2560]{1,0:T(8,128)(2,1)}, bf16[128,2560]{1,0:T(8,128)(2,1)S(1)}, u32[]{:S(2)}, u32[]{:S(2)}) collective-permute-start(bf16[128,2560]{1,0:T(8,128)(2,1)} %refs_1_.3), channel_id=1, source_target_pairs={{0,1},{1,0},{2,3},{3,2},{4,5},{5,4},{6,7},{7,6},{8,9},{9,8},{10,11... | collective-permute-start | bytes 1966088 | tf_op jit(solution)/shard_map/ppermute | solution.py:195
  18.7 64.8 %copy-start.4 = (bf16[128,2560]{1,0:T(8,128)(2,1)}, bf16[128,2560]{1,0:T(8,128)(2,1)S(1)}, u32[]{:S(2)}) copy-start(bf16[128,2560]{1,0:T(8,128)(2,1)S(1)} %collective-permute-done.refs_2_) | copy-start | bytes 1966084
  18.7 21.6 %collective-permute-start.9 = (bf16[128,2560]{1,0:T(8,128)(2,1)}, bf16[128,2560]{1,0:T(8,128)(2,1)S(1)}, u32[]{:S(2)}, u32[]{:S(2)}) collective-permute-start(bf16[128,2560]{1,0:T(8,128)(2,1)} %refs_3_.1), channel_id=1, source_target_pairs={{0,1},{1,0},{2,3},{3,2},{4,5},{5,4},{6,7},{7,6},{8,9},{9,8},{10,11... | collective-permute-start | bytes 1966088 | tf_op jit(solution)/shard_map/ppermute | solution.py:195
  21.9 61.6 %copy-start.5 = (bf16[128,2560]{1,0:T(8,128)(2,1)}, bf16[128,2560]{1,0:T(8,128)(2,1)S(1)}, u32[]{:S(2)}) copy-start(bf16[128,2560]{1,0:T(8,128)(2,1)S(1)} %collective-permute-done.1.refs_4_) | copy-start | bytes 1966084
  21.9 20.6 %collective-permute-start.6 = (bf16[128,2560]{1,0:T(8,128)(2,1)S(1)}, bf16[128,2560]{1,0:T(8,128)(2,1)S(1)}, u32[]{:S(2)}, u32[]{:S(2)}) collective-permute-start(bf16[128,2560]{1,0:T(8,128)(2,1)S(1)} %collective-permute-done.refs_2_), channel_id=1, source_target_pairs={{0,1},{1,0},{2,3},{3,2},{8,9},{9,8},{10,11},{11,10},{16,17},{17,16... | collective-permute-start | bytes 1966088 | tf_op jit(solution)/shard_map/ppermute | solution.py:195
  32.9 10.4 %collective-permute-start.7 = (bf16[128,2560]{1,0:T(8,128)(2,1)S(1)}, bf16[128,2560]{1,0:T(8,128)(2,1)S(1)}, u32[]{:S(2)}, u32[]{:S(2)}) collective-permute-start(bf16[128,2560]{1,0:T(8,128)(2,1)S(1)} %collective-permute-done.1.refs_4_), channel_id=1, source_target_pairs={{0,1},{1,0},{2,3},{3,2},{4,5},{5,4},{6,7},{7,6},{10,11},{11,10},{1... | collective-permute-start | bytes 1966088 | tf_op jit(solution)/shard_map/ppermute | solution.py:195
  36.3 13.8 %collective-permute-start.11 = (bf16[128,2560]{1,0:T(8,128)(2,1)}, bf16[128,2560]{1,0:T(8,128)(2,1)}, u32[]{:S(2)}, u32[]{:S(2)}) collective-permute-start(bf16[128,2560]{1,0:T(8,128)(2,1)} %collective-permute-done.10.refs_2_), channel_id=1, source_target_pairs={{0,1},{1,0},{2,3},{3,2},{8,9},{9,8},{10,11},{11,10},{16,17},{17,16... | collective-permute-start | bytes 1966088 | tf_op jit(solution)/shard_map/ppermute | solution.py:195
  39.7 9.8 %copy-start.8 = (bf16[128,2560]{1,0:T(8,128)(2,1)}, bf16[128,2560]{1,0:T(8,128)(2,1)S(1)}, u32[]{:S(2)}) copy-start(bf16[128,2560]{1,0:T(8,128)(2,1)S(1)} %collective-permute-done.8.refs_2_) | copy-start | bytes 1966084
  39.7 13.2 %collective-permute-start.2 = (bf16[128,2560]{1,0:T(8,128)(2,1)}, bf16[128,2560]{1,0:T(8,128)(2,1)S(1)}, u32[]{:S(2)}, u32[]{:S(2)}) collective-permute-start(bf16[128,2560]{1,0:T(8,128)(2,1)} %refs_1_.3), channel_id=1, source_target_pairs={{4,12},{6,14},{12,4},{14,6},{5,13},{7,15},{13,5},{15,7},{20,28},{2... | collective-permute-start | bytes 1966088 | tf_op jit(solution)/shard_map/ppermute | solution.py:190
  40.4 19.4 %collective-permute-start.4 = (bf16[128,2560]{1,0:T(8,128)(2,1)}, bf16[128,2560]{1,0:T(8,128)(2,1)}, u32[]{:S(2)}, u32[]{:S(2)}) collective-permute-start(bf16[128,2560]{1,0:T(8,128)(2,1)} %refs_1_.3), channel_id=1, source_target_pairs={{2,4},{4,2},{8,10},{10,8},{12,14},{14,12},{3,5},{5,3},{9,11},{11,9... | collective-permute-start | bytes 1966088 | tf_op jit(solution)/shard_map/ppermute | solution.py:190
  42.5 41.0 %copy-start.6 = (bf16[128,2560]{1,0:T(8,128)(2,1)}, bf16[128,2560]{1,0:T(8,128)(2,1)S(1)}, u32[]{:S(2)}) copy-start(bf16[128,2560]{1,0:T(8,128)(2,1)S(1)} %collective-permute-done.6.refs_3_) | copy-start | bytes 1966084
  42.6 20.5 %collective-permute-start.14 = (bf16[128,2560]{1,0:T(8,128)(2,1)}, bf16[128,2560]{1,0:T(8,128)(2,1)S(1)}, u32[]{:S(2)}, u32[]{:S(2)}) collective-permute-start(bf16[128,2560]{1,0:T(8,128)(2,1)} %refs_3_.1), channel_id=1, source_target_pairs={{4,12},{6,14},{12,4},{14,6},{5,13},{7,15},{13,5},{15,7},{20,28},{2... | collective-permute-start | bytes 1966088 | tf_op jit(solution)/shard_map/ppermute | solution.py:190
  44.1 29.7 %collective-permute-start.16 = (bf16[128,2560]{1,0:T(8,128)(2,1)}, bf16[128,2560]{1,0:T(8,128)(2,1)}, u32[]{:S(2)}, u32[]{:S(2)}) collective-permute-start(bf16[128,2560]{1,0:T(8,128)(2,1)} %refs_3_.1), channel_id=1, source_target_pairs={{2,4},{4,2},{8,10},{10,8},{12,14},{14,12},{3,5},{5,3},{9,11},{11,9... | collective-permute-start | bytes 1966088 | tf_op jit(solution)/shard_map/ppermute | solution.py:190
  50.2 41.5 %collective-permute-start.13 = (bf16[128,2560]{1,0:T(8,128)(2,1)}, bf16[128,2560]{1,0:T(8,128)(2,1)}, u32[]{:S(2)}, u32[]{:S(2)}) collective-permute-start(bf16[128,2560]{1,0:T(8,128)(2,1)} %collective-permute-done.12.refs_4_), channel_id=1, source_target_pairs={{0,1},{1,0},{2,3},{3,2},{4,5},{5,4},{6,7},{7,6},{10,11},{11,10},{1... | collective-permute-start | bytes 1966088 | tf_op jit(solution)/shard_map/ppermute | solution.py:195
  52.9 44.8 %collective-permute-start.3 = (bf16[128,2560]{1,0:T(8,128)(2,1)S(1)}, bf16[128,2560]{1,0:T(8,128)(2,1)}, u32[]{:S(2)}, u32[]{:S(2)}) collective-permute-start(bf16[128,2560]{1,0:T(8,128)(2,1)S(1)} %collective-permute-done.2.refs_2_), channel_id=1, source_target_pairs={{4,5},{5,4},{6,7},{7,6},{12,13},{13,12},{14,15},{15,14},{20,21},{2... | collective-permute-start | bytes 1966088 | tf_op jit(solution)/shard_map/ppermute | solution.py:195
  59.8 37.9 %collective-permute-start.5 = (bf16[128,2560]{1,0:T(8,128)(2,1)}, bf16[128,2560]{1,0:T(8,128)(2,1)}, u32[]{:S(2)}, u32[]{:S(2)}) collective-permute-start(bf16[128,2560]{1,0:T(8,128)(2,1)} %collective-permute-done.4.refs_4_), channel_id=1, source_target_pairs={{2,3},{3,2},{4,5},{5,4},{8,9},{9,8},{10,11},{11,10},{12,13},{13,12... | collective-permute-start | bytes 1966088 | tf_op jit(solution)/shard_map/ppermute | solution.py:195
  63.1 42.1 %collective-permute-start.15 = (bf16[128,2560]{1,0:T(8,128)(2,1)S(1)}, bf16[128,2560]{1,0:T(8,128)(2,1)}, u32[]{:S(2)}, u32[]{:S(2)}) collective-permute-start(bf16[128,2560]{1,0:T(8,128)(2,1)S(1)} %collective-permute-done.14.refs_2_), channel_id=1, source_target_pairs={{4,5},{5,4},{6,7},{7,6},{12,13},{13,12},{14,15},{15,14},{20,21},{2... | collective-permute-start | bytes 1966088 | tf_op jit(solution)/shard_map/ppermute | solution.py:195
  73.8 31.3 %collective-permute-start.17 = (bf16[128,2560]{1,0:T(8,128)(2,1)}, bf16[128,2560]{1,0:T(8,128)(2,1)}, u32[]{:S(2)}, u32[]{:S(2)}) collective-permute-start(bf16[128,2560]{1,0:T(8,128)(2,1)} %collective-permute-done.16.refs_4_), channel_id=1, source_target_pairs={{2,3},{3,2},{4,5},{5,4},{8,9},{9,8},{10,11},{11,10},{12,13},{13,12... | collective-permute-start | bytes 1966088 | tf_op jit(solution)/shard_map/ppermute | solution.py:195
  91.7 6.0 %copy-start.1 = (bf16[128,2560]{1,0:T(8,128)(2,1)S(1)}, bf16[128,2560]{1,0:T(8,128)(2,1)}, u32[]{:S(2)}) copy-start(bf16[128,2560]{1,0:T(8,128)(2,1)} %refs_1_.5) | copy-start | bytes 1966084
  (4 other events, 10.3 us)

commit v5 on v3

v5 whole, which is shorter than its diff:
```python
import functools

import jax
import jax.numpy as jnp
from jax import lax
from jax.experimental import pallas as pl
from jax.experimental.pallas import tpu as pltpu
from jax.sharding import PartitionSpec as P


HD = 128
TILE_H = 4
OFFSETS = (0, -1, 1, -TILE_H, TILE_H)
SCALE = HD ** (-0.5) * 1.4426950408889634
FAR_BELOW = -1e30
HEADS_AT_ONCE = 4
VMEM_BYTES = 16 * 1024 * 1024


def plan(rows):
    near, relay, far = ({}, {}), ({}, {}), [({}, {}), ({}, {})]
    for row in range(rows):
        other = row ^ 1
        if other < rows:
            near[0][other] = row
            near[1][row] = OFFSETS.index(other - row)
        start = row - row % TILE_H
        if row % TILE_H in (1, 2) and start + TILE_H <= rows:
            other = 2 * start + 3 - row
            relay[0][other ^ 1] = row
            relay[1][row] = OFFSETS.index(other - row)
        for way in (0, 1):
            other = row + TILE_H if (row // TILE_H) % 2 == way else row - TILE_H
            if 0 <= other < rows:
                far[way][0][other] = row
                far[way][1][row] = OFFSETS.index(other - row)
    return near, relay, [pair for pair in far if pair[0]]


def lanes(value):
    return [value[:, at : at + HD] for at in range(0, value.shape[1], HD)]


def over_row(reduce, join, slices):
    found = reduce(functools.reduce(join, slices), axis=1, keepdims=True)
    return jnp.broadcast_to(found, slices[0].shape)


def attend_chunk(heads, merging, mixed, held, bias_ref, refs, score_ref, weight_ref):
    refs = list(refs)
    blocks = mixed + held
    q_ref = refs.pop(0)
    k_refs, refs = refs[: 2 * blocks], refs[2 * blocks :]
    v_refs, refs = refs[: 2 * mixed], refs[2 * mixed :]
    if merging:
        before_ref, stat_ref, *refs = refs
    out_ref, *refs = refs
    held_refs, refs = refs[:held], refs[held:]
    total_ref = refs[0] if refs else None
    keys_each = 2 * k_refs[0].shape[0]
    each = keys_each // HD
    kept = {}

    def score(head, here):
        for n in range(blocks):
            keys = jnp.concatenate([k_refs[2 * n][:, here], k_refs[2 * n + 1][:, here]], axis=0)
            found = lax.dot_general(
                q_ref[:, here], keys, (((1,), (1,)), ((), ())), preferred_element_type=jnp.float32
            )
            found = found * SCALE
            if merging:
                found = found + bias_ref[n]
            score_ref[head, :, n * keys_each : (n + 1) * keys_each] = found

    def weigh(head, here):
        slices = lanes(score_ref[head])
        top = over_row(jnp.max, jnp.maximum, slices)
        if merging:
            before = stat_ref[:, here]
            top = jnp.maximum(top, before)
        weights = [jnp.exp2(s - top) for s in slices]
        total = over_row(jnp.sum, jnp.add, weights)
        factor = None
        if merging:
            factor = jnp.exp2(before - top)
            total = total + factor
        inverse = 1.0 / total
        if total_ref is not None:
            total_ref[:, here] = top + jnp.log2(total)
        for at, w in enumerate(weights):
            n = at // each
            if n < mixed:
                weight_ref[head, :, at * HD : (at + 1) * HD] = w.astype(jnp.bfloat16)
            else:
                start = head * keys_each + at % each * HD
                held_refs[n - mixed][:, start : start + HD] = (w * inverse).astype(jnp.bfloat16)
        kept[head] = (inverse, factor * inverse if merging else None)

    def mix(head, here):
        inverse, factor = kept.pop(head)
        out = jnp.dot(
            weight_ref[head],
            jnp.concatenate([v[:, here] for v in v_refs], axis=0),
            preferred_element_type=jnp.float32,
        )
        out = out * inverse
        if merging:
            out = out + before_ref[:, here] * factor
        out_ref[:, here] = out

    steps = [score, weigh, mix]
    for time in range(heads + len(steps) - 1):
        for number, step in enumerate(steps):
            head = time - number
            if 0 <= head < heads:
                step(head, slice(head * HD, (head + 1) * HD))


def finish_chunk(heads, blocks, refs):
    base_ref, refs = refs[0], refs[1:]
    weight_refs, v_refs, out_ref = refs[:blocks], refs[blocks : 3 * blocks], refs[-1]
    keys_each = 2 * v_refs[0].shape[0]
    for head in range(heads):
        here = slice(head * HD, (head + 1) * HD)
        weights = [w[:, head * keys_each : (head + 1) * keys_each] for w in weight_refs]
        out = jnp.dot(
            jnp.concatenate(weights, axis=1),
            jnp.concatenate([v[:, here] for v in v_refs], axis=0),
            preferred_element_type=jnp.float32,
        )
        out_ref[:, here] = (base_ref[:, here] + out).astype(out_ref.dtype)


def divisor(heads, most):
    return max(n for n in range(1, most + 1) if heads % n == 0)


def call(chunk, at_once, scalars, operands, out_types, scratch, dots, keys):
    tokens, width = operands[0].shape
    heads = divisor(width // HD, at_once)
    steps = width // (heads * HD)
    arrays = len(operands) + len(out_types)

    def kernel(*refs):
        scalar_refs, refs = refs[: len(scalars)], refs[len(scalars) :]
        array_refs, scratch_refs = refs[:arrays], refs[arrays:]

        def step(i, carry):
            views = []
            for ref in array_refs:
                wide = ref.shape[1] // steps
                views.append(ref.at[:, pl.ds(pl.multiple_of(i * wide, wide), wide)])
            chunk(heads, scalar_refs, views, scratch_refs)
            return carry

        lax.fori_loop(0, steps, step, 0)

    whole = pl.BlockSpec(memory_space=pltpu.VMEM)
    run = pl.pallas_call(
        kernel,
        in_specs=[pl.BlockSpec(memory_space=pltpu.SMEM)] * len(scalars) + [whole] * len(operands),
        out_specs=[whole] * len(out_types),
        out_shape=out_types,
        scratch_shapes=[pltpu.VMEM((heads,) + shape, t) for shape, t in scratch],
        cost_estimate=pl.CostEstimate(
            flops=dots * 2 * tokens * keys * width,
            transcendentals=tokens * keys * (width // HD),
            bytes_accessed=sum(a.size * a.dtype.itemsize for a in list(operands) + list(out_types)),
        ),
        compiler_params=pltpu.CompilerParams(vmem_limit_bytes=VMEM_BYTES),
    )
    return list(run(*scalars, *operands))


def attend(bias, queries, k_pairs, v_pairs, before, more):
    tokens, width = queries.shape
    merging, mixed, held = before is not None, len(v_pairs), len(k_pairs) - len(v_pairs)
    keys = 2 * tokens * len(k_pairs)

    def chunk(heads, scalar_refs, views, scratch_refs):
        attend_chunk(heads, merging, mixed, held, *(scalar_refs or (None,)), views, *scratch_refs)

    full = jax.ShapeDtypeStruct((tokens, width), jnp.float32)
    weight = jax.ShapeDtypeStruct((tokens, 2 * tokens * (width // HD)), jnp.bfloat16)
    operands = [queries] + [a for p in k_pairs for a in p] + [a for p in v_pairs for a in p]
    operands += list(before) if merging else []
    outs = [full] + [weight] * held + ([full] if more else [])
    scratch = [((tokens, keys), jnp.float32), ((tokens, 2 * tokens * mixed), jnp.bfloat16)]
    scalars = [bias] if merging else []
    return call(chunk, HEADS_AT_ONCE, scalars, operands, outs, scratch, 2, keys)


def finish(base, weights, v_pairs, dtype):
    tokens, width = base.shape
    blocks = len(v_pairs)

    def chunk(heads, scalar_refs, views, scratch_refs):
        finish_chunk(heads, blocks, views)

    operands = [base] + weights + [a for p in v_pairs for a in p]
    outs = [jax.ShapeDtypeStruct((tokens, width), dtype)]
    return call(chunk, 10, [], operands, outs, [], 1, 2 * tokens * blocks)[0]


def after(value, *others):
    return lax.optimization_barrier((value,) + others)[0]


def shards(routes, queries, keys, values, pattern):
    rows = lax.axis_size("row")
    cols = lax.axis_size("col")
    row = lax.axis_index("row")
    near, relay, far = routes

    def moved(value, route):
        return lax.ppermute(value, "row", sorted(route[0].items()))

    def paired(value, route):
        reached = range(rows) if route is None else sorted(route[1])
        pairs = [(r * cols + c, r * cols + cols - 1 - c) for r in reached for c in range(cols)]
        return value, lax.ppermute(value, ("row", "col"), pairs)

    own_row = lax.dynamic_index_in_dim(pattern, row, 0, keepdims=True)

    def biases(*given):
        table = [[route[1].get(r, len(OFFSETS)) for route in given] for r in range(rows)]
        picks = jnp.asarray(table, jnp.int32)[row]
        here = jnp.arange(len(OFFSETS), dtype=jnp.int32)[None, :] == picks[:, None]
        live = jnp.sum(jnp.where(here, own_row, 0), axis=1)
        return jnp.where(live == 1, 0.0, FAR_BELOW).astype(jnp.float32)

    v_near = moved(values, near)
    k_far = [moved(keys, route) for route in far]
    v_far = [moved(values, route) for route in far]
    k_own, v_own = paired(keys, None), paired(values, None)
    k_near = moved(after(keys, v_near), near)
    v_relay = moved(v_near, relay)
    k_relay = moved(k_near, relay)

    carried = attend(None, queries, [k_own], [v_own], None, True)
    carried = attend(
        biases(near), queries, [paired(k_near, near)], [paired(v_near, near)], carried, True
    )
    k_pairs = [paired(k_relay, relay)]
    k_pairs += [paired(k, route) for k, route in zip(k_far, far)]
    base, *weights = attend(
        biases(relay, *far), queries, k_pairs, [paired(v_relay, relay)], carried, False
    )
    v_pairs = [paired(v, route) for v, route in zip(v_far, far)]
    return finish(base, weights, v_pairs, queries.dtype)


def solution(mesh):
    placed = P(("groups", "row", "col"), None)
    routes = plan(mesh.shape["row"])

    def body(*args):
        return shards(routes, *args)

    return jax.shard_map(
        body,
        mesh=mesh,
        in_specs=(placed, placed, placed, P("groups", None)),
        out_specs=placed,
        check_vma=False,
    )
```

time: 104 us -> 111 us (1.067)
  the two profiles are of different devices: /device:TPU:9 before, /device:TPU:25 now
where the time goes in v5:
time: 111 us; the launch traced here: 110 us
  waiting for transfers between devices  63.7 us (57%)
  starting transfers between devices  18.8 us (17%)
  Pallas kernels  14.1 us (13%)
  local copies, waits for them, and re-layouts  10.8 us (10%)
  other arithmetic  2.2 us (2%)
    ppermute x6, waiting for transfers between devices, moved(): return lax.ppermute(value, 'row', sorted(route[0].items()))  63.7 us
    pallas_call x4, Pallas kernels, call(): return list(run(*scalars, *operands))  14.1 us
    ppermute x8, starting transfers between devices, paired(): return (value, lax.ppermute(value, ('row', 'col'), pairs))  11.4 us
    unnamed x22, local copies, waits for them, and re-layouts  8.78 us
    ppermute x6, starting transfers between devices, moved(): return lax.ppermute(value, 'row', sorted(route[0].items()))  7.4 us
  transfers between devices with their start and end apart: 14, of which 5 were waited for; matrix products, arithmetic and copies ran while one was open for 4% of the time, Pallas kernels for 10%

profile of v5, /device:TPU:25, one launch (start us, length us, event | category | flops | bytes accessed | tf_op | source)
XLA Modules:
  0.0 110.4 jit_solution(13301042406131991090)
XLA Ops:
  0.0 1.2 %collective-permute-start = (bf16[128,2560]{1,0:T(8,128)(2,1)}, bf16[128,2560]{1,0:T(8,128)(2,1)S(1)}, u32[]{:S(2)}, u32[]{:S(2)}) collective-permute-start(bf16[128,2560]{1,0:T(8,128)(2,1)} %refs_3_.1), channel_id=1, source_target_pairs={{0,2},{2,0},{4,6},{6,4},{8,10},{10,8},{12,14},{14,12},{1,3},{3,1},... | collective-permute-start | bytes 1966088 | tf_op jit(solution)/shard_map/ppermute | solution.py:216
  2.2 13.6 %collective-permute-done.refs_4_ = bf16[128,2560]{1,0:T(8,128)(2,1)S(1)} collective-permute-done((bf16[128,2560]{1,0:T(8,128)(2,1)}, bf16[128,2560]{1,0:T(8,128)(2,1)S(1)}, u32[]{:S(2)}, u32[]{:S(2)}) %collective-permute-start) | collective-permute-done | bytes 655392 | tf_op jit(solution)/shard_map/ppermute | solution.py:216
  15.8 1.2 %collective-permute-start.1 = (bf16[128,2560]{1,0:T(8,128)(2,1)}, bf16[128,2560]{1,0:T(8,128)(2,1)}, u32[]{:S(2)}, u32[]{:S(2)}) collective-permute-start(bf16[128,2560]{1,0:T(8,128)(2,1)} %refs_1_.3), channel_id=1, source_target_pairs={{0,2},{2,0},{4,6},{6,4},{8,10},{10,8},{12,14},{14,12},{1,3},{3,1},... | collective-permute-start | bytes 1966088 | tf_op jit(solution)/shard_map/ppermute | solution.py:216
  17.1 1.8 %collective-permute-start.11 = (bf16[128,2560]{1,0:T(8,128)(2,1)}, bf16[128,2560]{1,0:T(8,128)(2,1)S(1)}, u32[]{:S(2)}, u32[]{:S(2)}) collective-permute-start(bf16[128,2560]{1,0:T(8,128)(2,1)} %refs_3_.1), channel_id=1, source_target_pairs={{0,1},{1,0},{2,3},{3,2},{4,5},{5,4},{6,7},{7,6},{8,9},{9,8},{10,11... | collective-permute-start | bytes 1966088 | tf_op jit(solution)/shard_map/ppermute | solution.py:221
  18.9 2.3 %collective-permute-start.12 = (bf16[128,2560]{1,0:T(8,128)(2,1)}, bf16[128,2560]{1,0:T(8,128)(2,1)}, u32[]{:S(2)}, u32[]{:S(2)}) collective-permute-start(bf16[128,2560]{1,0:T(8,128)(2,1)} %refs_3_.1), channel_id=1, source_target_pairs={{0,8},{2,10},{4,12},{6,14},{8,0},{10,2},{12,4},{14,6},{1,9},{3,11}... | collective-permute-start | bytes 1966088 | tf_op jit(solution)/shard_map/ppermute | solution.py:216
  22.1 1.3 %collective-permute-start.6 = (bf16[128,2560]{1,0:T(8,128)(2,1)S(1)}, bf16[128,2560]{1,0:T(8,128)(2,1)S(1)}, u32[]{:S(2)}, u32[]{:S(2)}) collective-permute-start(bf16[128,2560]{1,0:T(8,128)(2,1)S(1)} %collective-permute-done.refs_4_), channel_id=1, source_target_pairs={{0,4},{6,2},{8,12},{14,10},{1,5},{7,3},{9,13},{15,11},{16,20},{22,... | collective-permute-start | bytes 1966088 | tf_op jit(solution)/shard_map/ppermute | solution.py:216
  23.4 7.5 %collective-permute-done.1.refs_2_ = bf16[128,2560]{1,0:T(8,128)(2,1)} collective-permute-done((bf16[128,2560]{1,0:T(8,128)(2,1)}, bf16[128,2560]{1,0:T(8,128)(2,1)}, u32[]{:S(2)}, u32[]{:S(2)}) %collective-permute-start.1) | collective-permute-done | bytes 655392 | tf_op jit(solution)/shard_map/ppermute | solution.py:216
  30.9 1.3 %collective-permute-start.2 = (bf16[128,2560]{1,0:T(8,128)(2,1)}, bf16[128,2560]{1,0:T(8,128)(2,1)S(1)}, u32[]{:S(2)}, u32[]{:S(2)}) collective-permute-start(bf16[128,2560]{1,0:T(8,128)(2,1)} %collective-permute-done.1.refs_2_), channel_id=1, source_target_pairs={{0,4},{6,2},{8,12},{14,10},{1,5},{7,3},{9,13},{15,11},{16,20},{22,... | collective-permute-start | bytes 1966088 | tf_op jit(solution)/shard_map/ppermute | solution.py:216
  33.0 2.4 %collective-permute-start.9 = (bf16[128,2560]{1,0:T(8,128)(2,1)S(1)}, bf16[128,2560]{1,0:T(8,128)(2,1)S(1)}, u32[]{:S(2)}, u32[]{:S(2)}) collective-permute-start(bf16[128,2560]{1,0:T(8,128)(2,1)S(1)} %collective-permute-done.refs_4_), channel_id=1, source_target_pairs={{0,1},{1,0},{2,3},{3,2},{4,5},{5,4},{6,7},{7,6},{8,9},{9,8},{10,11... | collective-permute-start | bytes 1966088 | tf_op jit(solution)/shard_map/ppermute | solution.py:221
  36.3 28.4 %collective-permute-done.4.refs_4_ = bf16[128,2560]{1,0:T(8,128)(2,1)S(1)} collective-permute-done((bf16[128,2560]{1,0:T(8,128)(2,1)}, bf16[128,2560]{1,0:T(8,128)(2,1)S(1)}, u32[]{:S(2)}, u32[]{:S(2)}) %collective-permute-start.4) | collective-permute-done | bytes 655392 | tf_op jit(solution)/shard_map/ppermute | solution.py:216
  65.3 13.6 %collective-permute-done.12.refs_2_ = bf16[128,2560]{1,0:T(8,128)(2,1)} collective-permute-done((bf16[128,2560]{1,0:T(8,128)(2,1)}, bf16[128,2560]{1,0:T(8,128)(2,1)}, u32[]{:S(2)}, u32[]{:S(2)}) %collective-permute-start.12) | collective-permute-done | bytes 655392 | tf_op jit(solution)/shard_map/ppermute | solution.py:216
  79.4 1.9 %collective-permute-start.7 = (bf16[128,2560]{1,0:T(8,128)(2,1)S(1)}, bf16[128,2560]{1,0:T(8,128)(2,1)S(1)}, u32[]{:S(2)}, u32[]{:S(2)}) collective-permute-start(bf16[128,2560]{1,0:T(8,128)(2,1)S(1)} %collective-permute-done.6.refs_6_), channel_id=1, source_target_pairs={{2,3},{3,2},{4,5},{5,4},{10,11},{11,10},{12,13},{13,12},{18,19},{1... | collective-permute-start | bytes 1966088 | tf_op jit(solution)/shard_map/ppermute | solution.py:221
  81.7 3.3 %collective-permute-start.3 = (bf16[128,2560]{1,0:T(8,128)(2,1)S(1)}, bf16[128,2560]{1,0:T(8,128)(2,1)}, u32[]{:S(2)}, u32[]{:S(2)}) collective-permute-start(bf16[128,2560]{1,0:T(8,128)(2,1)S(1)} %collective-permute-done.2.refs_2_), channel_id=1, source_target_pairs={{2,3},{3,2},{4,5},{5,4},{10,11},{11,10},{12,13},{13,12},{18,19},{1... | collective-permute-start | bytes 1966088 | tf_op jit(solution)/shard_map/ppermute | solution.py:221
  85.9 1.3 %constant_dynamic-slice_fusion = s32[1,1]{1,0:T(1,128)} fusion(s32[8,1]{1,0:T(8,128)} %constant.30.clone, s32[]{:T(128)S(6)} %select_n.24), kind=kLoop, calls=%fused_computation.4 | loop fusion | bytes 12 | tf_op jit(solution)/shard_map/dynamic_slice | solution.py:227
  87.2 2.0 %fusion.2 = (s32[]{:T(128)}, s32[5]{0:T(128)S(1)}) fusion(s32[]{:T(128)} %bitcast.2, s32[8,5]{1,0:T(8,128)} %param.9, s32[]{:T(128)S(6)} %select_n.24), kind=kLoop, calls=%fused_computation.8 | loop fusion | flops 14 | bytes 52 | tf_op jit(solution)/shard_map/reduce_sum | solution.py:229
  90.7 1.1 copy-done
  91.8 1.1 copy-done.5
  92.9 1.1 copy-done.6
  93.9 1.1 copy-done.8
  95.0 1.1 copy-done.10
  96.1 2.5 %shard_map.64 = (f32[128,2560]{1,0:T(8,128)S(1)}, f32[128,2560]{1,0:T(8,128)S(1)}) custom-call(bf16[128,2560]{1,0:T(8,128)(2,1)S(1)} %copy-done, bf16[128,2560]{1,0:T(8,128)(2,1)S(1)} %copy-done.5, bf16[128,2560]{1,0:T(8,128)(2,1)S(1)} %copy-done.8, bf16[128,2560]{1,0:T(8,128)(2,1)S(1)} %copy-done.6, bf16[128,2560]{1,0:T(8,128)(2,1)S(1)} %copy-done.10), custom_call_target="tpu_custom_call" | custom-call | flops 335544320 | bytes 5898240 | tf_op jit(solution)/shard_map/pallas_call | solution.py:172
  98.7 3.9 %shard_map.65 = (f32[128,2560]{1,0:T(8,128)S(1)}, f32[128,2560]{1,0:T(8,128)S(1)}) custom-call(f32[1]{0:T(128)} %bitcast.3.refs_0_, bf16[128,2560]{1,0:T(8,128)(2,1)S(1)} %copy-done, bf16[128,2560]{1,0:T(8,128)(2,1)} %collective-permute-done.1.refs_2_, bf16[128,2560]{1,0:T(8,128)(2,1)} %collective-permute-done.8.refs_3_, bf16[128,2560]{1,0:T(8,128)(2,1)S(1)} %copy-done.2, ...), custom_call_target="tpu_custom_call" | custom-call | flops 335544320 | bytes 8519680 | tf_op jit(solution)/shard_map/pallas_call | solution.py:172
  102.6 4.9 %shard_map.66 = (f32[128,2560]{1,0:T(8,128)S(1)}, bf16[128,5120]{1,0:T(8,128)(2,1)S(1)}) custom-call(f32[2]{0:T(128)S(1)} %compare_select_fusion.1.refs_0_, bf16[128,2560]{1,0:T(8,128)(2,1)S(1)} %copy-done, bf16[128,2560]{1,0:T(8,128)(2,1)S(1)} %collective-permute-done.2.refs_2_, bf16[128,2560]{1,0:T(8,128)(2,1)} %collective-permute-done.3.refs_3_, ...), custom_call_target="tpu_custom_call" | custom-call | flops 671088640 | bytes 9830400 | tf_op jit(solution)/shard_map/pallas_call | solution.py:172
  107.6 2.8 %shard_map.67 = bf16[128,2560]{1,0:T(8,128)(2,1)} custom-call(f32[128,2560]{1,0:T(8,128)S(1)} %get-tuple-element.17.refs_0_, bf16[128,5120]{1,0:T(8,128)(2,1)S(1)} %get-tuple-element.18.refs_1_, bf16[128,2560]{1,0:T(8,128)(2,1)} %collective-permute-done.12.refs_2_, bf16[128,2560]{1,0:T(8,128)(2,1)} %collective-permute-done.13.refs_3_), custom_call_target="tpu_custom_call" | custom-call | flops 167772160 | bytes 4587520 | tf_op jit(solution)/shard_map/pallas_call | solution.py:172
  (35 shorter events, 6.8 us)
Async XLA Ops:
  0.0 15.8 %collective-permute-start = (bf16[128,2560]{1,0:T(8,128)(2,1)}, bf16[128,2560]{1,0:T(8,128)(2,1)S(1)}, u32[]{:S(2)}, u32[]{:S(2)}) collective-permute-start(bf16[128,2560]{1,0:T(8,128)(2,1)} %refs_3_.1), channel_id=1, source_target_pairs={{0,2},{2,0},{4,6},{6,4},{8,10},{10,8},{12,14},{14,12},{1,3},{3,1},... | collective-permute-start | bytes 1966088 | tf_op jit(solution)/shard_map/ppermute | solution.py:216
  1.2 20.0 %collective-permute-start.10 = (bf16[128,2560]{1,0:T(8,128)(2,1)}, bf16[128,2560]{1,0:T(8,128)(2,1)S(1)}, u32[]{:S(2)}, u32[]{:S(2)}) collective-permute-start(bf16[128,2560]{1,0:T(8,128)(2,1)} %refs_1_.3), channel_id=1, source_target_pairs={{0,1},{1,0},{2,3},{3,2},{4,5},{5,4},{6,7},{7,6},{8,9},{9,8},{10,11... | collective-permute-start | bytes 1966088 | tf_op jit(solution)/shard_map/ppermute | solution.py:221
  15.8 15.1 %collective-permute-start.1 = (bf16[128,2560]{1,0:T(8,128)(2,1)}, bf16[128,2560]{1,0:T(8,128)(2,1)}, u32[]{:S(2)}, u32[]{:S(2)}) collective-permute-start(bf16[128,2560]{1,0:T(8,128)(2,1)} %refs_1_.3), channel_id=1, source_target_pairs={{0,2},{2,0},{4,6},{6,4},{8,10},{10,8},{12,14},{14,12},{1,3},{3,1},... | collective-permute-start | bytes 1966088 | tf_op jit(solution)/shard_map/ppermute | solution.py:216
  17.1 15.1 %collective-permute-start.11 = (bf16[128,2560]{1,0:T(8,128)(2,1)}, bf16[128,2560]{1,0:T(8,128)(2,1)S(1)}, u32[]{:S(2)}, u32[]{:S(2)}) collective-permute-start(bf16[128,2560]{1,0:T(8,128)(2,1)} %refs_3_.1), channel_id=1, source_target_pairs={{0,1},{1,0},{2,3},{3,2},{4,5},{5,4},{6,7},{7,6},{8,9},{9,8},{10,11... | collective-permute-start | bytes 1966088 | tf_op jit(solution)/shard_map/ppermute | solution.py:221
  18.9 45.8 %collective-permute-start.4 = (bf16[128,2560]{1,0:T(8,128)(2,1)}, bf16[128,2560]{1,0:T(8,128)(2,1)S(1)}, u32[]{:S(2)}, u32[]{:S(2)}) collective-permute-start(bf16[128,2560]{1,0:T(8,128)(2,1)} %refs_1_.3), channel_id=1, source_target_pairs={{0,8},{2,10},{4,12},{6,14},{8,0},{10,2},{12,4},{14,6},{1,9},{3,11}... | collective-permute-start | bytes 1966088 | tf_op jit(solution)/shard_map/ppermute | solution.py:216
  18.9 59.9 %collective-permute-start.12 = (bf16[128,2560]{1,0:T(8,128)(2,1)}, bf16[128,2560]{1,0:T(8,128)(2,1)}, u32[]{:S(2)}, u32[]{:S(2)}) collective-permute-start(bf16[128,2560]{1,0:T(8,128)(2,1)} %refs_3_.1), channel_id=1, source_target_pairs={{0,8},{2,10},{4,12},{6,14},{8,0},{10,2},{12,4},{14,6},{1,9},{3,11}... | collective-permute-start | bytes 1966088 | tf_op jit(solution)/shard_map/ppermute | solution.py:216
  22.1 57.3 %collective-permute-start.6 = (bf16[128,2560]{1,0:T(8,128)(2,1)S(1)}, bf16[128,2560]{1,0:T(8,128)(2,1)S(1)}, u32[]{:S(2)}, u32[]{:S(2)}) collective-permute-start(bf16[128,2560]{1,0:T(8,128)(2,1)S(1)} %collective-permute-done.refs_4_), channel_id=1, source_target_pairs={{0,4},{6,2},{8,12},{14,10},{1,5},{7,3},{9,13},{15,11},{16,20},{22,... | collective-permute-start | bytes 1966088 | tf_op jit(solution)/shard_map/ppermute | solution.py:216
  30.9 50.8 %collective-permute-start.2 = (bf16[128,2560]{1,0:T(8,128)(2,1)}, bf16[128,2560]{1,0:T(8,128)(2,1)S(1)}, u32[]{:S(2)}, u32[]{:S(2)}) collective-permute-start(bf16[128,2560]{1,0:T(8,128)(2,1)} %collective-permute-done.1.refs_2_), channel_id=1, source_target_pairs={{0,4},{6,2},{8,12},{14,10},{1,5},{7,3},{9,13},{15,11},{16,20},{22,... | collective-permute-start | bytes 1966088 | tf_op jit(solution)/shard_map/ppermute | solution.py:216
  32.2 0.8 copy-start.9
  33.0 52.0 %collective-permute-start.9 = (bf16[128,2560]{1,0:T(8,128)(2,1)S(1)}, bf16[128,2560]{1,0:T(8,128)(2,1)S(1)}, u32[]{:S(2)}, u32[]{:S(2)}) collective-permute-start(bf16[128,2560]{1,0:T(8,128)(2,1)S(1)} %collective-permute-done.refs_4_), channel_id=1, source_target_pairs={{0,1},{1,0},{2,3},{3,2},{4,5},{5,4},{6,7},{7,6},{8,9},{9,8},{10,11... | collective-permute-start | bytes 1966088 | tf_op jit(solution)/shard_map/ppermute | solution.py:221
  35.4 0.8 copy-start.1
  64.7 33.9 %collective-permute-start.8 = (bf16[128,2560]{1,0:T(8,128)(2,1)}, bf16[128,2560]{1,0:T(8,128)(2,1)}, u32[]{:S(2)}, u32[]{:S(2)}) collective-permute-start(bf16[128,2560]{1,0:T(8,128)(2,1)} %collective-permute-done.1.refs_2_), channel_id=1, source_target_pairs={{0,1},{1,0},{2,3},{3,2},{4,5},{5,4},{6,7},{7,6},{8,9},{9,8},{10,11... | collective-permute-start | bytes 1966088 | tf_op jit(solution)/shard_map/ppermute | solution.py:221
  78.9 23.7 %collective-permute-start.5 = (bf16[128,2560]{1,0:T(8,128)(2,1)S(1)}, bf16[128,2560]{1,0:T(8,128)(2,1)S(1)}, u32[]{:S(2)}, u32[]{:S(2)}) collective-permute-start(bf16[128,2560]{1,0:T(8,128)(2,1)S(1)} %collective-permute-done.4.refs_4_), channel_id=1, source_target_pairs={{0,1},{1,0},{2,3},{3,2},{4,5},{5,4},{6,7},{7,6},{8,9},{9,8},{10,11... | collective-permute-start | bytes 1966088 | tf_op jit(solution)/shard_map/ppermute | solution.py:221
  79.4 23.2 %collective-permute-start.7 = (bf16[128,2560]{1,0:T(8,128)(2,1)S(1)}, bf16[128,2560]{1,0:T(8,128)(2,1)S(1)}, u32[]{:S(2)}, u32[]{:S(2)}) collective-permute-start(bf16[128,2560]{1,0:T(8,128)(2,1)S(1)} %collective-permute-done.6.refs_6_), channel_id=1, source_target_pairs={{2,3},{3,2},{4,5},{5,4},{10,11},{11,10},{12,13},{13,12},{18,19},{1... | collective-permute-start | bytes 1966088 | tf_op jit(solution)/shard_map/ppermute | solution.py:221
  81.7 20.9 %collective-permute-start.3 = (bf16[128,2560]{1,0:T(8,128)(2,1)S(1)}, bf16[128,2560]{1,0:T(8,128)(2,1)}, u32[]{:S(2)}, u32[]{:S(2)}) collective-permute-start(bf16[128,2560]{1,0:T(8,128)(2,1)S(1)} %collective-permute-done.2.refs_2_), channel_id=1, source_target_pairs={{2,3},{3,2},{4,5},{5,4},{10,11},{11,10},{12,13},{13,12},{18,19},{1... | collective-permute-start | bytes 1966088 | tf_op jit(solution)/shard_map/ppermute | solution.py:221
  85.1 0.9 copy-start.3
  85.9 21.6 %collective-permute-start.13 = (bf16[128,2560]{1,0:T(8,128)(2,1)}, bf16[128,2560]{1,0:T(8,128)(2,1)}, u32[]{:S(2)}, u32[]{:S(2)}) collective-permute-start(bf16[128,2560]{1,0:T(8,128)(2,1)} %collective-permute-done.12.refs_2_), channel_id=1, source_target_pairs={{0,1},{1,0},{2,3},{3,2},{4,5},{5,4},{6,7},{7,6},{8,9},{9,8},{10,11... | collective-permute-start | bytes 1966088 | tf_op jit(solution)/shard_map/ppermute | solution.py:221
  90.7 1.1 copy-start
  91.8 1.1 copy-start.5
  92.9 1.1 copy-start.6
  93.9 1.1 copy-start.8
  95.0 1.1 copy-start.10
  96.1 2.5 %copy-start.2 = (bf16[128,2560]{1,0:T(8,128)(2,1)S(1)}, bf16[128,2560]{1,0:T(8,128)(2,1)}, u32[]{:S(2)}) copy-start(bf16[128,2560]{1,0:T(8,128)(2,1)} %copy-done.1) | copy-start | bytes 1966084
  96.1 2.5 %copy-start.4 = (bf16[128,2560]{1,0:T(8,128)(2,1)S(1)}, bf16[128,2560]{1,0:T(8,128)(2,1)}, u32[]{:S(2)}) copy-start(bf16[128,2560]{1,0:T(8,128)(2,1)} %copy-done.3) | copy-start | bytes 1966084
  (1 other events, 0.8 us)

commit v6 on v5

--- a/solution.py
+++ b/solution.py
@@ -18,7 +18,8 @@
 
 
 def plan(rows):
-    near, relay, far = ({}, {}), ({}, {}), [({}, {}), ({}, {})]
+    near, relay, cross = ({}, {}), ({}, {}), ({}, {})
+    far = [({}, {}), ({}, {})]
     for row in range(rows):
         other = row ^ 1
         if other < rows:
@@ -28,13 +29,14 @@
         if row % TILE_H in (1, 2) and start + TILE_H <= rows:
             other = 2 * start + 3 - row
             relay[0][other ^ 1] = row
-            relay[1][row] = OFFSETS.index(other - row)
+            cross[0][other] = row
+            relay[1][row] = cross[1][row] = OFFSETS.index(other - row)
         for way in (0, 1):
             other = row + TILE_H if (row // TILE_H) % 2 == way else row - TILE_H
             if 0 <= other < rows:
                 far[way][0][other] = row
                 far[way][1][row] = OFFSETS.index(other - row)
-    return near, relay, [pair for pair in far if pair[0]]
+    return near, relay, cross, [pair for pair in far if pair[0]]
 
 
 def lanes(value):
@@ -210,7 +212,7 @@
     rows = lax.axis_size("row")
     cols = lax.axis_size("col")
     row = lax.axis_index("row")
-    near, relay, far = routes
+    near, relay, cross, far = routes
 
     def moved(value, route):
         return lax.ppermute(value, "row", sorted(route[0].items()))
@@ -231,17 +233,18 @@
 
     v_near = moved(values, near)
     k_far = [moved(keys, route) for route in far]
-    v_far = [moved(values, route) for route in far]
     k_own, v_own = paired(keys, None), paired(values, None)
     k_near = moved(after(keys, v_near), near)
     v_relay = moved(v_near, relay)
-    k_relay = moved(k_near, relay)
+    v_again = after(values, v_near)
+    v_far = [moved(v_again, route) for route in far]
+    k_cross = moved(after(keys, k_near), cross)
 
     carried = attend(None, queries, [k_own], [v_own], None, True)
     carried = attend(
         biases(near), queries, [paired(k_near, near)], [paired(v_near, near)], carried, True
     )
-    k_pairs = [paired(k_relay, relay)]
+    k_pairs = [paired(k_cross, cross)]
     k_pairs += [paired(k, route) for k, route in zip(k_far, far)]
     base, *weights = attend(
         biases(relay, *far), queries, k_pairs, [paired(v_relay, relay)], carried, False

time: 111 us -> 105 us (0.946)
  the two profiles are of different devices: /device:TPU:25 before, /device:TPU:0 now
where the time goes in v6:
time: 105 us
  waiting for transfers between devices  59.6 us (57%)
  starting transfers between devices  17.3 us (16%)
  Pallas kernels  14.1 us (13%)
  local copies, waits for them, and re-layouts  10.8 us (10%)
  other arithmetic  2.2 us (2%)
    ppermute x6, waiting for transfers between devices, moved(): return lax.ppermute(value, 'row', sorted(route[0].items()))  59.5 us
    pallas_call x4, Pallas kernels, call(): return list(run(*scalars, *operands))  14.1 us
    ppermute x6, starting transfers between devices, moved(): return lax.ppermute(value, 'row', sorted(route[0].items()))  14.1 us
    unnamed x22, local copies, waits for them, and re-layouts  8.78 us
    ppermute x8, starting transfers between devices, paired(): return (value, lax.ppermute(value, ('row', 'col'), pairs))  3.21 us
    reduce_sum x2, other arithmetic, biases(): live = jnp.sum(jnp.where(here, own_row, 0), axis=1)  2.19 us
  transfers between devices with their start and end apart: 14, of which 4 were waited for; matrix products, arithmetic and copies ran while one was open for 4% of the time, Pallas kernels for 11%

profile of v6, /device:TPU:0, one launch (start us, length us, event | category | flops | bytes accessed | tf_op | source)
XLA Modules:
  0.0 104.7 jit_solution(10894893042896053615)
XLA Ops:
  0.0 3.0 %collective-permute-start = (bf16[128,2560]{1,0:T(8,128)(2,1)}, bf16[128,2560]{1,0:T(8,128)(2,1)S(1)}, u32[]{:S(2)}, u32[]{:S(2)}) collective-permute-start(bf16[128,2560]{1,0:T(8,128)(2,1)} %refs_3_.1), channel_id=1, source_target_pairs={{0,2},{2,0},{4,6},{6,4},{8,10},{10,8},{12,14},{14,12},{1,3},{3,1},... | collective-permute-start | bytes 1966088 | tf_op jit(solution)/shard_map/ppermute | solution.py:218
  3.0 14.9 %collective-permute-done.refs_4_ = bf16[128,2560]{1,0:T(8,128)(2,1)S(1)} collective-permute-done((bf16[128,2560]{1,0:T(8,128)(2,1)}, bf16[128,2560]{1,0:T(8,128)(2,1)S(1)}, u32[]{:S(2)}, u32[]{:S(2)}) %collective-permute-start) | collective-permute-done | bytes 655392 | tf_op jit(solution)/shard_map/ppermute | solution.py:218
  17.9 1.7 %collective-permute-start.1 = (bf16[128,2560]{1,0:T(8,128)(2,1)}, bf16[128,2560]{1,0:T(8,128)(2,1)}, u32[]{:S(2)}, u32[]{:S(2)}) collective-permute-start(bf16[128,2560]{1,0:T(8,128)(2,1)} %refs_1_.3), channel_id=1, source_target_pairs={{0,2},{2,0},{4,6},{6,4},{8,10},{10,8},{12,14},{14,12},{1,3},{3,1},... | collective-permute-start | bytes 1966088 | tf_op jit(solution)/shard_map/ppermute | solution.py:218
  20.2 2.6 %collective-permute-start.4 = (bf16[128,2560]{1,0:T(8,128)(2,1)}, bf16[128,2560]{1,0:T(8,128)(2,1)S(1)}, u32[]{:S(2)}, u32[]{:S(2)}) collective-permute-start(bf16[128,2560]{1,0:T(8,128)(2,1)} %refs_1_.3), channel_id=1, source_target_pairs={{0,8},{2,10},{4,12},{6,14},{8,0},{10,2},{12,4},{14,6},{1,9},{3,11}... | collective-permute-start | bytes 1966088 | tf_op jit(solution)/shard_map/ppermute | solution.py:218
  22.8 11.4 %collective-permute-done.1.refs_2_ = bf16[128,2560]{1,0:T(8,128)(2,1)} collective-permute-done((bf16[128,2560]{1,0:T(8,128)(2,1)}, bf16[128,2560]{1,0:T(8,128)(2,1)}, u32[]{:S(2)}, u32[]{:S(2)}) %collective-permute-start.1) | collective-permute-done | bytes 655392 | tf_op jit(solution)/shard_map/ppermute | solution.py:218
  34.1 3.5 %collective-permute-start.6 = (bf16[128,2560]{1,0:T(8,128)(2,1)S(1)}, bf16[128,2560]{1,0:T(8,128)(2,1)S(1)}, u32[]{:S(2)}, u32[]{:S(2)}) collective-permute-start(bf16[128,2560]{1,0:T(8,128)(2,1)S(1)} %collective-permute-done.refs_4_), channel_id=1, source_target_pairs={{0,4},{6,2},{8,12},{14,10},{1,5},{7,3},{9,13},{15,11},{16,20},{22,... | collective-permute-start | bytes 1966088 | tf_op jit(solution)/shard_map/ppermute | solution.py:218
  38.5 0.8 copy-done.7
  40.0 0.8 copy-done.9
  40.8 2.6 %collective-permute-start.12 = (bf16[128,2560]{1,0:T(8,128)(2,1)}, bf16[128,2560]{1,0:T(8,128)(2,1)}, u32[]{:S(2)}, u32[]{:S(2)}) collective-permute-start(bf16[128,2560]{1,0:T(8,128)(2,1)} %refs_3_.1), channel_id=1, source_target_pairs={{0,8},{2,10},{4,12},{6,14},{8,0},{10,2},{12,4},{14,6},{1,9},{3,11}... | collective-permute-start | bytes 1966088 | tf_op jit(solution)/shard_map/ppermute | solution.py:218
  43.4 9.6 %collective-permute-done.4.refs_4_ = bf16[128,2560]{1,0:T(8,128)(2,1)S(1)} collective-permute-done((bf16[128,2560]{1,0:T(8,128)(2,1)}, bf16[128,2560]{1,0:T(8,128)(2,1)S(1)}, u32[]{:S(2)}, u32[]{:S(2)}) %collective-permute-start.4) | collective-permute-done | bytes 655392 | tf_op jit(solution)/shard_map/ppermute | solution.py:218
  53.1 0.8 copy-done.3
  55.1 1.5 %collective-permute-start.3 = (bf16[128,2560]{1,0:T(8,128)(2,1)S(1)}, bf16[128,2560]{1,0:T(8,128)(2,1)}, u32[]{:S(2)}, u32[]{:S(2)}) collective-permute-start(bf16[128,2560]{1,0:T(8,128)(2,1)S(1)} %collective-permute-done.2.refs_2_), channel_id=1, source_target_pairs={{2,3},{3,2},{4,5},{5,4},{10,11},{11,10},{12,13},{13,12},{18,19},{1... | collective-permute-start | bytes 1966088 | tf_op jit(solution)/shard_map/ppermute | solution.py:223
  56.6 23.6 %collective-permute-done.12.refs_2_ = bf16[128,2560]{1,0:T(8,128)(2,1)} collective-permute-done((bf16[128,2560]{1,0:T(8,128)(2,1)}, bf16[128,2560]{1,0:T(8,128)(2,1)}, u32[]{:S(2)}, u32[]{:S(2)}) %collective-permute-start.12) | collective-permute-done | bytes 655392 | tf_op jit(solution)/shard_map/ppermute | solution.py:218
  80.2 1.3 %constant_dynamic-slice_fusion = s32[1,1]{1,0:T(1,128)} fusion(s32[8,1]{1,0:T(8,128)} %constant.30.clone, s32[]{:T(128)S(6)} %select_n.24), kind=kLoop, calls=%fused_computation.4 | loop fusion | bytes 12 | tf_op jit(solution)/shard_map/dynamic_slice | solution.py:229
  81.5 2.0 %fusion.2 = (s32[]{:T(128)}, s32[5]{0:T(128)S(1)}) fusion(s32[]{:T(128)} %bitcast.2, s32[8,5]{1,0:T(8,128)} %param.9, s32[]{:T(128)S(6)} %select_n.24), kind=kLoop, calls=%fused_computation.8 | loop fusion | flops 14 | bytes 52 | tf_op jit(solution)/shard_map/reduce_sum | solution.py:231
  85.0 1.1 %copy-done = bf16[128,2560]{1,0:T(8,128)(2,1)S(1)} copy-done((bf16[128,2560]{1,0:T(8,128)(2,1)S(1)}, bf16[128,2560]{1,0:T(8,128)(2,1)}, u32[]{:S(2)}) %copy-start) | copy-done | bytes 655384
  86.1 1.1 %copy-done.5 = bf16[128,2560]{1,0:T(8,128)(2,1)S(1)} copy-done((bf16[128,2560]{1,0:T(8,128)(2,1)S(1)}, bf16[128,2560]{1,0:T(8,128)(2,1)}, u32[]{:S(2)}) %copy-start.5) | copy-done | bytes 655384
  87.2 1.1 %copy-done.6 = bf16[128,2560]{1,0:T(8,128)(2,1)S(1)} copy-done((bf16[128,2560]{1,0:T(8,128)(2,1)S(1)}, bf16[128,2560]{1,0:T(8,128)(2,1)}, u32[]{:S(2)}) %copy-start.6) | copy-done | bytes 655384
  88.2 1.1 %copy-done.8 = bf16[128,2560]{1,0:T(8,128)(2,1)S(1)} copy-done((bf16[128,2560]{1,0:T(8,128)(2,1)S(1)}, bf16[128,2560]{1,0:T(8,128)(2,1)}, u32[]{:S(2)}) %copy-start.8) | copy-done | bytes 655384
  89.3 1.1 %copy-done.10 = bf16[128,2560]{1,0:T(8,128)(2,1)S(1)} copy-done((bf16[128,2560]{1,0:T(8,128)(2,1)S(1)}, bf16[128,2560]{1,0:T(8,128)(2,1)}, u32[]{:S(2)}) %copy-start.10) | copy-done | bytes 655384
  90.4 2.5 %shard_map.64 = (f32[128,2560]{1,0:T(8,128)S(1)}, f32[128,2560]{1,0:T(8,128)S(1)}) custom-call(bf16[128,2560]{1,0:T(8,128)(2,1)S(1)} %copy-done, bf16[128,2560]{1,0:T(8,128)(2,1)S(1)} %copy-done.5, bf16[128,2560]{1,0:T(8,128)(2,1)S(1)} %copy-done.8, bf16[128,2560]{1,0:T(8,128)(2,1)S(1)} %copy-done.6, bf16[128,2560]{1,0:T(8,128)(2,1)S(1)} %copy-done.10), custom_call_target="tpu_custom_call" | custom-call | flops 335544320 | bytes 5898240 | tf_op jit(solution)/shard_map/pallas_call | solution.py:174
  92.9 3.9 %shard_map.65 = (f32[128,2560]{1,0:T(8,128)S(1)}, f32[128,2560]{1,0:T(8,128)S(1)}) custom-call(f32[1]{0:T(128)} %bitcast.3.refs_0_, bf16[128,2560]{1,0:T(8,128)(2,1)S(1)} %copy-done, bf16[128,2560]{1,0:T(8,128)(2,1)} %collective-permute-done.1.refs_2_, bf16[128,2560]{1,0:T(8,128)(2,1)} %collective-permute-done.8.refs_3_, bf16[128,2560]{1,0:T(8,128)(2,1)S(1)} %copy-done.2, ...), custom_call_target="tpu_custom_call" | custom-call | flops 335544320 | bytes 8519680 | tf_op jit(solution)/shard_map/pallas_call | solution.py:174
  96.9 4.9 %shard_map.66 = (f32[128,2560]{1,0:T(8,128)S(1)}, bf16[128,5120]{1,0:T(8,128)(2,1)S(1)}) custom-call(f32[2]{0:T(128)S(1)} %compare_select_fusion.1.refs_0_, bf16[128,2560]{1,0:T(8,128)(2,1)S(1)} %copy-done, bf16[128,2560]{1,0:T(8,128)(2,1)S(1)} %collective-permute-done.2.refs_2_, bf16[128,2560]{1,0:T(8,128)(2,1)} %collective-permute-done.3.refs_3_, ...), custom_call_target="tpu_custom_call" | custom-call | flops 671088640 | bytes 9830400 | tf_op jit(solution)/shard_map/pallas_call | solution.py:174
  101.9 2.8 %shard_map.67 = bf16[128,2560]{1,0:T(8,128)(2,1)} custom-call(f32[128,2560]{1,0:T(8,128)S(1)} %get-tuple-element.20.refs_0_, bf16[128,5120]{1,0:T(8,128)(2,1)S(1)} %get-tuple-element.21.refs_1_, bf16[128,2560]{1,0:T(8,128)(2,1)} %collective-permute-done.12.refs_2_, bf16[128,2560]{1,0:T(8,128)(2,1)} %collective-permute-done.13.refs_3_), custom_call_target="tpu_custom_call" | custom-call | flops 167772160 | bytes 4587520 | tf_op jit(solution)/shard_map/pallas_call | solution.py:174
  (35 shorter events, 4.2 us)
Async XLA Ops:
  0.0 17.9 %collective-permute-start = (bf16[128,2560]{1,0:T(8,128)(2,1)}, bf16[128,2560]{1,0:T(8,128)(2,1)S(1)}, u32[]{:S(2)}, u32[]{:S(2)}) collective-permute-start(bf16[128,2560]{1,0:T(8,128)(2,1)} %refs_3_.1), channel_id=1, source_target_pairs={{0,2},{2,0},{4,6},{6,4},{8,10},{10,8},{12,14},{14,12},{1,3},{3,1},... | collective-permute-start | bytes 1966088 | tf_op jit(solution)/shard_map/ppermute | solution.py:218
  17.9 16.2 %collective-permute-start.1 = (bf16[128,2560]{1,0:T(8,128)(2,1)}, bf16[128,2560]{1,0:T(8,128)(2,1)}, u32[]{:S(2)}, u32[]{:S(2)}) collective-permute-start(bf16[128,2560]{1,0:T(8,128)(2,1)} %refs_1_.3), channel_id=1, source_target_pairs={{0,2},{2,0},{4,6},{6,4},{8,10},{10,8},{12,14},{14,12},{1,3},{3,1},... | collective-permute-start | bytes 1966088 | tf_op jit(solution)/shard_map/ppermute | solution.py:218
  19.7 18.8 %collective-permute-start.10 = (bf16[128,2560]{1,0:T(8,128)(2,1)}, bf16[128,2560]{1,0:T(8,128)(2,1)S(1)}, u32[]{:S(2)}, u32[]{:S(2)}) collective-permute-start(bf16[128,2560]{1,0:T(8,128)(2,1)} %refs_1_.3), channel_id=1, source_target_pairs={{0,1},{1,0},{2,3},{3,2},{4,5},{5,4},{6,7},{7,6},{8,9},{9,8},{10,11... | collective-permute-start | bytes 1966088 | tf_op jit(solution)/shard_map/ppermute | solution.py:223
  19.7 20.3 %collective-permute-start.11 = (bf16[128,2560]{1,0:T(8,128)(2,1)}, bf16[128,2560]{1,0:T(8,128)(2,1)S(1)}, u32[]{:S(2)}, u32[]{:S(2)}) collective-permute-start(bf16[128,2560]{1,0:T(8,128)(2,1)} %refs_3_.1), channel_id=1, source_target_pairs={{0,1},{1,0},{2,3},{3,2},{4,5},{5,4},{6,7},{7,6},{8,9},{9,8},{10,11... | collective-permute-start | bytes 1966088 | tf_op jit(solution)/shard_map/ppermute | solution.py:223
  20.2 32.9 %collective-permute-start.4 = (bf16[128,2560]{1,0:T(8,128)(2,1)}, bf16[128,2560]{1,0:T(8,128)(2,1)S(1)}, u32[]{:S(2)}, u32[]{:S(2)}) collective-permute-start(bf16[128,2560]{1,0:T(8,128)(2,1)} %refs_1_.3), channel_id=1, source_target_pairs={{0,8},{2,10},{4,12},{6,14},{8,0},{10,2},{12,4},{14,6},{1,9},{3,11}... | collective-permute-start | bytes 1966088 | tf_op jit(solution)/shard_map/ppermute | solution.py:218
  22.8 30.3 %collective-permute-start.9 = (bf16[128,2560]{1,0:T(8,128)(2,1)S(1)}, bf16[128,2560]{1,0:T(8,128)(2,1)S(1)}, u32[]{:S(2)}, u32[]{:S(2)}) collective-permute-start(bf16[128,2560]{1,0:T(8,128)(2,1)S(1)} %collective-permute-done.refs_4_), channel_id=1, source_target_pairs={{0,1},{1,0},{2,3},{3,2},{4,5},{5,4},{6,7},{7,6},{8,9},{9,8},{10,11... | collective-permute-start | bytes 1966088 | tf_op jit(solution)/shard_map/ppermute | solution.py:223
  34.1 20.3 %collective-permute-start.6 = (bf16[128,2560]{1,0:T(8,128)(2,1)S(1)}, bf16[128,2560]{1,0:T(8,128)(2,1)S(1)}, u32[]{:S(2)}, u32[]{:S(2)}) collective-permute-start(bf16[128,2560]{1,0:T(8,128)(2,1)S(1)} %collective-permute-done.refs_4_), channel_id=1, source_target_pairs={{0,4},{6,2},{8,12},{14,10},{1,5},{7,3},{9,13},{15,11},{16,20},{22,... | collective-permute-start | bytes 1966088 | tf_op jit(solution)/shard_map/ppermute | solution.py:218
  37.6 0.8 copy-start.1
  39.3 15.8 %collective-permute-start.2 = (bf16[128,2560]{1,0:T(8,128)(2,1)}, bf16[128,2560]{1,0:T(8,128)(2,1)S(1)}, u32[]{:S(2)}, u32[]{:S(2)}) collective-permute-start(bf16[128,2560]{1,0:T(8,128)(2,1)} %refs_1_.3), channel_id=1, source_target_pairs={{2,4},{4,2},{10,12},{12,10},{3,5},{5,3},{11,13},{13,11},{18,20},{2... | collective-permute-start | bytes 1966088 | tf_op jit(solution)/shard_map/ppermute | solution.py:218
  40.0 0.8 copy-start.9
  40.8 39.4 %collective-permute-start.12 = (bf16[128,2560]{1,0:T(8,128)(2,1)}, bf16[128,2560]{1,0:T(8,128)(2,1)}, u32[]{:S(2)}, u32[]{:S(2)}) collective-permute-start(bf16[128,2560]{1,0:T(8,128)(2,1)} %refs_3_.1), channel_id=1, source_target_pairs={{0,8},{2,10},{4,12},{6,14},{8,0},{10,2},{12,4},{14,6},{1,9},{3,11}... | collective-permute-start | bytes 1966088 | tf_op jit(solution)/shard_map/ppermute | solution.py:218
  53.0 39.9 %collective-permute-start.8 = (bf16[128,2560]{1,0:T(8,128)(2,1)}, bf16[128,2560]{1,0:T(8,128)(2,1)}, u32[]{:S(2)}, u32[]{:S(2)}) collective-permute-start(bf16[128,2560]{1,0:T(8,128)(2,1)} %collective-permute-done.1.refs_2_), channel_id=1, source_target_pairs={{0,1},{1,0},{2,3},{3,2},{4,5},{5,4},{6,7},{7,6},{8,9},{9,8},{10,11... | collective-permute-start | bytes 1966088 | tf_op jit(solution)/shard_map/ppermute | solution.py:223
  53.1 0.9 copy-start.3
  53.9 43.0 %collective-permute-start.5 = (bf16[128,2560]{1,0:T(8,128)(2,1)S(1)}, bf16[128,2560]{1,0:T(8,128)(2,1)S(1)}, u32[]{:S(2)}, u32[]{:S(2)}) collective-permute-start(bf16[128,2560]{1,0:T(8,128)(2,1)S(1)} %collective-permute-done.4.refs_4_), channel_id=1, source_target_pairs={{0,1},{1,0},{2,3},{3,2},{4,5},{5,4},{6,7},{7,6},{8,9},{9,8},{10,11... | collective-permute-start | bytes 1966088 | tf_op jit(solution)/shard_map/ppermute | solution.py:223
  54.4 42.5 %collective-permute-start.7 = (bf16[128,2560]{1,0:T(8,128)(2,1)S(1)}, bf16[128,2560]{1,0:T(8,128)(2,1)S(1)}, u32[]{:S(2)}, u32[]{:S(2)}) collective-permute-start(bf16[128,2560]{1,0:T(8,128)(2,1)S(1)} %collective-permute-done.6.refs_6_), channel_id=1, source_target_pairs={{2,3},{3,2},{4,5},{5,4},{10,11},{11,10},{12,13},{13,12},{18,19},{1... | collective-permute-start | bytes 1966088 | tf_op jit(solution)/shard_map/ppermute | solution.py:223
  55.1 41.8 %collective-permute-start.3 = (bf16[128,2560]{1,0:T(8,128)(2,1)S(1)}, bf16[128,2560]{1,0:T(8,128)(2,1)}, u32[]{:S(2)}, u32[]{:S(2)}) collective-permute-start(bf16[128,2560]{1,0:T(8,128)(2,1)S(1)} %collective-permute-done.2.refs_2_), channel_id=1, source_target_pairs={{2,3},{3,2},{4,5},{5,4},{10,11},{11,10},{12,13},{13,12},{18,19},{1... | collective-permute-start | bytes 1966088 | tf_op jit(solution)/shard_map/ppermute | solution.py:223
  80.2 21.6 %collective-permute-start.13 = (bf16[128,2560]{1,0:T(8,128)(2,1)}, bf16[128,2560]{1,0:T(8,128)(2,1)}, u32[]{:S(2)}, u32[]{:S(2)}) collective-permute-start(bf16[128,2560]{1,0:T(8,128)(2,1)} %collective-permute-done.12.refs_2_), channel_id=1, source_target_pairs={{0,1},{1,0},{2,3},{3,2},{4,5},{5,4},{6,7},{7,6},{8,9},{9,8},{10,11... | collective-permute-start | bytes 1966088 | tf_op jit(solution)/shard_map/ppermute | solution.py:223
  85.0 1.1 %copy-start = (bf16[128,2560]{1,0:T(8,128)(2,1)S(1)}, bf16[128,2560]{1,0:T(8,128)(2,1)}, u32[]{:S(2)}) copy-start(bf16[128,2560]{1,0:T(8,128)(2,1)} %refs_1_.5) | copy-start | bytes 1966084
  86.1 1.1 %copy-start.5 = (bf16[128,2560]{1,0:T(8,128)(2,1)S(1)}, bf16[128,2560]{1,0:T(8,128)(2,1)}, u32[]{:S(2)}) copy-start(bf16[128,2560]{1,0:T(8,128)(2,1)} %refs_1_.3) | copy-start | bytes 1966084
  87.2 1.1 %copy-start.6 = (bf16[128,2560]{1,0:T(8,128)(2,1)S(1)}, bf16[128,2560]{1,0:T(8,128)(2,1)}, u32[]{:S(2)}) copy-start(bf16[128,2560]{1,0:T(8,128)(2,1)} %refs_3_.1) | copy-start | bytes 1966084
  88.2 1.1 %copy-start.8 = (bf16[128,2560]{1,0:T(8,128)(2,1)S(1)}, bf16[128,2560]{1,0:T(8,128)(2,1)}, u32[]{:S(2)}) copy-start(bf16[128,2560]{1,0:T(8,128)(2,1)} %copy-done.7) | copy-start | bytes 1966084
  89.3 1.1 %copy-start.10 = (bf16[128,2560]{1,0:T(8,128)(2,1)S(1)}, bf16[128,2560]{1,0:T(8,128)(2,1)}, u32[]{:S(2)}) copy-start(bf16[128,2560]{1,0:T(8,128)(2,1)} %copy-done.9) | copy-start | bytes 1966084
  90.4 2.5 %copy-start.2 = (bf16[128,2560]{1,0:T(8,128)(2,1)S(1)}, bf16[128,2560]{1,0:T(8,128)(2,1)}, u32[]{:S(2)}) copy-start(bf16[128,2560]{1,0:T(8,128)(2,1)} %copy-done.1) | copy-start | bytes 1966084
  90.4 2.5 %copy-start.4 = (bf16[128,2560]{1,0:T(8,128)(2,1)S(1)}, bf16[128,2560]{1,0:T(8,128)(2,1)}, u32[]{:S(2)}) copy-start(bf16[128,2560]{1,0:T(8,128)(2,1)} %copy-done.3) | copy-start | bytes 1966084
  (1 other events, 0.8 us)

commit v7 on v6

--- a/solution.py
+++ b/solution.py
@@ -19,7 +19,7 @@
 
 def plan(rows):
     near, relay, cross = ({}, {}), ({}, {}), ({}, {})
-    far = [({}, {}), ({}, {})]
+    far = [({}, {}, {}), ({}, {}, {})]
     for row in range(rows):
         other = row ^ 1
         if other < rows:
@@ -34,9 +34,9 @@
         for way in (0, 1):
             other = row + TILE_H if (row // TILE_H) % 2 == way else row - TILE_H
             if 0 <= other < rows:
-                far[way][0][other] = row
-                far[way][1][row] = OFFSETS.index(other - row)
-    return near, relay, cross, [pair for pair in far if pair[0]]
+                far[way][0 if row % TILE_H >= TILE_H // 2 else 1][other] = row
+                far[way][2][row] = OFFSETS.index(other - row)
+    return near, relay, cross, [way for way in far if way[2]]
 
 
 def lanes(value):
@@ -48,26 +48,38 @@
     return jnp.broadcast_to(found, slices[0].shape)
 
 
-def attend_chunk(heads, merging, mixed, held, bias_ref, refs, score_ref, weight_ref):
-    refs = list(refs)
-    blocks = mixed + held
-    q_ref = refs.pop(0)
-    k_refs, refs = refs[: 2 * blocks], refs[2 * blocks :]
-    v_refs, refs = refs[: 2 * mixed], refs[2 * mixed :]
+def take(refs, pairs):
+    found, refs = [], list(refs)
+    for pair in pairs:
+        found.append([[refs.pop(0) for _ in half] for half in pair])
+    return found, refs
+
+
+def gathered(pair, here):
+    return jnp.concatenate(
+        [functools.reduce(jnp.add, [ref[:, here] for ref in half]) for half in pair], axis=0
+    )
+
+
+def attend_chunk(heads, merging, k_pairs, v_pairs, bias_ref, refs, score_ref, weight_ref):
+    blocks, mixed = len(k_pairs), len(v_pairs)
+    held = blocks - mixed
+    q_ref, *refs = refs
+    k_refs, refs = take(refs, k_pairs)
+    v_refs, refs = take(refs, v_pairs)
     if merging:
         before_ref, stat_ref, *refs = refs
     out_ref, *refs = refs
     held_refs, refs = refs[:held], refs[held:]
     total_ref = refs[0] if refs else None
-    keys_each = 2 * k_refs[0].shape[0]
+    keys_each = 2 * k_refs[0][0][0].shape[0]
     each = keys_each // HD
     kept = {}
 
     def score(head, here):
         for n in range(blocks):
-            keys = jnp.concatenate([k_refs[2 * n][:, here], k_refs[2 * n + 1][:, here]], axis=0)
             found = lax.dot_general(
-                q_ref[:, here], keys, (((1,), (1,)), ((), ())), preferred_element_type=jnp.float32
+                q_ref[:, here], gathered(k_refs[n], here), (((1,), (1,)), ((), ())), preferred_element_type=jnp.float32
             )
             found = found * SCALE
             if merging:
@@ -102,7 +114,7 @@
         inverse, factor = kept.pop(head)
         out = jnp.dot(
             weight_ref[head],
-            jnp.concatenate([v[:, here] for v in v_refs], axis=0),
+            jnp.concatenate([gathered(pair, here) for pair in v_refs], axis=0),
             preferred_element_type=jnp.float32,
         )
         out = out * inverse
@@ -118,16 +130,17 @@
                 step(head, slice(head * HD, (head + 1) * HD))
 
 
-def finish_chunk(heads, blocks, refs):
-    base_ref, refs = refs[0], refs[1:]
-    weight_refs, v_refs, out_ref = refs[:blocks], refs[blocks : 3 * blocks], refs[-1]
-    keys_each = 2 * v_refs[0].shape[0]
+def finish_chunk(heads, v_pairs, refs):
+    base_ref, *refs = refs
+    weight_refs, refs = refs[: len(v_pairs)], refs[len(v_pairs) :]
+    v_refs, (out_ref,) = take(refs, v_pairs)
+    keys_each = 2 * v_refs[0][0][0].shape[0]
     for head in range(heads):
         here = slice(head * HD, (head + 1) * HD)
         weights = [w[:, head * keys_each : (head + 1) * keys_each] for w in weight_refs]
         out = jnp.dot(
             jnp.concatenate(weights, axis=1),
-            jnp.concatenate([v[:, here] for v in v_refs], axis=0),
+            jnp.concatenate([gathered(pair, here) for pair in v_refs], axis=0),
             preferred_element_type=jnp.float32,
         )
         out_ref[:, here] = (base_ref[:, here] + out).astype(out_ref.dtype)
@@ -180,11 +193,12 @@
     keys = 2 * tokens * len(k_pairs)
 
     def chunk(heads, scalar_refs, views, scratch_refs):
-        attend_chunk(heads, merging, mixed, held, *(scalar_refs or (None,)), views, *scratch_refs)
+        bias = scalar_refs[0] if merging else None
+        attend_chunk(heads, merging, k_pairs, v_pairs, bias, views, *scratch_refs)
 
     full = jax.ShapeDtypeStruct((tokens, width), jnp.float32)
     weight = jax.ShapeDtypeStruct((tokens, 2 * tokens * (width // HD)), jnp.bfloat16)
-    operands = [queries] + [a for p in k_pairs for a in p] + [a for p in v_pairs for a in p]
+    operands = [queries] + [a for p in k_pairs + v_pairs for half in p for a in half]
     operands += list(before) if merging else []
     outs = [full] + [weight] * held + ([full] if more else [])
     scratch = [((tokens, keys), jnp.float32), ((tokens, 2 * tokens * mixed), jnp.bfloat16)]
@@ -197,9 +211,9 @@
     blocks = len(v_pairs)
 
     def chunk(heads, scalar_refs, views, scratch_refs):
-        finish_chunk(heads, blocks, views)
-
-    operands = [base] + weights + [a for p in v_pairs for a in p]
+        finish_chunk(heads, v_pairs, views)
+
+    operands = [base] + weights + [a for p in v_pairs for half in p for a in half]
     outs = [jax.ShapeDtypeStruct((tokens, width), dtype)]
     return call(chunk, 10, [], operands, outs, [], 1, 2 * tokens * blocks)[0]
 
@@ -214,43 +228,58 @@
     row = lax.axis_index("row")
     near, relay, cross, far = routes
 
-    def moved(value, route):
-        return lax.ppermute(value, "row", sorted(route[0].items()))
-
-    def paired(value, route):
-        reached = range(rows) if route is None else sorted(route[1])
+    def moved(value, sends):
+        return lax.ppermute(value, "row", sorted(sends.items()))
+
+    def swapped(value, sends):
+        reached = range(rows) if sends is None else sorted(sends.values())
         pairs = [(r * cols + c, r * cols + cols - 1 - c) for r in reached for c in range(cols)]
-        return value, lax.ppermute(value, ("row", "col"), pairs)
+        return lax.ppermute(value, ("row", "col"), pairs)
+
+    def paired(value, sends):
+        return (value,), (swapped(value, sends),)
 
     own_row = lax.dynamic_index_in_dim(pattern, row, 0, keepdims=True)
 
     def biases(*given):
-        table = [[route[1].get(r, len(OFFSETS)) for route in given] for r in range(rows)]
+        table = [[route[-1].get(r, len(OFFSETS)) for route in given] for r in range(rows)]
         picks = jnp.asarray(table, jnp.int32)[row]
         here = jnp.arange(len(OFFSETS), dtype=jnp.int32)[None, :] == picks[:, None]
         live = jnp.sum(jnp.where(here, own_row, 0), axis=1)
         return jnp.where(live == 1, 0.0, FAR_BELOW).astype(jnp.float32)
 
-    v_near = moved(values, near)
-    k_far = [moved(keys, route) for route in far]
+    v_near = moved(values, near[0])
+    k_soon = [moved(keys, way[0]) for way in far]
+    v_soon = [moved(values, way[0]) for way in far]
+    k_near = moved(keys, near[0])
     k_own, v_own = paired(keys, None), paired(values, None)
-    k_near = moved(after(keys, v_near), near)
-    v_relay = moved(v_near, relay)
-    v_again = after(values, v_near)
-    v_far = [moved(v_again, route) for route in far]
-    k_cross = moved(after(keys, k_near), cross)
+    k_again, v_again = after(keys, v_near), after(values, v_near)
+    v_relay = moved(v_near, relay[0])
+    k_cross = moved(k_again, cross[0])
+    k_then = [moved(k_again, way[1]) for way in far]
+    v_then = [moved(v_again, way[1]) for way in far]
+
+    def joined(soon, then):
+        found = []
+        for n, way in enumerate(far):
+            other_soon = swapped(soon[n], way[0])
+            other_then = swapped(then[n], way[1])
+            found.append(((soon[n], then[n]), (other_soon, other_then)))
+        return found
 
     carried = attend(None, queries, [k_own], [v_own], None, True)
     carried = attend(
-        biases(near), queries, [paired(k_near, near)], [paired(v_near, near)], carried, True
-    )
-    k_pairs = [paired(k_cross, cross)]
-    k_pairs += [paired(k, route) for k, route in zip(k_far, far)]
+        biases(near), queries, [paired(k_near, near[0])], [paired(v_near, near[0])], carried, True
+    )
     base, *weights = attend(
-        biases(relay, *far), queries, k_pairs, [paired(v_relay, relay)], carried, False
-    )
-    v_pairs = [paired(v, route) for v, route in zip(v_far, far)]
-    return finish(base, weights, v_pairs, queries.dtype)
+        biases(relay, *far),
+        queries,
+        [paired(k_cross, cross[0])] + joined(k_soon, k_then),
+        [paired(v_relay, relay[0])],
+        carried,
+        False,
+    )
+    return finish(base, weights, joined(v_soon, v_then), queries.dtype)
 
 
 def solution(mesh):

time: 105 us -> 116 us (1.10)
  the two profiles are of different devices: /device:TPU:0 before, /device:TPU:5 now
where the time goes in v7:
time: 116 us; the launch traced here: 115 us
  waiting for transfers between devices  55 us (47%)
  starting transfers between devices  30.9 us (27%)
  Pallas kernels  13.7 us (12%)
  local copies, waits for them, and re-layouts  12.4 us (11%)
  other arithmetic  2.1 us (2%)
    ppermute x8, waiting for transfers between devices, moved(): return lax.ppermute(value, 'row', sorted(sends.items()))  55 us
    ppermute x10, starting transfers between devices, swapped(): return lax.ppermute(value, ('row', 'col'), pairs)  16.4 us
    ppermute x8, starting transfers between devices, moved(): return lax.ppermute(value, 'row', sorted(sends.items()))  14.5 us
    pallas_call x4, Pallas kernels, call(): return list(run(*scalars, *operands))  13.7 us
    unnamed x30, local copies, waits for them, and re-layouts  10.5 us
  transfers between devices with their start and end apart: 18, of which 3 were waited for; matrix products, arithmetic and copies ran while one was open for 3% of the time, Pallas kernels for 9%

profile of v7, /device:TPU:5, one launch (start us, length us, event | category | flops | bytes accessed | tf_op | source)
XLA Modules:
  0.0 114.9 jit_solution(9122232645655129798)
XLA Ops:
  0.7 1.7 %collective-permute-start.9 = (bf16[128,2560]{1,0:T(8,128)(2,1)}, bf16[128,2560]{1,0:T(8,128)(2,1)S(1)}, u32[]{:S(2)}, u32[]{:S(2)}) collective-permute-start(bf16[128,2560]{1,0:T(8,128)(2,1)} %refs_1_.3), channel_id=1, source_target_pairs={{0,2},{2,0},{4,6},{6,4},{8,10},{10,8},{12,14},{14,12},{1,3},{3,1},... | collective-permute-start | bytes 1966088 | tf_op jit(solution)/shard_map/ppermute | solution.py:232
  3.4 12.4 %collective-permute-done.refs_4_ = bf16[128,2560]{1,0:T(8,128)(2,1)S(1)} collective-permute-done((bf16[128,2560]{1,0:T(8,128)(2,1)}, bf16[128,2560]{1,0:T(8,128)(2,1)S(1)}, u32[]{:S(2)}, u32[]{:S(2)}) %collective-permute-start) | collective-permute-done | bytes 655392 | tf_op jit(solution)/shard_map/ppermute | solution.py:232
  15.8 1.5 %collective-permute-start.14 = (bf16[128,2560]{1,0:T(8,128)(2,1)}, bf16[128,2560]{1,0:T(8,128)(2,1)}, u32[]{:S(2)}, u32[]{:S(2)}) collective-permute-start(bf16[128,2560]{1,0:T(8,128)(2,1)} %refs_3_.1), channel_id=1, source_target_pairs={{4,12},{6,14},{12,4},{14,6},{5,13},{7,15},{13,5},{15,7},{20,28},{2... | collective-permute-start | bytes 1966088 | tf_op jit(solution)/shard_map/ppermute | solution.py:232
  18.2 2.7 %collective-permute-start.11 = (bf16[128,2560]{1,0:T(8,128)(2,1)S(1)}, bf16[128,2560]{1,0:T(8,128)(2,1)S(1)}, u32[]{:S(2)}, u32[]{:S(2)}) collective-permute-start(bf16[128,2560]{1,0:T(8,128)(2,1)S(1)} %collective-permute-done.refs_4_), channel_id=1, source_target_pairs={{0,1},{1,0},{2,3},{3,2},{4,5},{5,4},{6,7},{7,6},{8,9},{9,8},{10,11... | collective-permute-start | bytes 1966088 | tf_op jit(solution)/shard_map/ppermute | solution.py:237
  20.8 9.1 %collective-permute-done.9.refs_2_ = bf16[128,2560]{1,0:T(8,128)(2,1)S(1)} collective-permute-done((bf16[128,2560]{1,0:T(8,128)(2,1)}, bf16[128,2560]{1,0:T(8,128)(2,1)S(1)}, u32[]{:S(2)}, u32[]{:S(2)}) %collective-permute-start.9) | collective-permute-done | bytes 655392 | tf_op jit(solution)/shard_map/ppermute | solution.py:232
  29.9 1.5 %collective-permute-start.10 = (bf16[128,2560]{1,0:T(8,128)(2,1)S(1)}, bf16[128,2560]{1,0:T(8,128)(2,1)S(1)}, u32[]{:S(2)}, u32[]{:S(2)}) collective-permute-start(bf16[128,2560]{1,0:T(8,128)(2,1)S(1)} %collective-permute-done.9.refs_2_), channel_id=1, source_target_pairs={{0,1},{1,0},{2,3},{3,2},{4,5},{5,4},{6,7},{7,6},{8,9},{9,8},{10,11... | collective-permute-start | bytes 1966088 | tf_op jit(solution)/shard_map/ppermute | solution.py:237
  33.1 3.1 %collective-permute-start.1 = (bf16[128,2560]{1,0:T(8,128)(2,1)}, bf16[128,2560]{1,0:T(8,128)(2,1)S(1)}, u32[]{:S(2)}, u32[]{:S(2)}) collective-permute-start(bf16[128,2560]{1,0:T(8,128)(2,1)} %refs_1_.3), channel_id=1, source_target_pairs={{2,4},{4,2},{10,12},{12,10},{3,5},{5,3},{11,13},{13,11},{18,20},{2... | collective-permute-start | bytes 1966088 | tf_op jit(solution)/shard_map/ppermute | solution.py:232
  36.3 4.2 %collective-permute-start.4 = (bf16[128,2560]{1,0:T(8,128)(2,1)}, bf16[128,2560]{1,0:T(8,128)(2,1)S(1)}, u32[]{:S(2)}, u32[]{:S(2)}) collective-permute-start(bf16[128,2560]{1,0:T(8,128)(2,1)} %refs_1_.3), channel_id=1, source_target_pairs={{0,8},{2,10},{8,0},{10,2},{1,9},{3,11},{9,1},{11,3},{16,24},{18,26... | collective-permute-start | bytes 1966088 | tf_op jit(solution)/shard_map/ppermute | solution.py:232
  40.5 1.3 %collective-permute-start.7 = (bf16[128,2560]{1,0:T(8,128)(2,1)S(1)}, bf16[128,2560]{1,0:T(8,128)(2,1)S(1)}, u32[]{:S(2)}, u32[]{:S(2)}) collective-permute-start(bf16[128,2560]{1,0:T(8,128)(2,1)S(1)} %collective-permute-done.refs_4_), channel_id=1, source_target_pairs={{0,4},{6,2},{8,12},{14,10},{1,5},{7,3},{9,13},{15,11},{16,20},{22,... | collective-permute-start | bytes 1966088 | tf_op jit(solution)/shard_map/ppermute | solution.py:232
  45.0 2.0 %collective-permute-start.15 = (bf16[128,2560]{1,0:T(8,128)(2,1)}, bf16[128,2560]{1,0:T(8,128)(2,1)}, u32[]{:S(2)}, u32[]{:S(2)}) collective-permute-start(bf16[128,2560]{1,0:T(8,128)(2,1)} %refs_3_.1), channel_id=1, source_target_pairs={{0,8},{2,10},{8,0},{10,2},{1,9},{3,11},{9,1},{11,3},{16,24},{18,26... | collective-permute-start | bytes 1966088 | tf_op jit(solution)/shard_map/ppermute | solution.py:232
  47.0 33.5 %collective-permute-done.1.refs_2_ = bf16[128,2560]{1,0:T(8,128)(2,1)S(1)} collective-permute-done((bf16[128,2560]{1,0:T(8,128)(2,1)}, bf16[128,2560]{1,0:T(8,128)(2,1)S(1)}, u32[]{:S(2)}, u32[]{:S(2)}) %collective-permute-start.1) | collective-permute-done | bytes 655392 | tf_op jit(solution)/shard_map/ppermute | solution.py:232
  80.5 2.8 %collective-permute-start.2 = (bf16[128,2560]{1,0:T(8,128)(2,1)S(1)}, bf16[128,2560]{1,0:T(8,128)(2,1)}, u32[]{:S(2)}, u32[]{:S(2)}) collective-permute-start(bf16[128,2560]{1,0:T(8,128)(2,1)S(1)} %collective-permute-done.1.refs_2_), channel_id=1, source_target_pairs={{2,3},{3,2},{4,5},{5,4},{10,11},{11,10},{12,13},{13,12},{18,19},{1... | collective-permute-start | bytes 1966088 | tf_op jit(solution)/shard_map/ppermute | solution.py:237
  83.2 1.9 %collective-permute-start.6 = (bf16[128,2560]{1,0:T(8,128)(2,1)S(1)}, bf16[128,2560]{1,0:T(8,128)(2,1)}, u32[]{:S(2)}, u32[]{:S(2)}) collective-permute-start(bf16[128,2560]{1,0:T(8,128)(2,1)S(1)} %collective-permute-done.4.refs_5_), channel_id=1, source_target_pairs={{0,1},{1,0},{2,3},{3,2},{8,9},{9,8},{10,11},{11,10},{16,17},{17,16... | collective-permute-start | bytes 1966088 | tf_op jit(solution)/shard_map/ppermute | solution.py:237
  85.2 2.4 %collective-permute-start.8 = (bf16[128,2560]{1,0:T(8,128)(2,1)S(1)}, bf16[128,2560]{1,0:T(8,128)(2,1)}, u32[]{:S(2)}, u32[]{:S(2)}) collective-permute-start(bf16[128,2560]{1,0:T(8,128)(2,1)S(1)} %collective-permute-done.7.refs_8_), channel_id=1, source_target_pairs={{2,3},{3,2},{4,5},{5,4},{10,11},{11,10},{12,13},{13,12},{18,19},{1... | collective-permute-start | bytes 1966088 | tf_op jit(solution)/shard_map/ppermute | solution.py:237
  87.6 1.5 %collective-permute-start.16 = (bf16[128,2560]{1,0:T(8,128)(2,1)}, bf16[128,2560]{1,0:T(8,128)(2,1)}, u32[]{:S(2)}, u32[]{:S(2)}) collective-permute-start(bf16[128,2560]{1,0:T(8,128)(2,1)} %collective-permute-done.14.refs_2_), channel_id=1, source_target_pairs={{4,5},{5,4},{6,7},{7,6},{12,13},{13,12},{14,15},{15,14},{20,21},{2... | collective-permute-start | bytes 1966088 | tf_op jit(solution)/shard_map/ppermute | solution.py:237
  89.1 1.9 %collective-permute-start.17 = (bf16[128,2560]{1,0:T(8,128)(2,1)}, bf16[128,2560]{1,0:T(8,128)(2,1)}, u32[]{:S(2)}, u32[]{:S(2)}) collective-permute-start(bf16[128,2560]{1,0:T(8,128)(2,1)} %collective-permute-done.15.refs_3_), channel_id=1, source_target_pairs={{0,1},{1,0},{2,3},{3,2},{8,9},{9,8},{10,11},{11,10},{16,17},{17,16... | collective-permute-start | bytes 1966088 | tf_op jit(solution)/shard_map/ppermute | solution.py:237
  91.1 1.2 %constant_dynamic-slice_fusion = s32[1,1]{1,0:T(1,128)} fusion(s32[8,1]{1,0:T(8,128)} %constant.30.clone, s32[]{:T(128)S(6)} %select_n.24), kind=kLoop, calls=%fused_computation.4 | loop fusion | bytes 12 | tf_op jit(solution)/shard_map/dynamic_slice | solution.py:246
  92.2 1.9 %fusion.2 = (s32[]{:T(128)}, s32[5]{0:T(128)S(1)}) fusion(s32[]{:T(128)} %bitcast.2, s32[8,5]{1,0:T(8,128)} %param.9, s32[]{:T(128)S(6)} %select_n.24), kind=kLoop, calls=%fused_computation.8 | loop fusion | flops 14 | bytes 52 | tf_op jit(solution)/shard_map/reduce_sum | solution.py:248
  96.8 1.1 copy-done.9
  97.8 1.1 copy-done.10
  101.1 2.5 %shard_map.64 = (f32[128,2560]{1,0:T(8,128)S(1)}, f32[128,2560]{1,0:T(8,128)S(1)}) custom-call(bf16[128,2560]{1,0:T(8,128)(2,1)S(1)} %copy-done, bf16[128,2560]{1,0:T(8,128)(2,1)S(1)} %copy-done.9, bf16[128,2560]{1,0:T(8,128)(2,1)S(1)} %copy-done.12, bf16[128,2560]{1,0:T(8,128)(2,1)S(1)} %copy-done.10, bf16[128,2560]{1,0:T(8,128)(2,1)S(1)} %copy-done.14), custom_call_target="tpu_custom_call" | custom-call | flops 335544320 | bytes 5898240 | tf_op jit(solution)/shard_map/pallas_call | solution.py:187
  103.7 2.7 %shard_map.65 = (f32[128,2560]{1,0:T(8,128)S(1)}, f32[128,2560]{1,0:T(8,128)S(1)}) custom-call(f32[1]{0:T(128)} %bitcast.3.refs_0_, bf16[128,2560]{1,0:T(8,128)(2,1)S(1)} %copy-done, bf16[128,2560]{1,0:T(8,128)(2,1)S(1)} %copy-done.4, bf16[128,2560]{1,0:T(8,128)(2,1)S(1)} %copy-done.8, bf16[128,2560]{1,0:T(8,128)(2,1)S(1)} %copy-done.2, ...), custom_call_target="tpu_custom_call" | custom-call | flops 335544320 | bytes 8519680 | tf_op jit(solution)/shard_map/pallas_call | solution.py:187
  106.4 5.3 %shard_map.66 = (f32[128,2560]{1,0:T(8,128)S(1)}, bf16[128,5120]{1,0:T(8,128)(2,1)S(1)}) custom-call(f32[2]{0:T(128)S(1)} %compare_select_fusion.1.refs_0_, bf16[128,2560]{1,0:T(8,128)(2,1)S(1)} %copy-done, bf16[128,2560]{1,0:T(8,128)(2,1)S(1)} %collective-permute-done.1.refs_2_, bf16[128,2560]{1,0:T(8,128)(2,1)} %collective-permute-done.2.refs_3_, ...), custom_call_target="tpu_custom_call" | custom-call | flops 671088640 | bytes 11141120 | tf_op jit(solution)/shard_map/pallas_call | solution.py:187
  111.7 3.2 %shard_map.67 = bf16[128,2560]{1,0:T(8,128)(2,1)} custom-call(f32[128,2560]{1,0:T(8,128)S(1)} %get-tuple-element.18.refs_0_, bf16[128,5120]{1,0:T(8,128)(2,1)S(1)} %get-tuple-element.19.refs_1_, bf16[128,2560]{1,0:T(8,128)(2,1)} %collective-permute-done.14.refs_2_, bf16[128,2560]{1,0:T(8,128)(2,1)} %collective-permute-done.15.refs_3_, ...), custom_call_target="tpu_custom_call" | custom-call | flops 167772160 | bytes 5898240 | tf_op jit(solution)/shard_map/pallas_call | solution.py:187
  (51 shorter events, 11.6 us)
Async XLA Ops:
  0.0 15.8 %collective-permute-start = (bf16[128,2560]{1,0:T(8,128)(2,1)}, bf16[128,2560]{1,0:T(8,128)(2,1)S(1)}, u32[]{:S(2)}, u32[]{:S(2)}) collective-permute-start(bf16[128,2560]{1,0:T(8,128)(2,1)} %refs_3_.1), channel_id=1, source_target_pairs={{0,2},{2,0},{4,6},{6,4},{8,10},{10,8},{12,14},{14,12},{1,3},{3,1},... | collective-permute-start | bytes 1966088 | tf_op jit(solution)/shard_map/ppermute | solution.py:232
  0.0 17.3 %collective-permute-start.12 = (bf16[128,2560]{1,0:T(8,128)(2,1)}, bf16[128,2560]{1,0:T(8,128)(2,1)S(1)}, u32[]{:S(2)}, u32[]{:S(2)}) collective-permute-start(bf16[128,2560]{1,0:T(8,128)(2,1)} %refs_1_.3), channel_id=1, source_target_pairs={{0,1},{1,0},{2,3},{3,2},{4,5},{5,4},{6,7},{7,6},{8,9},{9,8},{10,11... | collective-permute-start | bytes 1966088 | tf_op jit(solution)/shard_map/ppermute | solution.py:237
  0.7 29.2 %collective-permute-start.9 = (bf16[128,2560]{1,0:T(8,128)(2,1)}, bf16[128,2560]{1,0:T(8,128)(2,1)S(1)}, u32[]{:S(2)}, u32[]{:S(2)}) collective-permute-start(bf16[128,2560]{1,0:T(8,128)(2,1)} %refs_1_.3), channel_id=1, source_target_pairs={{0,2},{2,0},{4,6},{6,4},{8,10},{10,8},{12,14},{14,12},{1,3},{3,1},... | collective-permute-start | bytes 1966088 | tf_op jit(solution)/shard_map/ppermute | solution.py:232
  2.4 29.8 %collective-permute-start.13 = (bf16[128,2560]{1,0:T(8,128)(2,1)}, bf16[128,2560]{1,0:T(8,128)(2,1)S(1)}, u32[]{:S(2)}, u32[]{:S(2)}) collective-permute-start(bf16[128,2560]{1,0:T(8,128)(2,1)} %refs_3_.1), channel_id=1, source_target_pairs={{0,1},{1,0},{2,3},{3,2},{4,5},{5,4},{6,7},{7,6},{8,9},{9,8},{10,11... | collective-permute-start | bytes 1966088 | tf_op jit(solution)/shard_map/ppermute | solution.py:237
  2.7 33.5 %collective-permute-start.3 = (bf16[128,2560]{1,0:T(8,128)(2,1)}, bf16[128,2560]{1,0:T(8,128)(2,1)S(1)}, u32[]{:S(2)}, u32[]{:S(2)}) collective-permute-start(bf16[128,2560]{1,0:T(8,128)(2,1)} %refs_1_.3), channel_id=1, source_target_pairs={{4,12},{6,14},{12,4},{14,6},{5,13},{7,15},{13,5},{15,7},{20,28},{2... | collective-permute-start | bytes 1966088 | tf_op jit(solution)/shard_map/ppermute | solution.py:232
  15.8 24.7 %collective-permute-start.14 = (bf16[128,2560]{1,0:T(8,128)(2,1)}, bf16[128,2560]{1,0:T(8,128)(2,1)}, u32[]{:S(2)}, u32[]{:S(2)}) collective-permute-start(bf16[128,2560]{1,0:T(8,128)(2,1)} %refs_3_.1), channel_id=1, source_target_pairs={{4,12},{6,14},{12,4},{14,6},{5,13},{7,15},{13,5},{15,7},{20,28},{2... | collective-permute-start | bytes 1966088 | tf_op jit(solution)/shard_map/ppermute | solution.py:232
  18.2 24.5 %collective-permute-start.11 = (bf16[128,2560]{1,0:T(8,128)(2,1)S(1)}, bf16[128,2560]{1,0:T(8,128)(2,1)S(1)}, u32[]{:S(2)}, u32[]{:S(2)}) collective-permute-start(bf16[128,2560]{1,0:T(8,128)(2,1)S(1)} %collective-permute-done.refs_4_), channel_id=1, source_target_pairs={{0,1},{1,0},{2,3},{3,2},{4,5},{5,4},{6,7},{7,6},{8,9},{9,8},{10,11... | collective-permute-start | bytes 1966088 | tf_op jit(solution)/shard_map/ppermute | solution.py:237
  29.9 14.3 %collective-permute-start.10 = (bf16[128,2560]{1,0:T(8,128)(2,1)S(1)}, bf16[128,2560]{1,0:T(8,128)(2,1)S(1)}, u32[]{:S(2)}, u32[]{:S(2)}) collective-permute-start(bf16[128,2560]{1,0:T(8,128)(2,1)S(1)} %collective-permute-done.9.refs_2_), channel_id=1, source_target_pairs={{0,1},{1,0},{2,3},{3,2},{4,5},{5,4},{6,7},{7,6},{8,9},{9,8},{10,11... | collective-permute-start | bytes 1966088 | tf_op jit(solution)/shard_map/ppermute | solution.py:237
  33.1 47.4 %collective-permute-start.1 = (bf16[128,2560]{1,0:T(8,128)(2,1)}, bf16[128,2560]{1,0:T(8,128)(2,1)S(1)}, u32[]{:S(2)}, u32[]{:S(2)}) collective-permute-start(bf16[128,2560]{1,0:T(8,128)(2,1)} %refs_1_.3), channel_id=1, source_target_pairs={{2,4},{4,2},{10,12},{12,10},{3,5},{5,3},{11,13},{13,11},{18,20},{2... | collective-permute-start | bytes 1966088 | tf_op jit(solution)/shard_map/ppermute | solution.py:232
  36.3 47.0 %collective-permute-start.4 = (bf16[128,2560]{1,0:T(8,128)(2,1)}, bf16[128,2560]{1,0:T(8,128)(2,1)S(1)}, u32[]{:S(2)}, u32[]{:S(2)}) collective-permute-start(bf16[128,2560]{1,0:T(8,128)(2,1)} %refs_1_.3), channel_id=1, source_target_pairs={{0,8},{2,10},{8,0},{10,2},{1,9},{3,11},{9,1},{11,3},{16,24},{18,26... | collective-permute-start | bytes 1966088 | tf_op jit(solution)/shard_map/ppermute | solution.py:232
  40.5 44.7 %collective-permute-start.7 = (bf16[128,2560]{1,0:T(8,128)(2,1)S(1)}, bf16[128,2560]{1,0:T(8,128)(2,1)S(1)}, u32[]{:S(2)}, u32[]{:S(2)}) collective-permute-start(bf16[128,2560]{1,0:T(8,128)(2,1)S(1)} %collective-permute-done.refs_4_), channel_id=1, source_target_pairs={{0,4},{6,2},{8,12},{14,10},{1,5},{7,3},{9,13},{15,11},{16,20},{22,... | collective-permute-start | bytes 1966088 | tf_op jit(solution)/shard_map/ppermute | solution.py:232
  43.5 44.1 %collective-permute-start.5 = (bf16[128,2560]{1,0:T(8,128)(2,1)S(1)}, bf16[128,2560]{1,0:T(8,128)(2,1)S(1)}, u32[]{:S(2)}, u32[]{:S(2)}) collective-permute-start(bf16[128,2560]{1,0:T(8,128)(2,1)S(1)} %collective-permute-done.3.refs_4_), channel_id=1, source_target_pairs={{4,5},{5,4},{6,7},{7,6},{12,13},{13,12},{14,15},{15,14},{20,21},{2... | collective-permute-start | bytes 1966088 | tf_op jit(solution)/shard_map/ppermute | solution.py:237
  45.0 44.1 %collective-permute-start.15 = (bf16[128,2560]{1,0:T(8,128)(2,1)}, bf16[128,2560]{1,0:T(8,128)(2,1)}, u32[]{:S(2)}, u32[]{:S(2)}) collective-permute-start(bf16[128,2560]{1,0:T(8,128)(2,1)} %refs_3_.1), channel_id=1, source_target_pairs={{0,8},{2,10},{8,0},{10,2},{1,9},{3,11},{9,1},{11,3},{16,24},{18,26... | collective-permute-start | bytes 1966088 | tf_op jit(solution)/shard_map/ppermute | solution.py:232
  80.5 25.9 %collective-permute-start.2 = (bf16[128,2560]{1,0:T(8,128)(2,1)S(1)}, bf16[128,2560]{1,0:T(8,128)(2,1)}, u32[]{:S(2)}, u32[]{:S(2)}) collective-permute-start(bf16[128,2560]{1,0:T(8,128)(2,1)S(1)} %collective-permute-done.1.refs_2_), channel_id=1, source_target_pairs={{2,3},{3,2},{4,5},{5,4},{10,11},{11,10},{12,13},{13,12},{18,19},{1... | collective-permute-start | bytes 1966088 | tf_op jit(solution)/shard_map/ppermute | solution.py:237
  83.2 23.1 %collective-permute-start.6 = (bf16[128,2560]{1,0:T(8,128)(2,1)S(1)}, bf16[128,2560]{1,0:T(8,128)(2,1)}, u32[]{:S(2)}, u32[]{:S(2)}) collective-permute-start(bf16[128,2560]{1,0:T(8,128)(2,1)S(1)} %collective-permute-done.4.refs_5_), channel_id=1, source_target_pairs={{0,1},{1,0},{2,3},{3,2},{8,9},{9,8},{10,11},{11,10},{16,17},{17,16... | collective-permute-start | bytes 1966088 | tf_op jit(solution)/shard_map/ppermute | solution.py:237
  85.2 21.2 %collective-permute-start.8 = (bf16[128,2560]{1,0:T(8,128)(2,1)S(1)}, bf16[128,2560]{1,0:T(8,128)(2,1)}, u32[]{:S(2)}, u32[]{:S(2)}) collective-permute-start(bf16[128,2560]{1,0:T(8,128)(2,1)S(1)} %collective-permute-done.7.refs_8_), channel_id=1, source_target_pairs={{2,3},{3,2},{4,5},{5,4},{10,11},{11,10},{12,13},{13,12},{18,19},{1... | collective-permute-start | bytes 1966088 | tf_op jit(solution)/shard_map/ppermute | solution.py:237
  87.6 24.1 %collective-permute-start.16 = (bf16[128,2560]{1,0:T(8,128)(2,1)}, bf16[128,2560]{1,0:T(8,128)(2,1)}, u32[]{:S(2)}, u32[]{:S(2)}) collective-permute-start(bf16[128,2560]{1,0:T(8,128)(2,1)} %collective-permute-done.14.refs_2_), channel_id=1, source_target_pairs={{4,5},{5,4},{6,7},{7,6},{12,13},{13,12},{14,15},{15,14},{20,21},{2... | collective-permute-start | bytes 1966088 | tf_op jit(solution)/shard_map/ppermute | solution.py:237
  89.1 22.5 %collective-permute-start.17 = (bf16[128,2560]{1,0:T(8,128)(2,1)}, bf16[128,2560]{1,0:T(8,128)(2,1)}, u32[]{:S(2)}, u32[]{:S(2)}) collective-permute-start(bf16[128,2560]{1,0:T(8,128)(2,1)} %collective-permute-done.15.refs_3_), channel_id=1, source_target_pairs={{0,1},{1,0},{2,3},{3,2},{8,9},{9,8},{10,11},{11,10},{16,17},{17,16... | collective-permute-start | bytes 1966088 | tf_op jit(solution)/shard_map/ppermute | solution.py:237
  95.7 1.1 copy-start
  96.8 1.1 copy-start.9
  101.1 2.5 %copy-start.2 = (bf16[128,2560]{1,0:T(8,128)(2,1)S(1)}, bf16[128,2560]{1,0:T(8,128)(2,1)}, u32[]{:S(2)}) copy-start(bf16[128,2560]{1,0:T(8,128)(2,1)} %copy-done.1) | copy-start | bytes 1966084
  101.1 2.5 %copy-start.4 = (bf16[128,2560]{1,0:T(8,128)(2,1)S(1)}, bf16[128,2560]{1,0:T(8,128)(2,1)}, u32[]{:S(2)}) copy-start(bf16[128,2560]{1,0:T(8,128)(2,1)} %copy-done.3) | copy-start | bytes 1966084
  101.1 2.5 %copy-start.6 = (bf16[128,2560]{1,0:T(8,128)(2,1)S(1)}, bf16[128,2560]{1,0:T(8,128)(2,1)}, u32[]{:S(2)}) copy-start(bf16[128,2560]{1,0:T(8,128)(2,1)} %copy-done.5) | copy-start | bytes 1966084
  101.1 2.5 %copy-start.8 = (bf16[128,2560]{1,0:T(8,128)(2,1)S(1)}, bf16[128,2560]{1,0:T(8,128)(2,1)}, u32[]{:S(2)}) copy-start(bf16[128,2560]{1,0:T(8,128)(2,1)} %copy-done.7) | copy-start | bytes 1966084
  (9 other events, 8.3 us)

commit v8 on v6

--- a/solution.py
+++ b/solution.py
@@ -18,7 +18,7 @@
 
 
 def plan(rows):
-    near, relay, cross = ({}, {}), ({}, {}), ({}, {})
+    near, cross = ({}, {}), ({}, {})
     far = [({}, {}), ({}, {})]
     for row in range(rows):
         other = row ^ 1
@@ -28,15 +28,14 @@
         start = row - row % TILE_H
         if row % TILE_H in (1, 2) and start + TILE_H <= rows:
             other = 2 * start + 3 - row
-            relay[0][other ^ 1] = row
             cross[0][other] = row
-            relay[1][row] = cross[1][row] = OFFSETS.index(other - row)
+            cross[1][row] = OFFSETS.index(other - row)
         for way in (0, 1):
             other = row + TILE_H if (row // TILE_H) % 2 == way else row - TILE_H
             if 0 <= other < rows:
                 far[way][0][other] = row
                 far[way][1][row] = OFFSETS.index(other - row)
-    return near, relay, cross, [pair for pair in far if pair[0]]
+    return [near, cross] + [pair for pair in far if pair[0]]
 
 
 def lanes(value):
@@ -48,7 +47,7 @@
     return jnp.broadcast_to(found, slices[0].shape)
 
 
-def attend_chunk(heads, merging, mixed, held, bias_ref, refs, score_ref, weight_ref):
+def attend_chunk(heads, merging, mixed, held, bias_ref, refs, score_ref, weight_ref=None):
     refs = list(refs)
     blocks = mixed + held
     q_ref = refs.pop(0)
@@ -100,6 +99,9 @@
 
     def mix(head, here):
         inverse, factor = kept.pop(head)
+        if not mixed:
+            out_ref[:, here] = before_ref[:, here] * factor
+            return
         out = jnp.dot(
             weight_ref[head],
             jnp.concatenate([v[:, here] for v in v_refs], axis=0),
@@ -187,7 +189,8 @@
     operands = [queries] + [a for p in k_pairs for a in p] + [a for p in v_pairs for a in p]
     operands += list(before) if merging else []
     outs = [full] + [weight] * held + ([full] if more else [])
-    scratch = [((tokens, keys), jnp.float32), ((tokens, 2 * tokens * mixed), jnp.bfloat16)]
+    scratch = [((tokens, keys), jnp.float32)]
+    scratch += [((tokens, 2 * tokens * mixed), jnp.bfloat16)] if mixed else []
     scalars = [bias] if merging else []
     return call(chunk, HEADS_AT_ONCE, scalars, operands, outs, scratch, 2, keys)
 
@@ -202,17 +205,12 @@
     operands = [base] + weights + [a for p in v_pairs for a in p]
     outs = [jax.ShapeDtypeStruct((tokens, width), dtype)]
     return call(chunk, 10, [], operands, outs, [], 1, 2 * tokens * blocks)[0]
-
-
-def after(value, *others):
-    return lax.optimization_barrier((value,) + others)[0]
 
 
 def shards(routes, queries, keys, values, pattern):
     rows = lax.axis_size("row")
     cols = lax.axis_size("col")
     row = lax.axis_index("row")
-    near, relay, cross, far = routes
 
     def moved(value, route):
         return lax.ppermute(value, "row", sorted(route[0].items()))
@@ -231,25 +229,13 @@
         live = jnp.sum(jnp.where(here, own_row, 0), axis=1)
         return jnp.where(live == 1, 0.0, FAR_BELOW).astype(jnp.float32)
 
-    v_near = moved(values, near)
-    k_far = [moved(keys, route) for route in far]
+    ks = [moved(keys, route) for route in routes]
+    vs = [moved(values, route) for route in routes]
     k_own, v_own = paired(keys, None), paired(values, None)
-    k_near = moved(after(keys, v_near), near)
-    v_relay = moved(v_near, relay)
-    v_again = after(values, v_near)
-    v_far = [moved(v_again, route) for route in far]
-    k_cross = moved(after(keys, k_near), cross)
-
     carried = attend(None, queries, [k_own], [v_own], None, True)
-    carried = attend(
-        biases(near), queries, [paired(k_near, near)], [paired(v_near, near)], carried, True
-    )
-    k_pairs = [paired(k_cross, cross)]
-    k_pairs += [paired(k, route) for k, route in zip(k_far, far)]
-    base, *weights = attend(
-        biases(relay, *far), queries, k_pairs, [paired(v_relay, relay)], carried, False
-    )
-    v_pairs = [paired(v, route) for v, route in zip(v_far, far)]
+    k_pairs = [paired(k, route) for k, route in zip(ks, routes)]
+    base, *weights = attend(biases(*routes), queries, k_pairs, [], carried, False)
+    v_pairs = [paired(v, route) for v, route in zip(vs, routes)]
     return finish(base, weights, v_pairs, queries.dtype)
 
 

time: 105 us -> 84.9 us (0.81)
  the two profiles are of different devices: /device:TPU:0 before, /device:TPU:9 now
where the time goes in v8:
time: 84.9 us; the launch traced here: 84.4 us
  waiting for transfers between devices  46.7 us (55%)
  starting transfers between devices  18.5 us (22%)
  Pallas kernels  11.1 us (13%)
  local copies, waits for them, and re-layouts  7.81 us (9%)
    ppermute x6, waiting for transfers between devices, moved(): return lax.ppermute(value, 'row', sorted(route[0].items()))  46.7 us
    pallas_call x3, Pallas kernels, call(): return list(run(*scalars, *operands))  11.1 us
    ppermute x6, starting transfers between devices, moved(): return lax.ppermute(value, 'row', sorted(route[0].items()))  9.83 us
    ppermute x8, starting transfers between devices, paired(): return (value, lax.ppermute(value, ('row', 'col'), pairs))  8.63 us
    unnamed x16, local copies, waits for them, and re-layouts  7.11 us
  transfers between devices with their start and end apart: 14, of which 5 were waited for; matrix products, arithmetic and copies ran while one was open for 1% of the time, Pallas kernels for 9%

profile of v8, /device:TPU:9, one launch (start us, length us, event | category | flops | bytes accessed | tf_op | source)
XLA Modules:
  0.0 84.4 jit_solution(11198926294932122985)
XLA Ops:
  0.0 0.7 collective-permute-start.6
  0.8 1.2 %collective-permute-start = (bf16[128,2560]{1,0:T(8,128)(2,1)}, bf16[128,2560]{1,0:T(8,128)(2,1)S(1)}, u32[]{:S(2)}, u32[]{:S(2)}) collective-permute-start(bf16[128,2560]{1,0:T(8,128)(2,1)} %refs_1_.2), channel_id=1, source_target_pairs={{0,2},{2,0},{4,6},{6,4},{8,10},{10,8},{12,14},{14,12},{1,3},{3,1},... | collective-permute-start | bytes 1966088 | tf_op jit(solution)/shard_map/ppermute | solution.py:216
  2.0 1.9 %collective-permute-start.2 = (bf16[128,2560]{1,0:T(8,128)(2,1)}, bf16[128,2560]{1,0:T(8,128)(2,1)S(1)}, u32[]{:S(2)}, u32[]{:S(2)}) collective-permute-start(bf16[128,2560]{1,0:T(8,128)(2,1)} %refs_1_.2), channel_id=1, source_target_pairs={{2,4},{4,2},{10,12},{12,10},{3,5},{5,3},{11,13},{13,11},{18,20},{2... | collective-permute-start | bytes 1966088 | tf_op jit(solution)/shard_map/ppermute | solution.py:216
  3.9 2.5 %collective-permute-start.4 = (bf16[128,2560]{1,0:T(8,128)(2,1)}, bf16[128,2560]{1,0:T(8,128)(2,1)S(1)}, u32[]{:S(2)}, u32[]{:S(2)}) collective-permute-start(bf16[128,2560]{1,0:T(8,128)(2,1)} %refs_1_.2), channel_id=1, source_target_pairs={{0,8},{2,10},{4,12},{6,14},{8,0},{10,2},{12,4},{14,6},{1,9},{3,11}... | collective-permute-start | bytes 1966088 | tf_op jit(solution)/shard_map/ppermute | solution.py:216
  6.4 0.8 copy-done.4
  7.2 4.2 %collective-permute-start.10 = (bf16[128,2560]{1,0:T(8,128)(2,1)}, bf16[128,2560]{1,0:T(8,128)(2,1)S(1)}, u32[]{:S(2)}, u32[]{:S(2)}) collective-permute-start(bf16[128,2560]{1,0:T(8,128)(2,1)} %refs_3_.1), channel_id=1, source_target_pairs={{2,4},{4,2},{10,12},{12,10},{3,5},{5,3},{11,13},{13,11},{18,20},{2... | collective-permute-start | bytes 1966088 | tf_op jit(solution)/shard_map/ppermute | solution.py:216
  11.4 0.8 copy-done.6
  12.3 18.6 %collective-permute-done.refs_2_ = bf16[128,2560]{1,0:T(8,128)(2,1)S(1)} collective-permute-done((bf16[128,2560]{1,0:T(8,128)(2,1)}, bf16[128,2560]{1,0:T(8,128)(2,1)S(1)}, u32[]{:S(2)}, u32[]{:S(2)}) %collective-permute-start) | collective-permute-done | bytes 655392 | tf_op jit(solution)/shard_map/ppermute | solution.py:216
  30.9 4.5 %collective-permute-done.2.refs_4_ = bf16[128,2560]{1,0:T(8,128)(2,1)S(1)} collective-permute-done((bf16[128,2560]{1,0:T(8,128)(2,1)}, bf16[128,2560]{1,0:T(8,128)(2,1)S(1)}, u32[]{:S(2)}, u32[]{:S(2)}) %collective-permute-start.2) | collective-permute-done | bytes 655392 | tf_op jit(solution)/shard_map/ppermute | solution.py:216
  35.4 0.9 %collective-permute-start.1 = (bf16[128,2560]{1,0:T(8,128)(2,1)S(1)}, bf16[128,2560]{1,0:T(8,128)(2,1)}, u32[]{:S(2)}, u32[]{:S(2)}) collective-permute-start(bf16[128,2560]{1,0:T(8,128)(2,1)S(1)} %collective-permute-done.refs_2_), channel_id=1, source_target_pairs={{0,1},{1,0},{2,3},{3,2},{4,5},{5,4},{6,7},{7,6},{8,9},{9,8},{10,11... | collective-permute-start | bytes 1966088 | tf_op jit(solution)/shard_map/ppermute | solution.py:221
  36.3 11.5 %collective-permute-done.4.refs_6_ = bf16[128,2560]{1,0:T(8,128)(2,1)S(1)} collective-permute-done((bf16[128,2560]{1,0:T(8,128)(2,1)}, bf16[128,2560]{1,0:T(8,128)(2,1)S(1)}, u32[]{:S(2)}, u32[]{:S(2)}) %collective-permute-start.4) | collective-permute-done | bytes 655392 | tf_op jit(solution)/shard_map/ppermute | solution.py:216
  47.8 2.5 %collective-permute-start.3 = (bf16[128,2560]{1,0:T(8,128)(2,1)S(1)}, bf16[128,2560]{1,0:T(8,128)(2,1)}, u32[]{:S(2)}, u32[]{:S(2)}) collective-permute-start(bf16[128,2560]{1,0:T(8,128)(2,1)S(1)} %collective-permute-done.2.refs_4_), channel_id=1, source_target_pairs={{2,3},{3,2},{4,5},{5,4},{10,11},{11,10},{12,13},{13,12},{18,19},{1... | collective-permute-start | bytes 1966088 | tf_op jit(solution)/shard_map/ppermute | solution.py:221
  50.3 10.4 %collective-permute-done.10.refs_6_ = bf16[128,2560]{1,0:T(8,128)(2,1)S(1)} collective-permute-done((bf16[128,2560]{1,0:T(8,128)(2,1)}, bf16[128,2560]{1,0:T(8,128)(2,1)S(1)}, u32[]{:S(2)}, u32[]{:S(2)}) %collective-permute-start.10) | collective-permute-done | bytes 655392 | tf_op jit(solution)/shard_map/ppermute | solution.py:216
  61.2 1.7 %collective-permute-done.12.refs_8_ = bf16[128,2560]{1,0:T(8,128)(2,1)S(1)} collective-permute-done((bf16[128,2560]{1,0:T(8,128)(2,1)}, bf16[128,2560]{1,0:T(8,128)(2,1)S(1)}, u32[]{:S(2)}, u32[]{:S(2)}) %collective-permute-start.12) | collective-permute-done | bytes 655392 | tf_op jit(solution)/shard_map/ppermute | solution.py:216
  62.9 3.4 %collective-permute-start.11 = (bf16[128,2560]{1,0:T(8,128)(2,1)S(1)}, bf16[128,2560]{1,0:T(8,128)(2,1)S(1)}, u32[]{:S(2)}, u32[]{:S(2)}) collective-permute-start(bf16[128,2560]{1,0:T(8,128)(2,1)S(1)} %collective-permute-done.10.refs_6_), channel_id=1, source_target_pairs={{2,3},{3,2},{4,5},{5,4},{10,11},{11,10},{12,13},{13,12},{18,19},{1... | collective-permute-start | bytes 1966088 | tf_op jit(solution)/shard_map/ppermute | solution.py:221
  67.0 0.7 dynamic-slice_bitcast_fusion.1
  67.9 1.1 %copy-done.1 = bf16[128,2560]{1,0:T(8,128)(2,1)S(1)} copy-done((bf16[128,2560]{1,0:T(8,128)(2,1)S(1)}, bf16[128,2560]{1,0:T(8,128)(2,1)}, u32[]{:S(2)}) %copy-start.1) | copy-done | bytes 655384
  68.9 1.1 %copy-done.2 = bf16[128,2560]{1,0:T(8,128)(2,1)S(1)} copy-done((bf16[128,2560]{1,0:T(8,128)(2,1)S(1)}, bf16[128,2560]{1,0:T(8,128)(2,1)}, u32[]{:S(2)}) %copy-start.2) | copy-done | bytes 655384
  70.0 1.1 %copy-done.3 = bf16[128,2560]{1,0:T(8,128)(2,1)S(1)} copy-done((bf16[128,2560]{1,0:T(8,128)(2,1)S(1)}, bf16[128,2560]{1,0:T(8,128)(2,1)}, u32[]{:S(2)}) %copy-start.3) | copy-done | bytes 655384
  71.1 1.1 %copy-done.5 = bf16[128,2560]{1,0:T(8,128)(2,1)S(1)} copy-done((bf16[128,2560]{1,0:T(8,128)(2,1)S(1)}, bf16[128,2560]{1,0:T(8,128)(2,1)}, u32[]{:S(2)}) %copy-start.5) | copy-done | bytes 655384
  72.2 1.1 %copy-done.7 = bf16[128,2560]{1,0:T(8,128)(2,1)S(1)} copy-done((bf16[128,2560]{1,0:T(8,128)(2,1)S(1)}, bf16[128,2560]{1,0:T(8,128)(2,1)}, u32[]{:S(2)}) %copy-start.7) | copy-done | bytes 655384
  73.3 2.5 %shard_map.55 = (f32[128,2560]{1,0:T(8,128)S(1)}, f32[128,2560]{1,0:T(8,128)S(1)}) custom-call(bf16[128,2560]{1,0:T(8,128)(2,1)S(1)} %copy-done.1, bf16[128,2560]{1,0:T(8,128)(2,1)S(1)} %copy-done.2, bf16[128,2560]{1,0:T(8,128)(2,1)S(1)} %copy-done.5, bf16[128,2560]{1,0:T(8,128)(2,1)S(1)} %copy-done.3, bf16[128,2560]{1,0:T(8,128)(2,1)S(1)} %copy-done.7), custom_call_target="tpu_custom_call" | custom-call | flops 335544320 | bytes 5898240 | tf_op jit(solution)/shard_map/pallas_call | solution.py:176
  75.8 5.3 %shard_map.56 = (f32[128,2560]{1,0:T(8,128)S(1)}, bf16[128,5120]{1,0:T(8,128)(2,1)S(1)}, bf16[128,5120]{1,0:T(8,128)(2,1)S(1)}, bf16[128,5120]{1,0:T(8,128)(2,1)S(1)}) custom-call(f32[3]{0:T(128)S(1)} %compare_select_fusion.refs_0_, bf16[128,2560]{1,0:T(8,128)(2,1)S(1)} %copy-done.1, bf16[128,2560]{1,0:T(8,128)(2,1)S(1)} %collective-permute-done.refs_2_, ...), custom_call_target="tpu_custom_call" | custom-call | flops 1006632960 | bytes 12451840 | tf_op jit(solution)/shard_map/pallas_call | solution.py:176
  81.1 3.3 %shard_map.57 = bf16[128,2560]{1,0:T(8,128)(2,1)} custom-call(f32[128,2560]{1,0:T(8,128)S(1)} %get-tuple-element.13.refs_0_, bf16[128,5120]{1,0:T(8,128)(2,1)S(1)} %get-tuple-element.14.refs_1_, bf16[128,5120]{1,0:T(8,128)(2,1)S(1)} %get-tuple-element.15.refs_2_, bf16[128,5120]{1,0:T(8,128)(2,1)S(1)} %get-tuple-element.16.refs_3_, ...), custom_call_target="tpu_custom_call" | custom-call | flops 503316480 | bytes 9830400 | tf_op jit(solution)/shard_map/pallas_call | solution.py:176
  (27 shorter events, 1.4 us)
Async XLA Ops:
  0.0 67.0 %copy-start = (s32[8,5]{1,0:T(8,128)S(1)}, s32[8,5]{1,0:T(8,128)}, u32[]{:S(2)}) copy-start(s32[8,5]{1,0:T(8,128)} %param.8) | copy-start | bytes 484
  0.0 6.4 %collective-permute-start.6 = (bf16[128,2560]{1,0:T(8,128)(2,1)}, bf16[128,2560]{1,0:T(8,128)(2,1)S(1)}, u32[]{:S(2)}, u32[]{:S(2)}) collective-permute-start(bf16[128,2560]{1,0:T(8,128)(2,1)} %refs_1_.2), channel_id=1, source_target_pairs={{0,1},{1,0},{2,3},{3,2},{4,5},{5,4},{6,7},{7,6},{8,9},{9,8},{10,11... | collective-permute-start | bytes 1966088 | tf_op jit(solution)/shard_map/ppermute | solution.py:221
  0.7 10.7 %collective-permute-start.7 = (bf16[128,2560]{1,0:T(8,128)(2,1)}, bf16[128,2560]{1,0:T(8,128)(2,1)S(1)}, u32[]{:S(2)}, u32[]{:S(2)}) collective-permute-start(bf16[128,2560]{1,0:T(8,128)(2,1)} %refs_3_.1), channel_id=1, source_target_pairs={{0,1},{1,0},{2,3},{3,2},{4,5},{5,4},{6,7},{7,6},{8,9},{9,8},{10,11... | collective-permute-start | bytes 1966088 | tf_op jit(solution)/shard_map/ppermute | solution.py:221
  0.8 30.1 %collective-permute-start = (bf16[128,2560]{1,0:T(8,128)(2,1)}, bf16[128,2560]{1,0:T(8,128)(2,1)S(1)}, u32[]{:S(2)}, u32[]{:S(2)}) collective-permute-start(bf16[128,2560]{1,0:T(8,128)(2,1)} %refs_1_.2), channel_id=1, source_target_pairs={{0,2},{2,0},{4,6},{6,4},{8,10},{10,8},{12,14},{14,12},{1,3},{3,1},... | collective-permute-start | bytes 1966088 | tf_op jit(solution)/shard_map/ppermute | solution.py:216
  2.0 33.4 %collective-permute-start.2 = (bf16[128,2560]{1,0:T(8,128)(2,1)}, bf16[128,2560]{1,0:T(8,128)(2,1)S(1)}, u32[]{:S(2)}, u32[]{:S(2)}) collective-permute-start(bf16[128,2560]{1,0:T(8,128)(2,1)} %refs_1_.2), channel_id=1, source_target_pairs={{2,4},{4,2},{10,12},{12,10},{3,5},{5,3},{11,13},{13,11},{18,20},{2... | collective-permute-start | bytes 1966088 | tf_op jit(solution)/shard_map/ppermute | solution.py:216
  3.9 43.9 %collective-permute-start.4 = (bf16[128,2560]{1,0:T(8,128)(2,1)}, bf16[128,2560]{1,0:T(8,128)(2,1)S(1)}, u32[]{:S(2)}, u32[]{:S(2)}) collective-permute-start(bf16[128,2560]{1,0:T(8,128)(2,1)} %refs_1_.2), channel_id=1, source_target_pairs={{0,8},{2,10},{4,12},{6,14},{8,0},{10,2},{12,4},{14,6},{1,9},{3,11}... | collective-permute-start | bytes 1966088 | tf_op jit(solution)/shard_map/ppermute | solution.py:216
  6.4 0.8 copy-start.4
  7.2 53.5 %collective-permute-start.10 = (bf16[128,2560]{1,0:T(8,128)(2,1)}, bf16[128,2560]{1,0:T(8,128)(2,1)S(1)}, u32[]{:S(2)}, u32[]{:S(2)}) collective-permute-start(bf16[128,2560]{1,0:T(8,128)(2,1)} %refs_3_.1), channel_id=1, source_target_pairs={{2,4},{4,2},{10,12},{12,10},{3,5},{5,3},{11,13},{13,11},{18,20},{2... | collective-permute-start | bytes 1966088 | tf_op jit(solution)/shard_map/ppermute | solution.py:216
  11.4 0.9 %copy-start.6 = (bf16[128,2560]{1,0:T(8,128)(2,1)}, bf16[128,2560]{1,0:T(8,128)(2,1)S(1)}, u32[]{:S(2)}) copy-start(bf16[128,2560]{1,0:T(8,128)(2,1)S(1)} %collective-permute-done.7.refs_4_) | copy-start | bytes 1966084
  12.2 50.7 %collective-permute-start.12 = (bf16[128,2560]{1,0:T(8,128)(2,1)}, bf16[128,2560]{1,0:T(8,128)(2,1)S(1)}, u32[]{:S(2)}, u32[]{:S(2)}) collective-permute-start(bf16[128,2560]{1,0:T(8,128)(2,1)} %refs_3_.1), channel_id=1, source_target_pairs={{0,8},{2,10},{4,12},{6,14},{8,0},{10,2},{12,4},{14,6},{1,9},{3,11}... | collective-permute-start | bytes 1966088 | tf_op jit(solution)/shard_map/ppermute | solution.py:216
  30.9 35.5 %collective-permute-start.8 = (bf16[128,2560]{1,0:T(8,128)(2,1)}, bf16[128,2560]{1,0:T(8,128)(2,1)}, u32[]{:S(2)}, u32[]{:S(2)}) collective-permute-start(bf16[128,2560]{1,0:T(8,128)(2,1)} %refs_3_.1), channel_id=1, source_target_pairs={{0,2},{2,0},{4,6},{6,4},{8,10},{10,8},{12,14},{14,12},{1,3},{3,1},... | collective-permute-start | bytes 1966088 | tf_op jit(solution)/shard_map/ppermute | solution.py:216
  35.4 31.1 %collective-permute-start.1 = (bf16[128,2560]{1,0:T(8,128)(2,1)S(1)}, bf16[128,2560]{1,0:T(8,128)(2,1)}, u32[]{:S(2)}, u32[]{:S(2)}) collective-permute-start(bf16[128,2560]{1,0:T(8,128)(2,1)S(1)} %collective-permute-done.refs_2_), channel_id=1, source_target_pairs={{0,1},{1,0},{2,3},{3,2},{4,5},{5,4},{6,7},{7,6},{8,9},{9,8},{10,11... | collective-permute-start | bytes 1966088 | tf_op jit(solution)/shard_map/ppermute | solution.py:221
  47.8 28.0 %collective-permute-start.3 = (bf16[128,2560]{1,0:T(8,128)(2,1)S(1)}, bf16[128,2560]{1,0:T(8,128)(2,1)}, u32[]{:S(2)}, u32[]{:S(2)}) collective-permute-start(bf16[128,2560]{1,0:T(8,128)(2,1)S(1)} %collective-permute-done.2.refs_4_), channel_id=1, source_target_pairs={{2,3},{3,2},{4,5},{5,4},{10,11},{11,10},{12,13},{13,12},{18,19},{1... | collective-permute-start | bytes 1966088 | tf_op jit(solution)/shard_map/ppermute | solution.py:221
  60.7 15.1 %collective-permute-start.5 = (bf16[128,2560]{1,0:T(8,128)(2,1)S(1)}, bf16[128,2560]{1,0:T(8,128)(2,1)}, u32[]{:S(2)}, u32[]{:S(2)}) collective-permute-start(bf16[128,2560]{1,0:T(8,128)(2,1)S(1)} %collective-permute-done.4.refs_6_), channel_id=1, source_target_pairs={{0,1},{1,0},{2,3},{3,2},{4,5},{5,4},{6,7},{7,6},{8,9},{9,8},{10,11... | collective-permute-start | bytes 1966088 | tf_op jit(solution)/shard_map/ppermute | solution.py:221
  62.9 18.1 %collective-permute-start.11 = (bf16[128,2560]{1,0:T(8,128)(2,1)S(1)}, bf16[128,2560]{1,0:T(8,128)(2,1)S(1)}, u32[]{:S(2)}, u32[]{:S(2)}) collective-permute-start(bf16[128,2560]{1,0:T(8,128)(2,1)S(1)} %collective-permute-done.10.refs_6_), channel_id=1, source_target_pairs={{2,3},{3,2},{4,5},{5,4},{10,11},{11,10},{12,13},{13,12},{18,19},{1... | collective-permute-start | bytes 1966088 | tf_op jit(solution)/shard_map/ppermute | solution.py:221
  66.4 14.7 %collective-permute-start.13 = (bf16[128,2560]{1,0:T(8,128)(2,1)S(1)}, bf16[128,2560]{1,0:T(8,128)(2,1)S(1)}, u32[]{:S(2)}, u32[]{:S(2)}) collective-permute-start(bf16[128,2560]{1,0:T(8,128)(2,1)S(1)} %collective-permute-done.12.refs_8_), channel_id=1, source_target_pairs={{0,1},{1,0},{2,3},{3,2},{4,5},{5,4},{6,7},{7,6},{8,9},{9,8},{10,11... | collective-permute-start | bytes 1966088 | tf_op jit(solution)/shard_map/ppermute | solution.py:221
  66.5 14.6 %collective-permute-start.9 = (bf16[128,2560]{1,0:T(8,128)(2,1)}, bf16[128,2560]{1,0:T(8,128)(2,1)S(1)}, u32[]{:S(2)}, u32[]{:S(2)}) collective-permute-start(bf16[128,2560]{1,0:T(8,128)(2,1)} %collective-permute-done.8.refs_4_), channel_id=1, source_target_pairs={{0,1},{1,0},{2,3},{3,2},{4,5},{5,4},{6,7},{7,6},{8,9},{9,8},{10,11... | collective-permute-start | bytes 1966088 | tf_op jit(solution)/shard_map/ppermute | solution.py:221
  67.8 1.1 %copy-start.1 = (bf16[128,2560]{1,0:T(8,128)(2,1)S(1)}, bf16[128,2560]{1,0:T(8,128)(2,1)}, u32[]{:S(2)}) copy-start(bf16[128,2560]{1,0:T(8,128)(2,1)} %refs_1_.3) | copy-start | bytes 1966084
  68.9 1.1 %copy-start.2 = (bf16[128,2560]{1,0:T(8,128)(2,1)S(1)}, bf16[128,2560]{1,0:T(8,128)(2,1)}, u32[]{:S(2)}) copy-start(bf16[128,2560]{1,0:T(8,128)(2,1)} %refs_1_.2) | copy-start | bytes 1966084
  70.0 1.1 %copy-start.3 = (bf16[128,2560]{1,0:T(8,128)(2,1)S(1)}, bf16[128,2560]{1,0:T(8,128)(2,1)}, u32[]{:S(2)}) copy-start(bf16[128,2560]{1,0:T(8,128)(2,1)} %refs_3_.1) | copy-start | bytes 1966084
  71.1 1.1 %copy-start.5 = (bf16[128,2560]{1,0:T(8,128)(2,1)S(1)}, bf16[128,2560]{1,0:T(8,128)(2,1)}, u32[]{:S(2)}) copy-start(bf16[128,2560]{1,0:T(8,128)(2,1)} %copy-done.4) | copy-start | bytes 1966084
  72.2 1.1 %copy-start.7 = (bf16[128,2560]{1,0:T(8,128)(2,1)S(1)}, bf16[128,2560]{1,0:T(8,128)(2,1)}, u32[]{:S(2)}) copy-start(bf16[128,2560]{1,0:T(8,128)(2,1)} %copy-done.6) | copy-start | bytes 1966084
